TPU v7x, 512 devices: a whole 4x4x16 slice. The times are simulated.
512 devices in a mesh: row: 32 (over x, z_lo), col: 16 (over y, z_hi, core).
Axes of the slice: x: 4, y: 4, z: 16 (z_hi: 2, z_lo: 8; z = z_hi * 8 + z_lo), core: 2. Of those that a mesh axis runs over, the one named last changes fastest.
Arguments:
- traces: bfloat16 [32, 2048, 2048], P(None, 'row', 'col'), may hold values from -6 to 6
- source_pos: int32 [2048], P('row'), may hold values from 0 to 16383
- receiver_pos: int32 [2048], replicated, may hold values from 0 to 16383
- aperture_list: int32 [128, 1024], P('row'), may hold values from 0 to 2047, as said below
- band_index: int32 [16384], P('row'), may hold values from 0 to 31
- weight_tiles: bfloat16 [32, 2, 128], replicated, may hold values from -4 to 4
Outputs:
- primaries: bfloat16 [32, 2048, 2048], P(None, 'row', 'col')
- image: float32 [2048, 16384], P('col', 'row')
Inputs may be any that keep to these rules, and one draw needn't show every extreme that they name: `aperture_list`: the 1024 receivers listed for one tile are distinct.
All inputs are finite; a program needn't handle non-finite values.
Results may differ from a plain program's by a relative error of at most 0.012.
Values may be sent and summed in bfloat16 or wider, within the bound.
A program may use at most 64 MiB of HBM per device.

v0:
```python
import math

import jax
import jax.numpy as jnp
from jax import lax
from jax.sharding import PartitionSpec as P

NFFT = 4096
NF = 4


def phase_tables(samples):
    freq_bins = (2 * jnp.arange(NF, dtype=jnp.int32) + 1) * (NFFT // (4 * NF))
    sample_ticks = jnp.arange(samples, dtype=jnp.int32)
    phase_turns = freq_bins[:, None] * sample_ticks[None, :] % NFFT
    phase_angle = phase_turns.astype(jnp.float32) * (2.0 * math.pi / NFFT)
    return (jnp.cos(phase_angle), jnp.sin(phase_angle))


def aperture_matrix(tile_index_lists, positions, columns, first_row, row_count, spread_len):
    tile_count, listed = tile_index_lists.shape
    col_width = columns.shape[0]
    inside = (tile_index_lists >= first_row) & (tile_index_lists < first_row + row_count)
    local_index = jnp.where(inside, tile_index_lists - first_row, row_count)
    tile_rows = jnp.broadcast_to(
        jnp.arange(tile_count, dtype=jnp.int32)[:, None], tile_index_lists.shape
    )
    member = (
        jnp.zeros((tile_count, row_count), jnp.float32)
        .at[tile_rows, local_index]
        .add(1.0, mode="drop")
    )
    widened = jnp.repeat(member.T, col_width // tile_count, axis=1)
    offset = (positions[:, None] - columns[None, :]).astype(jnp.float32) / spread_len
    taper_weight = 1.0 / (1.0 + offset * offset)
    return (widened * taper_weight * (2.0 / math.sqrt(listed))).astype(jnp.bfloat16)


def shot_weights(positions, columns, spread_len):
    offset = (positions[:, None] - columns[None, :]).astype(jnp.float32) / spread_len
    return 1.0 / (1.0 + offset * offset)


def complex_product(left_section, right_section):
    real_real = jnp.einsum(
        "qju,quy->qjy", left_section[0], right_section[0], preferred_element_type=jnp.float32
    )
    imag_imag = jnp.einsum(
        "qju,quy->qjy", left_section[1], right_section[1], preferred_element_type=jnp.float32
    )
    real_imag = jnp.einsum(
        "qju,quy->qjy", left_section[0], right_section[1], preferred_element_type=jnp.float32
    )
    imag_real = jnp.einsum(
        "qju,quy->qjy", left_section[1], right_section[0], preferred_element_type=jnp.float32
    )
    return jnp.stack([real_real - imag_imag, real_imag + imag_real])


def slab_stack(slab_block, aperture, stacking_weights):
    depth_slab_samples, shot_count, listed_rows = slab_block.shape
    stacked = jnp.dot(
        slab_block.reshape(depth_slab_samples * shot_count, listed_rows),
        aperture,
        preferred_element_type=jnp.float32,
    )
    stacked = stacked.reshape(depth_slab_samples, shot_count, aperture.shape[1])
    return jnp.sum(stacked * stacking_weights[None], axis=1)


def per_device(traces, source_pos, receiver_pos, aperture_list, band_index, weight_tiles):
    samples, shot_count, recv_count = traces.shape
    col_count = lax.axis_size("col")
    surface_count = recv_count * col_count
    image_panel_width = band_index.shape[0]
    depth_slab_samples = samples // col_count
    cosine, sine_table = phase_tables(samples)
    forward = (jnp.concatenate([cosine, -sine_table], 0) / math.sqrt(samples)).astype(jnp.bfloat16)
    spectra = jnp.dot(
        forward,
        traces.reshape(samples, shot_count * recv_count),
        preferred_element_type=jnp.float32,
    )
    spectra = spectra.astype(jnp.bfloat16).reshape(2, NF, shot_count, recv_count)
    columns_whole = lax.all_gather(spectra, "row", axis=2, tiled=True)
    summed = complex_product(lax.all_gather(spectra, "col", axis=3, tiled=True), columns_whole)
    multiples = -summed / math.sqrt(surface_count)
    inverse = jnp.concatenate([cosine, -sine_table], 0).T / math.sqrt(NF)
    wave_field = jnp.dot(
        inverse,
        multiples.reshape(2 * NF, shot_count * recv_count),
        precision=lax.Precision.HIGHEST,
        preferred_element_type=jnp.float32,
    )
    primaries = (
        traces.astype(jnp.float32) - wave_field.reshape(samples, shot_count, recv_count)
    ).astype(jnp.bfloat16)
    columns = lax.axis_index("row") * image_panel_width + jnp.arange(
        image_panel_width, dtype=jnp.int32
    )
    spread_len = image_panel_width * lax.axis_size("row") // 4
    stacking_weights = shot_weights(source_pos, columns, spread_len)
    slab_block = lax.all_to_all(primaries, "col", split_axis=0, concat_axis=2, tiled=True)
    aperture = aperture_matrix(aperture_list, receiver_pos, columns, 0, surface_count, spread_len)
    stacked = slab_stack(slab_block, aperture, stacking_weights)
    column_stack = (stacked / math.sqrt(shot_count)).astype(jnp.bfloat16)
    tile_kinds = weight_tiles.shape[0]
    select = band_index[None, :] == jnp.arange(tile_kinds, dtype=jnp.int32)[:, None]
    widened = jnp.where(select[:, None, :], column_stack[None], jnp.zeros((), jnp.bfloat16))
    image_out = jnp.einsum(
        "kz,kx->zx",
        weight_tiles.reshape(tile_kinds * depth_slab_samples, weight_tiles.shape[2]),
        widened.reshape(tile_kinds * depth_slab_samples, image_panel_width),
        preferred_element_type=jnp.float32,
    )
    return (primaries, image_out)


def solution(mesh):
    placed = (P(None, "row", "col"), P("row"), P(), P("row", None), P("row"), P())
    return jax.shard_map(
        per_device,
        mesh=mesh,
        in_specs=placed,
        out_specs=(P(None, "row", "col"), P("col", "row")),
        check_vma=False,
    )
```

profile of v0, /device:TPU:1, one launch (start us, length us, event | category | flops | bytes accessed | tf_op | source)
XLA Modules:
  0.0 404.5 jit_solution(7858936798405555199)
XLA Ops:
  7.2 0.0 copy-start
  7.2 0.0 all-gather.3.cloned.1.call-start
  7.2 0.1 fusion.30
  7.4 1.4 fusion.10
  8.8 0.7 copy.33
  9.5 0.0 all-gather.3.cloned.1.call-update
  9.5 0.0 all-gather.5.cloned.1.call-start
  9.5 0.7 all-gather.5.cloned.1.call-update
  10.3 0.7 fusion.19
  11.0 0.7 multiply_reduce_fusion
  11.7 0.8 and_reduce_fusion
  12.5 95.1 %all-gather.3.cloned.1.call-done = bf16[2,4,64,2048]{3,2,1,0:T(8,128)(2,1)} async-done(((bf16[2,4,64,128]{3,2,1,0:T(8,128)(2,1)}), bf16[2,4,64,2048]{3,2,1,0:T(8,128)(2,1)}) %all-gather.3.cloned.1.call-update) | async-done | bytes 2097168 | tf_op jit(solution)/shard_map/all_gather | solution.py:86
  107.6 211.9 %all-gather.5.cloned.1.call-done = bf16[2,4,2048,128]{3,2,1,0:T(8,128)(2,1)} async-done(((bf16[2,4,64,128]{3,2,1,0:T(8,128)(2,1)}), bf16[2,4,2048,128]{3,2,1,0:T(8,128)(2,1)}) %all-gather.5.cloned.1.call-update) | async-done | bytes 4194320 | tf_op jit(solution)/shard_map/all_gather | solution.py:85
  319.5 2.5 fusion.1
  322.0 2.4 fusion
  324.5 0.0 copy-start.1
  324.5 0.5 fusion.7
  325.0 0.5 fusion.9
  325.5 1.3 fusion.4
  326.8 1.0 copy.30
  327.8 33.6 %all-to-all-start = ((bf16[32,64,128]{2,1,0:T(8,128)(2,1)}), bf16[32,64,128]{2,1,0:T(8,128)(2,1)S(1)}, u32[]{:S(2)}, u32[]{:S(2)}) async-start(bf16[32,64,128]{2,1,0:T(8,128)(2,1)} %copy.30), calls=%async_computation | async-start | bytes 1048576 | tf_op jit(solution)/shard_map/all_to_all | solution.py:103
  361.5 22.1 %scatter_custom_fusion = f32[8192]{0:T(1024)S(1)} fusion(s32[4096]{0:T(1024)S(1)} %bitcast.76, f32[4096]{0:T(1024)S(1)} %broadcast.205, f32[]{:T(128)} %constant.56.clone.1), kind=kCustom, calls=%fused_computation.41 | custom fusion | flops 4096 | bytes 32772
  383.6 0.0 copy-start.3
  383.6 0.4 copy.28
  384.0 8.6 %multiply_convert_fusion = bf16[2048,4,128]{2,1,0:T(4,128)(2,1)} fusion(s32[4,128]{1,0:T(4,128)S(1)} %add_add_fusion, s32[2048]{0:T(1024)S(1)} %copy-done.2, f32[2048,4]{1,0:T(8,128)S(1)} %copy.28), kind=kLoop, calls=%fused_computation.2 | loop fusion | flops 9437184 | bytes 2140160 | tf_op jit(solution)/shard_map/convert_element_type | solution.py:36
  392.6 2.7 reshape.161
  395.4 0.1 add_divide_fusion
  395.5 0.3 copy.49
  395.9 0.2 dot_general.40
  396.1 0.5 fusion.5
  396.6 0.2 convolution_bitcast_fusion
  396.8 0.8 copy.31
  (23 shorter events, 0.1 us)
Async XLA Ops:
  7.2 389.4 %copy-start = (bf16[32,2,128]{2,1,0:T(2,128)(2,1)S(1)}, bf16[32,2,128]{2,1,0:T(2,128)(2,1)}, u32[]{:S(2)}) copy-start(bf16[32,2,128]{2,1,0:T(2,128)(2,1)} %param.11) | copy-start | bytes 49156
  7.2 100.4 %all-gather.3.cloned.1.call-start = ((), (), s32[]{:S(2)}) async-start(), calls=%async_computation.1 | async-start | bytes 2228224 | tf_op jit(solution)/shard_map/all_gather | solution.py:86
  9.5 310.0 %all-gather.5.cloned.1.call-start = ((), (), s32[]{:S(2)}) async-start(), calls=%async_computation.2 | async-start | bytes 4325376 | tf_op jit(solution)/shard_map/all_gather | solution.py:85
  107.6 216.9 %copy-start.6 = (bf16[2,4,64,2048]{3,2,1,0:T(8,128)(2,1)S(1)}, bf16[2,4,64,2048]{3,2,1,0:T(8,128)(2,1)}, u32[]{:S(2)}) copy-start(bf16[2,4,64,2048]{3,2,1,0:T(8,128)(2,1)} %all-gather.3.cloned.1.call-done) | copy-start | bytes 6291460
  319.5 5.0 %copy-start.5 = (bf16[2,4,2048,128]{3,2,1,0:T(8,128)(2,1)S(1)}, bf16[2,4,2048,128]{3,2,1,0:T(8,128)(2,1)}, u32[]{:S(2)}) copy-start(bf16[2,4,2048,128]{3,2,1,0:T(8,128)(2,1)} %all-gather.5.cloned.1.call-done) | copy-start | bytes 12582916
  324.5 1.1 copy-start.1
  325.0 59.0 %copy-start.2 = (s32[2048]{0:T(1024)S(1)}, s32[2048]{0:T(1024)}, u32[]{:S(2)}) copy-start(s32[2048]{0:T(1024)} %param.8) | copy-start | bytes 24580
  327.8 67.7 %all-to-all-start = ((bf16[32,64,128]{2,1,0:T(8,128)(2,1)}), bf16[32,64,128]{2,1,0:T(8,128)(2,1)S(1)}, u32[]{:S(2)}, u32[]{:S(2)}) async-start(bf16[32,64,128]{2,1,0:T(8,128)(2,1)} %copy.30), calls=%async_computation | async-start | bytes 1048576 | tf_op jit(solution)/shard_map/all_to_all | solution.py:103
  383.6 11.8 %copy-start.3 = (s32[512]{0:T(512)S(1)}, s32[512]{0:T(512)}, u32[]{:S(2)}) copy-start(s32[512]{0:T(512)} %param.10) | copy-start | bytes 6148
  383.6 11.8 %copy-start.4 = (s32[64]{0:T(128)S(1)}, s32[64]{0:T(128)}, u32[]{:S(2)}) copy-start(s32[64]{0:T(128)} %param.7) | copy-start | bytes 772
Sparse Core Ops, SparseCore 0:
  11.7 95.8 all-gather.2
  110.2 209.1 all-gather.4
where the time goes:
time: 405 us
  waiting for transfers between devices  308 us (76%)
  starting transfers between devices  33.7 us (8%)
  other arithmetic  33.2 us (8%)
  between operations  14.3 us (4%)
  matrix products  9.38 us (2%)
  local copies, waits for them, and re-layouts  6.27 us (2%)
    all_gather x1, waiting for transfers between devices, per_device(): columns_whole = lax.all_gather(spectra, 'row', axis=2, tiled=True)  212 us
    all_gather x1, waiting for transfers between devices, per_device(): lax.all_gather(spectra, 'col', axis=3, tiled=True)  95.1 us
    all_to_all x1, starting transfers between devices, per_device(): lax.all_to_all(primaries, 'col', split_axis=0, concat_axis=2, tiled=True)  33.6 us
    unnamed x4, other arithmetic  23.6 us
    convert_element_type x1, other arithmetic, aperture_matrix(): (widened * taper_weight * (2.0 / math.sqrt(listed))).astype(jnp.bfloat16)  8.57 us
  transfers between devices with their start and end apart: 3, of which 2 were waited for; matrix products, arithmetic and copies ran while one was open for 9% of the time, Pallas kernels for 0%

commit v1 on v0

v1 whole, which is shorter than its diff:
```python
import math

import jax
import jax.numpy as jnp
from jax import lax
from jax.sharding import Mesh
from jax.sharding import PartitionSpec as P

NFFT = 4096
NF = 4

ROW = ("x", "zl")
COL = ("y", "zh", "c")


def phase_tables(samples):
    freq_bins = (2 * jnp.arange(NF, dtype=jnp.int32) + 1) * (NFFT // (4 * NF))
    sample_ticks = jnp.arange(samples, dtype=jnp.int32)
    phase_turns = freq_bins[:, None] * sample_ticks[None, :] % NFFT
    phase_angle = phase_turns.astype(jnp.float32) * (2.0 * math.pi / NFFT)
    return (jnp.cos(phase_angle), jnp.sin(phase_angle))


def aperture_rows(tile_index_lists, positions, columns, first_row, row_count, spread_len):
    tile_count, listed = tile_index_lists.shape
    col_width = columns.shape[0]
    rows = first_row + jnp.arange(row_count, dtype=jnp.int32)
    hits = (tile_index_lists[:, :, None] == rows[None, None, :]).astype(jnp.float32)
    member = jnp.sum(hits, axis=1)
    widened = jnp.repeat(member.T, col_width // tile_count, axis=1)
    offset = (positions[:, None] - columns[None, :]).astype(jnp.float32) / spread_len
    taper_weight = 1.0 / (1.0 + offset * offset)
    return (widened * taper_weight * (2.0 / math.sqrt(listed))).astype(jnp.bfloat16)


def shot_weights(positions, columns, spread_len):
    offset = (positions[:, None] - columns[None, :]).astype(jnp.float32) / spread_len
    return 1.0 / (1.0 + offset * offset)


def complex_product(left_section, right_section):
    real_real = jnp.einsum(
        "qju,quy->qjy", left_section[0], right_section[0], preferred_element_type=jnp.float32
    )
    imag_imag = jnp.einsum(
        "qju,quy->qjy", left_section[1], right_section[1], preferred_element_type=jnp.float32
    )
    real_imag = jnp.einsum(
        "qju,quy->qjy", left_section[0], right_section[1], preferred_element_type=jnp.float32
    )
    imag_real = jnp.einsum(
        "qju,quy->qjy", left_section[1], right_section[0], preferred_element_type=jnp.float32
    )
    return jnp.stack([real_real - imag_imag, real_imag + imag_real])


def axis_pos(names):
    index = 0
    for name in names:
        index = index * lax.axis_size(name) + lax.axis_index(name)
    return index


def axis_count(names):
    count = 1
    for name in names:
        count *= lax.axis_size(name)
    return count


def per_device(traces, source_pos, receiver_pos, aperture_list, band_index, weight_tiles):
    samples, shot_count, recv_count = traces.shape
    col_count = axis_count(COL)
    row_count = axis_count(ROW)
    surface_count = recv_count * col_count
    image_panel_width = band_index.shape[0]
    depth_slab_samples = samples // col_count
    cosine, sine_table = phase_tables(samples)
    forward = (jnp.concatenate([cosine, -sine_table], 0) / math.sqrt(samples)).astype(jnp.bfloat16)
    spectra = jnp.dot(
        forward,
        traces.reshape(samples, shot_count * recv_count),
        preferred_element_type=jnp.float32,
    )
    spectra = spectra.astype(jnp.bfloat16).reshape(2, NF, shot_count, recv_count)

    columns_whole = lax.all_gather(spectra, "zl", axis=2, tiled=True)
    columns_whole = lax.all_gather(columns_whole, "x", axis=2, tiled=True)
    row_parts = lax.all_gather(spectra, "zh", axis=0)
    row_parts = lax.all_gather(row_parts, "c", axis=0)
    row_parts = lax.all_gather(row_parts, "y", axis=0)
    rows_whole = jnp.transpose(row_parts, (3, 4, 5, 0, 2, 1, 6)).reshape(
        2, NF, shot_count, surface_count
    )

    col_pos = axis_pos(COL)
    row_pos = axis_pos(ROW)
    columns = row_pos * image_panel_width + jnp.arange(image_panel_width, dtype=jnp.int32)
    spread_len = image_panel_width * row_count // 4
    stacking_weights = shot_weights(source_pos, columns, spread_len)
    my_receivers = lax.dynamic_slice_in_dim(receiver_pos, col_pos * recv_count, recv_count, 0)
    aperture = aperture_rows(
        aperture_list, my_receivers, columns, col_pos * recv_count, recv_count, spread_len
    )
    rows_whole, columns_whole, aperture, stacking_weights = lax.optimization_barrier(
        (rows_whole, columns_whole, aperture, stacking_weights)
    )

    summed = complex_product(rows_whole, columns_whole)
    multiples = -summed / math.sqrt(surface_count)
    inverse = jnp.concatenate([cosine, -sine_table], 0).T / math.sqrt(NF)
    wave_field = jnp.dot(
        inverse,
        multiples.reshape(2 * NF, shot_count * recv_count),
        precision=lax.Precision.HIGHEST,
        preferred_element_type=jnp.float32,
    )
    primaries = (
        traces.astype(jnp.float32) - wave_field.reshape(samples, shot_count, recv_count)
    ).astype(jnp.bfloat16)

    partial = jnp.dot(
        primaries.reshape(samples * shot_count, recv_count),
        aperture,
        preferred_element_type=jnp.float32,
    ).reshape(samples, shot_count, image_panel_width)
    partial = jnp.sum(partial * stacking_weights[None], axis=1)
    stacked = lax.psum_scatter(partial, COL, scatter_dimension=0, tiled=True)
    column_stack = (stacked / math.sqrt(shot_count)).astype(jnp.bfloat16)

    tile_kinds = weight_tiles.shape[0]
    select = band_index[None, :] == jnp.arange(tile_kinds, dtype=jnp.int32)[:, None]
    widened = jnp.where(select[:, None, :], column_stack[None], jnp.zeros((), jnp.bfloat16))
    image_out = jnp.einsum(
        "kz,kx->zx",
        weight_tiles.reshape(tile_kinds * depth_slab_samples, weight_tiles.shape[2]),
        widened.reshape(tile_kinds * depth_slab_samples, image_panel_width),
        preferred_element_type=jnp.float32,
    )
    return (primaries, image_out)


def solution(mesh):
    n_row = mesh.shape["row"]
    n_col = mesh.shape["col"]
    fine = Mesh(
        mesh.devices.reshape(4, n_row // 4, 4, n_col // 8, 2), ("x", "zl", "y", "zh", "c")
    )
    placed = (P(None, ROW, COL), P(ROW), P(), P(ROW, None), P(ROW), P())
    return jax.shard_map(
        per_device,
        mesh=fine,
        in_specs=placed,
        out_specs=(P(None, ROW, COL), P(COL, ROW)),
        check_vma=False,
    )
```

time: 405 us -> 436 us (1.077)
  waiting for transfers between devices: 308 us -> 375 us
  starting transfers between devices: 33.7 us -> 0.16 us
  other arithmetic: 33.2 us -> 1.95 us
  blocking collectives: 0 us -> 23.7 us
  local copies, waits for them, and re-layouts: 6.27 us -> 11.2 us
    unnamed x2 -> x5, waiting for transfers between devices: 0.71 us -> 241 us
    all_gather x2 -> x3, waiting for transfers between devices: 307 us -> 134 us  [the longest x1 51.5 us: per_device(): columns_whole = lax.all_gather(columns_whole, 'x', axis=2, tiled=True)]
    all_to_all x1 -> x0, starting transfers between devices: 33.6 us -> none  [per_device(): lax.all_to_all(primaries, 'col', split_axis=0, concat_axis=2, tiled=True)]
    all_gather x0 -> x2, blocking collectives: none -> 23.7 us  [the longest x1 18 us: per_device(): row_parts = lax.all_gather(spectra, 'zh', axis=0)]
    unnamed x4 -> x0, other arithmetic: 23.6 us -> none
    convert_element_type x1, other arithmetic: 8.57 us -> 0.15 us  [aperture_rows(): (widened * taper_weight * (2.0 / math.sqrt(listed))).astype(jnp.bfloat16)]
  transfers between devices with their start and end apart: 3 -> 4, of which waited for: 2 -> 4; matrix products, arithmetic and copies ran while one was open for 9% -> 2% of each run, Pallas kernels for 0% -> 0%
where the time goes in v1:
time: 436 us
  waiting for transfers between devices  375 us (86%)
  blocking collectives  23.7 us (5%)
  between operations  14.6 us (3%)
  local copies, waits for them, and re-layouts  11.2 us (3%)
  matrix products  9.91 us (2%)
    unnamed x5, waiting for transfers between devices  241 us
    all_gather x1, waiting for transfers between devices, per_device(): columns_whole = lax.all_gather(columns_whole, 'x', axis=2, tiled=True)  51.5 us
    all_gather x1, waiting for transfers between devices, per_device(): columns_whole = lax.all_gather(spectra, 'zl', axis=2, tiled=True)  43.6 us
    all_gather x1, waiting for transfers between devices, per_device(): row_parts = lax.all_gather(row_parts, 'y', axis=0)  38.5 us
    all_gather x1, blocking collectives, per_device(): row_parts = lax.all_gather(spectra, 'zh', axis=0)  18 us
  transfers between devices with their start and end apart: 4, of which 4 were waited for; matrix products, arithmetic and copies ran while one was open for 2% of the time, Pallas kernels for 0%

profile of v1, /device:TPU:1, one launch (start us, length us, event | category | flops | bytes accessed | tf_op | source)
XLA Modules:
  0.0 436.1 jit_solution(10430945906404159967)
XLA Ops:
  7.3 0.1 fusion.54
  7.4 1.4 fusion.25
  8.8 0.7 copy.33
  9.5 0.0 all-gather.10.cloned.1.call-start
  9.6 18.0 %all_gather.21 = bf16[2,2,4,64,128]{4,3,2,1,0:T(8,128)(2,1)S(1)} all-gather(bf16[1,2,4,64,128]{4,3,2,1,0:T(8,128)(2,1)} %bitcast.81), channel_id=1, replica_groups=mesh['x'=4,'zl'=8,'y'=4,'zh'=2,'c'=2] {'zh'}, dimensions={0}, use_global_device_ids=true | all-gather | bytes 393216 | tf_op jit(solution)/shard_map/all_gather | solution.py:89
  27.5 5.7 %all-gather = bf16[4,2,4,64,128]{4,3,2,1,0:T(8,128)(2,1)} all-gather(bf16[2,2,4,64,128]{4,3,2,1,0:T(8,128)(2,1)S(1)} %all_gather.21), channel_id=2, replica_groups=mesh['x'=4,'zl'=8,'y'=4,'zh'=2,'c'=2] {'c'}, dimensions={0}, use_global_device_ids=true | all-gather | bytes 786432 | tf_op jit(solution)/shard_map/all_gather | solution.py:90
  33.3 0.0 all-gather.8.cloned.1.call-start
  33.3 43.6 %all-gather.6.cloned.1.call-done = bf16[2,4,512,128]{3,2,1,0:T(8,128)(2,1)} async-done(((bf16[2,4,64,128]{3,2,1,0:T(8,128)(2,1)}), bf16[2,4,512,128]{3,2,1,0:T(8,128)(2,1)}) %all-gather.6.cloned.1.call-update) | async-done | bytes 1048592 | tf_op jit(solution)/shard_map/all_gather | solution.py:87
  77.0 0.0 all-reduce.3.cloned.1.call-start
  77.1 0.8 convert_reduce_fusion
  77.9 0.1 copy.27
  78.0 0.8 dynamic_slice.3
  78.8 0.1 add_divide_fusion
  78.9 0.2 broadcast_in_dim.15
  79.1 0.2 fusion.38
  79.2 38.5 %all-gather.10.cloned.1.call-done = bf16[8,2,2,4,64,128]{5,4,3,2,1,0:T(8,128)(2,1)} async-done(((bf16[2,2,2,4,64,128]{5,4,3,2,1,0:T(8,128)(2,1)}), bf16[8,2,2,4,64,128]{5,4,3,2,1,0:T(8,128)(2,1)}) %all-gather.10.cloned.1.call-update) | async-done | bytes 2097168 | tf_op jit(solution)/shard_map/all_gather | solution.py:91
  117.7 3.7 copy.26
  121.4 2.8 reshape.66
  124.2 51.5 %all-gather.8.cloned.1.call-done = bf16[2,4,2048,128]{3,2,1,0:T(8,128)(2,1)} async-done(((bf16[2,4,512,128]{3,2,1,0:T(8,128)(2,1)}), bf16[2,4,2048,128]{3,2,1,0:T(8,128)(2,1)}) %all-gather.8.cloned.1.call-update) | async-done | bytes 4194320 | tf_op jit(solution)/shard_map/all_gather | solution.py:88
  175.8 2.5 fusion
  178.3 2.1 fusion.2
  180.4 0.5 fusion.22
  181.0 0.5 fusion.16
  181.5 0.5 copy-done.1
  182.0 1.3 fusion.12
  183.3 0.2 copy.30
  183.5 1.3 multiply_reduce_fusion
  184.9 1.3 dynamic-slice
  186.9 240.9 %all-reduce.3.cloned.1.call-done = f32[32,512]{1,0:T(8,128)} async-done(((f32[32,512]{1,0:T(8,128)}), f32[32,512]{1,0:T(8,128)}) %all-reduce.3.cloned.1.call-update) | async-done | bytes 65552
  427.8 0.7 fusion.46
  428.5 0.2 convolution_bitcast_fusion
  428.7 0.8 copy.31
  (25 shorter events, 0.2 us)
Async XLA Ops:
  7.2 421.4 %copy-start = (bf16[32,2,128]{2,1,0:T(2,128)(2,1)S(1)}, bf16[32,2,128]{2,1,0:T(2,128)(2,1)}, u32[]{:S(2)}) copy-start(bf16[32,2,128]{2,1,0:T(2,128)(2,1)} %param.11) | copy-start | bytes 49156
  7.2 69.9 %copy-start.4 = (s32[4,1024]{1,0:T(4,128)S(1)}, s32[4,1024]{1,0:T(4,128)}, u32[]{:S(2)}) copy-start(s32[4,1024]{1,0:T(4,128)} %param.9) | copy-start | bytes 49156
  7.2 71.6 %copy-start.6 = (s32[64]{0:T(128)S(1)}, s32[64]{0:T(128)}, u32[]{:S(2)}) copy-start(s32[64]{0:T(128)} %param.7) | copy-start | bytes 772
  7.2 69.8 %all-gather.6.cloned.1.call-start = ((), (), s32[]{:S(2)}) async-start(), calls=%async_computation | async-start | bytes 1179648 | tf_op jit(solution)/shard_map/all_gather | solution.py:87
  9.5 108.2 %all-gather.10.cloned.1.call-start = ((), (), s32[]{:S(2)}) async-start(), calls=%async_computation.2 | async-start | bytes 2621440 | tf_op jit(solution)/shard_map/all_gather | solution.py:91
  33.3 142.5 %all-gather.8.cloned.1.call-start = ((), (), s32[]{:S(2)}) async-start(), calls=%async_computation.1 | async-start | bytes 5242880 | tf_op jit(solution)/shard_map/all_gather | solution.py:88
  77.0 350.8 %all-reduce.3.cloned.1.call-start = ((), (), s32[]{:S(2)}) async-start(), calls=%async_computation.3 | async-start | bytes 131072
  124.2 54.1 %copy-start.2 = (bf16[2,4,64,2048]{3,2,1,0:T(8,128)(2,1)S(1)}, bf16[2,4,64,2048]{3,2,1,0:T(8,128)(2,1)}, u32[]{:S(2)}) copy-start(bf16[2,4,64,2048]{3,2,1,0:T(8,128)(2,1)} %reshape.66) | copy-start | bytes 6291460
  175.8 4.7 %copy-start.7 = (bf16[2,4,2048,128]{3,2,1,0:T(8,128)(2,1)S(1)}, bf16[2,4,2048,128]{3,2,1,0:T(8,128)(2,1)}, u32[]{:S(2)}) copy-start(bf16[2,4,2048,128]{3,2,1,0:T(8,128)(2,1)} %all-gather.8.cloned.1.call-done) | copy-start | bytes 12582916
  181.0 1.0 copy-start.1
  183.3 1.6 copy-start.5
  183.5 246.1 %copy-start.3 = (bf16[32,64,128]{2,1,0:T(8,128)(2,1)}, bf16[32,64,128]{2,1,0:T(8,128)(2,1)S(1)}, u32[]{:S(2)}) copy-start(bf16[32,64,128]{2,1,0:T(8,128)(2,1)S(1)} %copy.30) | copy-start | bytes 1572868
Sparse Core Ops, SparseCore 0:
  10.7 66.2 all-gather.5
  79.1 38.5 all-gather.9
  119.8 55.9 all-gather.7
  185.0 242.7 all-reduce.2

commit v2 on v1

--- a/solution.py
+++ b/solution.py
@@ -3,6 +3,8 @@
 import jax
 import jax.numpy as jnp
 from jax import lax
+from jax.experimental import pallas as pl
+from jax.experimental.pallas import tpu as pltpu
 from jax.sharding import Mesh
 from jax.sharding import PartitionSpec as P
 
@@ -66,6 +68,238 @@
     for name in names:
         count *= lax.axis_size(name)
     return count
+
+
+MESH_ID = pl.DeviceIdType.MESH
+NX, NZ, NY = 4, 8, 4
+
+
+def gather_kernel(spec_ref, colw_ref, roww_ref, recv_row, recv_col, send_row, send_col):
+    x = lax.axis_index("x")
+    z = lax.axis_index("zl")
+    y = lax.axis_index("y")
+    h = lax.axis_index("zh")
+    c = lax.axis_index("c")
+    xp = lax.rem(x + 1, NX)
+    xm = lax.rem(x + NX - 1, NX)
+    yp = lax.rem(y + 1, NY)
+    ym = lax.rem(y + NY - 1, NY)
+    me_row = x * NZ + z
+    me_col = (y * 2 + h) * 2 + c
+
+    barrier = pltpu.get_barrier_semaphore()
+    for peer in ({"x": xp}, {"x": xm}, {"y": yp}, {"y": ym}, {"zh": 1 - h}, {"c": 1 - c}):
+        pl.semaphore_signal(barrier, 1, device_id=peer, device_id_type=MESH_ID)
+
+    @pl.when(z > 0)
+    def _():
+        pl.semaphore_signal(barrier, 1, device_id={"zl": z - 1}, device_id_type=MESH_ID)
+
+    @pl.when(z < NZ - 1)
+    def _():
+        pl.semaphore_signal(barrier, 1, device_id={"zl": z + 1}, device_id_type=MESH_ID)
+
+    ends = jnp.logical_or(z == 0, z == NZ - 1)
+    pl.when(ends)(lambda: pl.semaphore_wait(barrier, 7))
+    pl.when(jnp.logical_not(ends))(lambda: pl.semaphore_wait(barrier, 8))
+
+    started = []
+
+    def row_copy(b, d, peer, own=False):
+        src = spec_ref if own else colw_ref.at[b]
+        return pltpu.make_async_remote_copy(
+            src, colw_ref.at[b], send_row.at[b, d], recv_row.at[b],
+            device_id=peer, device_id_type=MESH_ID,
+        )
+
+    def col_copy(j, d, peer, own=False):
+        src = spec_ref if own else roww_ref.at[j]
+        return pltpu.make_async_remote_copy(
+            src, roww_ref.at[j], send_col.at[j, d], recv_col.at[j],
+            device_id=peer, device_id_type=MESH_ID,
+        )
+
+    def start(desc, cond=None):
+        if cond is None:
+            desc.start()
+        else:
+            pl.when(cond)(desc.start)
+        started.append((desc, cond))
+
+    def wait_row(b, cond=None):
+        desc = row_copy(b, 0, {"x": x})
+        if cond is None:
+            desc.wait_recv()
+        else:
+            pl.when(cond)(desc.wait_recv)
+
+    def wait_col(j, cond=None):
+        desc = col_copy(j, 0, {"y": y})
+        if cond is None:
+            desc.wait_recv()
+        else:
+            pl.when(cond)(desc.wait_recv)
+
+    start(col_copy(me_col, 0, {"c": 1 - c}, own=True))
+    start(col_copy(me_col, 1, {"zh": 1 - h}, own=True))
+    start(row_copy(me_row, 0, {"zl": z + 1}, own=True), z < NZ - 1)
+    start(row_copy(me_row, 1, {"zl": z - 1}, own=True), z > 0)
+    start(row_copy(me_row, 2, {"x": xp}, own=True))
+    start(row_copy(me_row, 3, {"x": xm}, own=True))
+    start(col_copy(me_col, 2, {"y": yp}, own=True))
+    start(col_copy(me_col, 3, {"y": ym}, own=True))
+    colw_ref[me_row] = spec_ref[...]
+    roww_ref[me_col] = spec_ref[...]
+
+    j_h = (y * 2 + 1 - h) * 2 + c
+    j_c = (y * 2 + h) * 2 + 1 - c
+    j_hc = (y * 2 + 1 - h) * 2 + 1 - c
+    wait_col(j_h)
+    start(col_copy(j_h, 0, {"c": 1 - c}))
+    start(col_copy(j_h, 2, {"y": yp}))
+    start(col_copy(j_h, 3, {"y": ym}))
+    wait_col(j_c)
+    start(col_copy(j_c, 2, {"y": yp}))
+    start(col_copy(j_c, 3, {"y": ym}))
+
+    def x_forward(zsrc, cond):
+        even = lax.rem(zsrc, 2) == 0
+        b_left = xm * NZ + zsrc
+        b_right = xp * NZ + zsrc
+        wait_row(b_left, jnp.logical_and(cond, even))
+        start(row_copy(b_left, 2, {"x": xp}), jnp.logical_and(cond, even))
+        odd = jnp.logical_not(even)
+        wait_row(b_right, jnp.logical_and(cond, odd))
+        start(row_copy(b_right, 3, {"x": xm}), jnp.logical_and(cond, odd))
+
+    for k in range(1, NZ):
+        lo = z >= k
+        b = x * NZ + z - k
+        wait_row(b, lo)
+        start(row_copy(b, 0, {"zl": z + 1}), jnp.logical_and(lo, z < NZ - 1))
+        start(row_copy(b, 2, {"x": xp}), lo)
+        start(row_copy(b, 3, {"x": xm}), lo)
+        hi = z + k < NZ
+        b = x * NZ + z + k
+        wait_row(b, hi)
+        start(row_copy(b, 1, {"zl": z - 1}), jnp.logical_and(hi, z > 0))
+        start(row_copy(b, 2, {"x": xp}), hi)
+        start(row_copy(b, 3, {"x": xm}), hi)
+        if k == 1:
+            x_forward(z, True)
+            wait_col(j_hc)
+            start(col_copy(j_hc, 2, {"y": yp}))
+            start(col_copy(j_hc, 3, {"y": ym}))
+            for cc in range(2):
+                jl = (ym * 2 + 0) * 2 + cc
+                wait_col(jl)
+                start(col_copy(jl, 2, {"y": yp}))
+                jr = (yp * 2 + 1) * 2 + cc
+                wait_col(jr)
+                start(col_copy(jr, 3, {"y": ym}))
+        else:
+            x_forward(z - (k - 1), z >= k - 1)
+            x_forward(z + (k - 1), z + (k - 1) < NZ)
+    x_forward(z - (NZ - 1), z >= NZ - 1)
+    x_forward(z + (NZ - 1), z + (NZ - 1) < NZ)
+
+    x2 = lax.rem(x + 2, NX)
+    for zz in range(NZ):
+        if zz % 2 == 1:
+            wait_row(xm * NZ + zz)
+        else:
+            wait_row(xp * NZ + zz)
+        wait_row(x2 * NZ + zz)
+    y2 = lax.rem(y + 2, NY)
+    for cc in range(2):
+        wait_col((ym * 2 + 1) * 2 + cc)
+        wait_col((yp * 2 + 0) * 2 + cc)
+        for hh in range(2):
+            wait_col((y2 * 2 + hh) * 2 + cc)
+    for desc, cond in started:
+        if cond is None:
+            desc.wait_send()
+        else:
+            pl.when(cond)(desc.wait_send)
+
+
+def gather_spectra(spectra_planes, row_count, col_count):
+    planes = spectra_planes.shape
+    return pl.pallas_call(
+        gather_kernel,
+        out_shape=(
+            jax.ShapeDtypeStruct((row_count,) + planes, spectra_planes.dtype),
+            jax.ShapeDtypeStruct((col_count,) + planes, spectra_planes.dtype),
+        ),
+        in_specs=[pl.BlockSpec(memory_space=pltpu.VMEM)],
+        out_specs=(pl.BlockSpec(memory_space=pltpu.VMEM), pl.BlockSpec(memory_space=pltpu.VMEM)),
+        scratch_shapes=[
+            pltpu.SemaphoreType.DMA((row_count,)),
+            pltpu.SemaphoreType.DMA((col_count,)),
+            pltpu.SemaphoreType.DMA((row_count, 4)),
+            pltpu.SemaphoreType.DMA((col_count, 4)),
+        ],
+        compiler_params=pltpu.CompilerParams(collective_id=0, has_side_effects=True),
+    )(spectra_planes)
+
+
+def reduce_kernel(part_ref, out_ref, slots, recv_sem, send_sem):
+    y = lax.axis_index("y")
+    h = lax.axis_index("zh")
+    c = lax.axis_index("c")
+    me = (y * 2 + h) * 2 + c
+    peers = []
+    for yy in range(NY):
+        for hh in range(2):
+            for cc in range(2):
+                peers.append(((yy * 2 + hh) * 2 + cc, {"y": yy, "zh": hh, "c": cc}))
+    barrier = pltpu.get_barrier_semaphore()
+    for j, peer in peers:
+        pl.when(j != me)(
+            lambda peer=peer: pl.semaphore_signal(
+                barrier, 1, device_id=peer, device_id_type=MESH_ID
+            )
+        )
+    pl.semaphore_wait(barrier, len(peers) - 1)
+    copies = []
+    for j, peer in peers:
+        desc = pltpu.make_async_remote_copy(
+            part_ref.at[j], slots.at[me], send_sem.at[j], recv_sem.at[me],
+            device_id=peer, device_id_type=MESH_ID,
+        )
+        pl.when(j != me)(desc.start)
+        copies.append((j, desc))
+    slots[me] = part_ref[me]
+    for j, desc in copies:
+        recv = pltpu.make_async_remote_copy(
+            part_ref.at[j], slots.at[j], send_sem.at[j], recv_sem.at[j],
+            device_id={"y": y}, device_id_type=MESH_ID,
+        )
+        pl.when(j != me)(recv.wait_recv)
+    total = slots[0]
+    for j in range(1, len(peers)):
+        total = total + slots[j]
+    out_ref[...] = total
+    for j, desc in copies:
+        pl.when(j != me)(desc.wait_send)
+
+
+def reduce_bands(partial, col_count):
+    rows, width = partial.shape
+    band = rows // col_count
+    parts = partial.reshape(col_count, band, width)
+    return pl.pallas_call(
+        reduce_kernel,
+        out_shape=jax.ShapeDtypeStruct((band, width), partial.dtype),
+        in_specs=[pl.BlockSpec(memory_space=pltpu.VMEM)],
+        out_specs=pl.BlockSpec(memory_space=pltpu.VMEM),
+        scratch_shapes=[
+            pltpu.VMEM((col_count, band, width), partial.dtype),
+            pltpu.SemaphoreType.DMA((col_count,)),
+            pltpu.SemaphoreType.DMA((col_count,)),
+        ],
+        compiler_params=pltpu.CompilerParams(collective_id=1, has_side_effects=True),
+    )(parts)
 
 
 def per_device(traces, source_pos, receiver_pos, aperture_list, band_index, weight_tiles):
@@ -84,14 +318,11 @@
     )
     spectra = spectra.astype(jnp.bfloat16).reshape(2, NF, shot_count, recv_count)
 
-    columns_whole = lax.all_gather(spectra, "zl", axis=2, tiled=True)
-    columns_whole = lax.all_gather(columns_whole, "x", axis=2, tiled=True)
-    row_parts = lax.all_gather(spectra, "zh", axis=0)
-    row_parts = lax.all_gather(row_parts, "c", axis=0)
-    row_parts = lax.all_gather(row_parts, "y", axis=0)
-    rows_whole = jnp.transpose(row_parts, (3, 4, 5, 0, 2, 1, 6)).reshape(
-        2, NF, shot_count, surface_count
-    )
+    colw, roww = gather_spectra(
+        spectra.reshape(2 * NF, shot_count, recv_count), row_count, col_count
+    )
+    columns_whole = jnp.transpose(colw, (1, 0, 2, 3)).reshape(2, NF, row_count * shot_count, recv_count)
+    rows_whole = jnp.transpose(roww, (1, 2, 0, 3)).reshape(2, NF, shot_count, surface_count)
 
     col_pos = axis_pos(COL)
     row_pos = axis_pos(ROW)
@@ -125,7 +356,7 @@
         preferred_element_type=jnp.float32,
     ).reshape(samples, shot_count, image_panel_width)
     partial = jnp.sum(partial * stacking_weights[None], axis=1)
-    stacked = lax.psum_scatter(partial, COL, scatter_dimension=0, tiled=True)
+    stacked = reduce_bands(partial, col_count)
     column_stack = (stacked / math.sqrt(shot_count)).astype(jnp.bfloat16)
 
     tile_kinds = weight_tiles.shape[0]

time: 436 us -> 122 us (0.28)
  waiting for transfers between devices: 375 us -> 0 us
  Pallas kernels: 0 us -> 96.6 us
  blocking collectives: 23.7 us -> 0 us
  between operations: 14.6 us -> 0.83 us
    unnamed x5 -> x0, waiting for transfers between devices: 241 us -> none
    all_gather x3 -> x0, waiting for transfers between devices: 134 us -> none  [the longest x1 51.5 us: per_device(): columns_whole = lax.all_gather(columns_whole, 'x', axis=2, tiled=True)]
    pallas_call x0 -> x2, Pallas kernels: none -> 96.6 us  [the longest x1 73.4 us: gather_spectra(): pl.pallas_call(gather_kernel, out_shape=(jax.ShapeDtypeStruct((row_count,...]
    all_gather x2 -> x0, blocking collectives: 23.7 us -> none  [the longest x1 18 us: per_device(): row_parts = lax.all_gather(spectra, 'zh', axis=0)]
    transpose x1 -> x2, local copies, waits for them, and re-layouts: 3.75 us -> 8.61 us  [the longest x1 5.65 us: per_device(): jnp.transpose(colw, (1, 0, 2, 3))]
  transfers between devices with their start and end apart: 4 -> 0, of which waited for: 4 -> 0; matrix products, arithmetic and copies ran while one was open for 2% -> 0% of each run, Pallas kernels for 0% -> 0%
where the time goes in v2:
time: 122 us
  Pallas kernels  96.6 us (79%)
  local copies, waits for them, and re-layouts  15.4 us (13%)
  matrix products  7.4 us (6%)
  other arithmetic  1.88 us (2%)
    pallas_call x1, Pallas kernels, gather_spectra(): pl.pallas_call(gather_kernel, out_shape=(jax.ShapeDtypeStruct((row_count,...  73.4 us
    pallas_call x1, Pallas kernels, reduce_bands(): pl.pallas_call(reduce_kernel, out_shape=jax.ShapeDtypeStruct((band, width...  23.2 us
    transpose x1, local copies, waits for them, and re-layouts, per_device(): jnp.transpose(colw, (1, 0, 2, 3))  5.65 us
    transpose x1, local copies, waits for them, and re-layouts, per_device(): jnp.transpose(roww, (1, 2, 0, 3)).reshape(2, NF, shot_count, surface_count)  2.96 us
    unnamed x19, local copies, waits for them, and re-layouts  2.68 us

profile of v2, /device:TPU:1, one launch (start us, length us, event | category | flops | bytes accessed | tf_op | source)
XLA Modules:
  0.0 122.1 jit_solution(8700855497054090689)
XLA Ops:
  0.6 0.0 copy-start
  0.7 0.1 fusion.53
  0.8 1.4 %fusion.25 = bf16[1,8,64,128]{3,1,2,0:T(8,128)(2,1)S(1)} fusion(bf16[4,8,64,128]{3,2,1,0:T(8,128)(2,1)} %bitcast.80, f32[4,32]{1,0:T(4,128)S(1)} %get-tuple-element.21, f32[4,32]{1,0:T(4,128)S(1)} %get-tuple-element.20), kind=kOutput, calls=%fused_computation.22 | convolution fusion | flops 4260608 | bytes 656384 | tf_op jit(solution)/shard_map/dot_general | solution.py:314
  2.2 0.7 copy.45
  2.9 73.4 %shard_map.77 = (bf16[32,8,64,128]{3,2,1,0:T(8,128)(2,1)}, bf16[16,8,64,128]{3,2,1,0:T(8,128)(2,1)}) custom-call(bf16[8,64,128]{2,1,0:T(8,128)(2,1)} %bitcast.84), custom_call_target="tpu_custom_call" | custom-call | tf_op jit(solution)/shard_map/pallas_call | solution.py:228
  76.3 3.0 %copy.21 = bf16[8,64,16,128]{3,2,1,0:T(8,128)(2,1)S(1)} copy(bf16[8,64,16,128]{3,1,0,2:T(8,128)(2,1)} %bitcast.81) | data formatting | bytes 4194304 | tf_op jit(solution)/shard_map/transpose | solution.py:325
  79.3 2.3 %reshape.69 = bf16[2,4,64,2048]{3,2,1,0:T(8,128)(2,1)} reshape(bf16[8,64,16,128]{3,2,1,0:T(8,128)(2,1)S(1)} %copy.21) | data formatting | bytes 4194304 | tf_op jit(solution)/shard_map/reshape | solution.py:325
  81.6 5.7 %copy.22 = bf16[8,32,64,128]{3,2,1,0:T(8,128)(2,1)} copy(bf16[8,32,64,128]{3,2,0,1:T(8,128)(2,1)} %bitcast.79) | data formatting | bytes 8388608 | tf_op jit(solution)/shard_map/transpose | solution.py:324
  87.3 0.0 copy-done.5
  87.3 0.8 convert_reduce_fusion
  88.1 0.1 copy.23
  88.2 0.2 broadcast_in_dim.15
  88.4 0.8 dynamic_slice.3
  89.2 0.1 fusion.38
  89.3 0.1 add_divide_fusion
  89.4 2.2 %fusion = f32[4,64,128]{2,1,0:T(8,128)S(1)} fusion(bf16[2,4,2048,128]{3,2,1,0:T(8,128)(2,1)} %bitcast.75, bf16[2,4,64,2048]{3,2,1,0:T(8,128)(2,1)S(1)} %copy-done.3), kind=kOutput, calls=%fused_computation.2 | convolution fusion | flops 134217728 | bytes 3276800 | tf_op jit(solution)/shard_map/qju,quy->qjy/dot_general | solution.py:50
  91.7 0.4 copy-done.1
  92.1 0.5 fusion.22
  92.6 0.5 fusion.2
  93.2 0.0 copy-start.2
  93.2 0.5 fusion.16
  93.7 0.0 copy-start.6
  93.7 0.5 copy-done.2
  94.2 1.3 %fusion.12 = bf16[32,64,128]{2,0,1:T(8,128)(2,1)S(1)} fusion(bf16[32,64,128]{2,1,0:T(8,128)(2,1)S(1)} %copy-done.2, f32[1,8,64,128]{3,2,1,0:T(8,128)S(1)} %bitcast.83, f32[4,32]{1,0:T(4,128)S(1)} %get-tuple-element.21, f32[4,32]{1,0:T(4,128)S(1)} %get-tuple-element.20), kind=kOutput, calls=%fused_computation.16 | convolution fusion | flops 25952768 | bytes 1311744 | tf_op jit(solution)/shard_map/dot_general | solution.py:343
  95.5 0.2 copy.26
  95.7 0.0 copy-start.4
  95.7 0.7 multiply_reduce_fusion
  96.5 0.7 reshape.72.part_ref
  97.1 23.2 %shard_map.78 = f32[2,512]{1,0:T(2,128)} custom-call(f32[16,2,512]{2,1,0:T(2,128)} %reshape.72.part_ref), custom_call_target="tpu_custom_call" | custom-call | tf_op jit(solution)/shard_map/pallas_call | solution.py:291
  120.3 0.7 multiply_convert_fusion
  121.0 0.2 convolution_bitcast_fusion
  121.2 0.8 copy.27
  (14 shorter events, 0.1 us)
Async XLA Ops:
  0.6 120.4 %copy-start = (bf16[32,2,128]{2,1,0:T(2,128)(2,1)S(1)}, bf16[32,2,128]{2,1,0:T(2,128)(2,1)}, u32[]{:S(2)}) copy-start(bf16[32,2,128]{2,1,0:T(2,128)(2,1)} %param.11) | copy-start | bytes 49156
  81.6 5.7 %copy-start.5 = (s32[4,1024]{1,0:T(4,128)S(1)}, s32[4,1024]{1,0:T(4,128)}, u32[]{:S(2)}) copy-start(s32[4,1024]{1,0:T(4,128)} %param.9) | copy-start | bytes 49156
  81.6 7.7 %copy-start.7 = (s32[64]{0:T(128)S(1)}, s32[64]{0:T(128)}, u32[]{:S(2)}) copy-start(s32[64]{0:T(128)} %param.7) | copy-start | bytes 772
  81.6 7.8 %copy-start.3 = (bf16[2,4,64,2048]{3,2,1,0:T(8,128)(2,1)S(1)}, bf16[2,4,64,2048]{3,2,1,0:T(8,128)(2,1)}, u32[]{:S(2)}) copy-start(bf16[2,4,64,2048]{3,2,1,0:T(8,128)(2,1)} %reshape.69) | copy-start | bytes 6291460
  89.3 2.8 %copy-start.1 = (bf16[8,32,64,128]{3,2,1,0:T(8,128)(2,1)S(1)}, bf16[8,32,64,128]{3,2,1,0:T(8,128)(2,1)}, u32[]{:S(2)}) copy-start(bf16[8,32,64,128]{3,2,1,0:T(8,128)(2,1)} %copy.22) | copy-start | bytes 12582916
  93.2 1.0 copy-start.2
  93.7 2.0 %copy-start.6 = (s32[512]{0:T(512)S(1)}, s32[512]{0:T(512)}, u32[]{:S(2)}) copy-start(s32[512]{0:T(512)} %param.10) | copy-start | bytes 6148
  95.7 26.4 %copy-start.4 = (bf16[32,64,128]{2,1,0:T(8,128)(2,1)}, bf16[32,64,128]{2,1,0:T(8,128)(2,1)S(1)}, u32[]{:S(2)}) copy-start(bf16[32,64,128]{2,1,0:T(8,128)(2,1)S(1)} %copy.26) | copy-start | bytes 1572868

commit v3 on v2

--- a/solution.py
+++ b/solution.py
@@ -105,17 +105,26 @@
 
     started = []
 
+    shots = spec_ref.shape[1]
+    recvs = spec_ref.shape[2]
+
+    def colw_blk(b):
+        return colw_ref.at[:, pl.ds(pl.multiple_of(b * shots, shots), shots), :]
+
+    def roww_blk(j):
+        return roww_ref.at[:, :, pl.ds(pl.multiple_of(j * recvs, recvs), recvs)]
+
     def row_copy(b, d, peer, own=False):
-        src = spec_ref if own else colw_ref.at[b]
+        src = spec_ref if own else colw_blk(b)
         return pltpu.make_async_remote_copy(
-            src, colw_ref.at[b], send_row.at[b, d], recv_row.at[b],
+            src, colw_blk(b), send_row.at[b, d], recv_row.at[b],
             device_id=peer, device_id_type=MESH_ID,
         )
 
     def col_copy(j, d, peer, own=False):
-        src = spec_ref if own else roww_ref.at[j]
+        src = spec_ref if own else roww_blk(j)
         return pltpu.make_async_remote_copy(
-            src, roww_ref.at[j], send_col.at[j, d], recv_col.at[j],
+            src, roww_blk(j), send_col.at[j, d], recv_col.at[j],
             device_id=peer, device_id_type=MESH_ID,
         )
 
@@ -148,8 +157,8 @@
     start(row_copy(me_row, 3, {"x": xm}, own=True))
     start(col_copy(me_col, 2, {"y": yp}, own=True))
     start(col_copy(me_col, 3, {"y": ym}, own=True))
-    colw_ref[me_row] = spec_ref[...]
-    roww_ref[me_col] = spec_ref[...]
+    colw_ref[:, pl.ds(pl.multiple_of(me_row * shots, shots), shots), :] = spec_ref[...]
+    roww_ref[:, :, pl.ds(pl.multiple_of(me_col * recvs, recvs), recvs)] = spec_ref[...]
 
     j_h = (y * 2 + 1 - h) * 2 + c
     j_c = (y * 2 + h) * 2 + 1 - c
@@ -224,12 +233,12 @@
 
 
 def gather_spectra(spectra_planes, row_count, col_count):
-    planes = spectra_planes.shape
+    planes, shots, recvs = spectra_planes.shape
     return pl.pallas_call(
         gather_kernel,
         out_shape=(
-            jax.ShapeDtypeStruct((row_count,) + planes, spectra_planes.dtype),
-            jax.ShapeDtypeStruct((col_count,) + planes, spectra_planes.dtype),
+            jax.ShapeDtypeStruct((planes, row_count * shots, recvs), spectra_planes.dtype),
+            jax.ShapeDtypeStruct((planes, shots, col_count * recvs), spectra_planes.dtype),
         ),
         in_specs=[pl.BlockSpec(memory_space=pltpu.VMEM)],
         out_specs=(pl.BlockSpec(memory_space=pltpu.VMEM), pl.BlockSpec(memory_space=pltpu.VMEM)),
@@ -321,8 +330,8 @@
     colw, roww = gather_spectra(
         spectra.reshape(2 * NF, shot_count, recv_count), row_count, col_count
     )
-    columns_whole = jnp.transpose(colw, (1, 0, 2, 3)).reshape(2, NF, row_count * shot_count, recv_count)
-    rows_whole = jnp.transpose(roww, (1, 2, 0, 3)).reshape(2, NF, shot_count, surface_count)
+    columns_whole = colw.reshape(2, NF, row_count * shot_count, recv_count)
+    rows_whole = roww.reshape(2, NF, shot_count, surface_count)
 
     col_pos = axis_pos(COL)
     row_pos = axis_pos(ROW)

time: 122 us -> 115 us (0.943)
  local copies, waits for them, and re-layouts: 15.4 us -> 4 us
  matrix products: 7.4 us -> 9.47 us
  other arithmetic: 1.88 us -> 3.67 us
    transpose x2 -> x0, local copies, waits for them, and re-layouts: 8.61 us -> none  [the longest x1 5.65 us: per_device(): jnp.transpose(colw, (1, 0, 2, 3))]
    reshape x1 -> x0, local copies, waits for them, and re-layouts: 2.33 us -> none  [per_device(): jnp.transpose(roww, (1, 2, 0, 3)).reshape(2, NF, shot_count, surface_count)]
    dot_general x1, matrix products: 0.51 us -> 2.55 us  [complex_product(): jnp.einsum('qju,quy->qjy', left_section[1], right_section[1], preferred_e...]
    dot_general x1, matrix products: 0.51 us -> 2.31 us  [complex_product(): jnp.einsum('qju,quy->qjy', left_section[0], right_section[0], preferred_e...]
    dot_general x1, matrix products: 2.25 us -> 0.49 us  [complex_product(): jnp.einsum('qju,quy->qjy', left_section[0], right_section[1], preferred_e...]
    unnamed x19 -> x15, local copies, waits for them, and re-layouts: 2.68 us -> 2.26 us
where the time goes in v3:
time: 115 us
  Pallas kernels  96.6 us (84%)
  matrix products  9.47 us (8%)
  local copies, waits for them, and re-layouts  4 us (3%)
  other arithmetic  3.67 us (3%)
    pallas_call x1, Pallas kernels, gather_spectra(): pl.pallas_call(gather_kernel, out_shape=(jax.ShapeDtypeStruct((planes, ro...  73.4 us
    pallas_call x1, Pallas kernels, reduce_bands(): pl.pallas_call(reduce_kernel, out_shape=jax.ShapeDtypeStruct((band, width...  23.2 us
    dot_general x1, matrix products, complex_product(): jnp.einsum('qju,quy->qjy', left_section[1], right_section[1], preferred_e...  2.55 us
    dot_general x1, matrix products, complex_product(): jnp.einsum('qju,quy->qjy', left_section[0], right_section[0], preferred_e...  2.31 us

profile of v3, /device:TPU:1, one launch (start us, length us, event | category | flops | bytes accessed | tf_op | source)
XLA Modules:
  0.0 114.6 jit_solution(8677403831113213626)
XLA Ops:
  0.6 0.0 copy-start
  0.7 0.8 dynamic_slice.3
  1.4 1.9 %convert_reduce_fusion = f32[4,128]{1,0:T(4,128)S(1)} fusion(s32[128]{0:T(128)S(1)} %iota_add_fusion.1, s32[4,1024]{1,0:T(4,128)} %param.9), kind=kLoop, calls=%fused_computation.10 | loop fusion | flops 1572352 | bytes 18944 | tf_op jit(solution)/shard_map/reduce_sum | solution.py:31
  3.3 0.1 copy.14
  3.5 0.2 broadcast_in_dim.15
  3.7 0.1 fusion.38
  3.8 0.8 add_divide_fusion
  4.6 0.1 fusion.53
  4.7 1.4 %fusion.25 = bf16[1,8,64,128]{3,1,2,0:T(8,128)(2,1)S(1)} fusion(bf16[4,8,64,128]{3,2,1,0:T(8,128)(2,1)} %bitcast.72, f32[4,32]{1,0:T(4,128)S(1)} %get-tuple-element.19, f32[4,32]{1,0:T(4,128)S(1)} %get-tuple-element.18), kind=kOutput, calls=%fused_computation.22 | convolution fusion | flops 4260608 | bytes 656384 | tf_op jit(solution)/shard_map/dot_general | solution.py:323
  6.2 0.7 copy.36
  6.8 73.4 %shard_map.77 = (bf16[8,2048,128]{2,1,0:T(8,128)(2,1)}, bf16[8,64,2048]{2,1,0:T(8,128)(2,1)}) custom-call(bf16[8,64,128]{2,1,0:T(8,128)(2,1)} %bitcast.75), custom_call_target="tpu_custom_call" | custom-call | tf_op jit(solution)/shard_map/pallas_call | solution.py:237
  80.3 0.0 copy-start.5
  80.3 0.0 copy-start.4
  80.3 2.5 %fusion.2 = f32[4,64,128]{2,1,0:T(8,128)S(1)} fusion(bf16[2,4,2048,128]{3,2,1,0:T(8,128)(2,1)} %bitcast.77, bf16[2,4,64,2048]{3,2,1,0:T(8,128)(2,1)} %bitcast.81), kind=kOutput, calls=%fused_computation.4 | convolution fusion | flops 134217728 | bytes 3276800 | tf_op jit(solution)/shard_map/qju,quy->qjy/dot_general | solution.py:47
  82.8 0.0 copy-done.5
  82.8 2.3 %fusion.16 = f32[1,4,64,128]{3,2,1,0:T(8,128)S(1)} fusion(f32[4,64,128]{2,1,0:T(8,128)S(1)} %fusion.2, bf16[2,4,2048,128]{3,2,1,0:T(8,128)(2,1)} %bitcast.78, bf16[2,4,64,2048]{3,2,1,0:T(8,128)(2,1)S(1)} %bitcast.82), kind=kOutput, calls=%fused_computation.19 | convolution fusion | flops 134250496 | bytes 3407872 | tf_op jit(solution)/shard_map/qju,quy->qjy/dot_general | solution.py:44
  85.2 0.0 copy-done.4
  85.2 0.5 fusion
  85.7 0.0 copy-start.1
  85.7 0.5 fusion.22
  86.2 0.5 copy-done.1
  86.7 1.3 %fusion.12 = bf16[32,64,128]{2,0,1:T(8,128)(2,1)S(1)} fusion(bf16[32,64,128]{2,1,0:T(8,128)(2,1)S(1)} %copy-done.1, f32[1,8,64,128]{3,2,1,0:T(8,128)S(1)} %bitcast.74, f32[4,32]{1,0:T(4,128)S(1)} %get-tuple-element.19, f32[4,32]{1,0:T(4,128)S(1)} %get-tuple-element.18), kind=kOutput, calls=%fused_computation.16 | convolution fusion | flops 25952768 | bytes 1311744 | tf_op jit(solution)/shard_map/dot_general | solution.py:352
  88.0 0.0 copy-start.3
  88.0 0.2 copy.17
  88.2 0.0 copy-start.2
  88.2 0.7 multiply_reduce_fusion
  88.9 0.7 reshape.72.part_ref
  89.6 23.2 %shard_map.78 = f32[2,512]{1,0:T(2,128)} custom-call(f32[16,2,512]{2,1,0:T(2,128)} %reshape.72.part_ref), custom_call_target="tpu_custom_call" | custom-call | tf_op jit(solution)/shard_map/pallas_call | solution.py:300
  112.8 0.7 multiply_convert_fusion
  113.5 0.0 copy-done.3
  113.5 0.2 convolution_bitcast_fusion
  113.7 0.8 copy.18
  (7 shorter events, 0.1 us)
Async XLA Ops:
  0.6 112.9 %copy-start = (bf16[32,2,128]{2,1,0:T(2,128)(2,1)S(1)}, bf16[32,2,128]{2,1,0:T(2,128)(2,1)}, u32[]{:S(2)}) copy-start(bf16[32,2,128]{2,1,0:T(2,128)(2,1)} %param.11) | copy-start | bytes 49156
  80.3 2.6 %copy-start.5 = (bf16[8,64,2048]{2,1,0:T(8,128)(2,1)S(1)}, bf16[8,64,2048]{2,1,0:T(8,128)(2,1)}, u32[]{:S(2)}) copy-start(bf16[8,64,2048]{2,1,0:T(8,128)(2,1)} %get-tuple-element.8) | copy-start | bytes 6291460
  80.3 4.9 %copy-start.4 = (bf16[8,2048,128]{2,1,0:T(8,128)(2,1)S(1)}, bf16[8,2048,128]{2,1,0:T(8,128)(2,1)}, u32[]{:S(2)}) copy-start(bf16[8,2048,128]{2,1,0:T(8,128)(2,1)} %get-tuple-element.9) | copy-start | bytes 12582916
  85.7 1.0 copy-start.1
  88.0 25.5 %copy-start.3 = (s32[512]{0:T(512)S(1)}, s32[512]{0:T(512)}, u32[]{:S(2)}) copy-start(s32[512]{0:T(512)} %param.10) | copy-start | bytes 6148
  88.2 26.4 %copy-start.2 = (bf16[32,64,128]{2,1,0:T(8,128)(2,1)}, bf16[32,64,128]{2,1,0:T(8,128)(2,1)S(1)}, u32[]{:S(2)}) copy-start(bf16[32,64,128]{2,1,0:T(8,128)(2,1)S(1)} %copy.17) | copy-start | bytes 1572868

commit v4 on v3

--- a/solution.py
+++ b/solution.py
@@ -104,27 +104,31 @@
     pl.when(jnp.logical_not(ends))(lambda: pl.semaphore_wait(barrier, 8))
 
     started = []
-
     shots = spec_ref.shape[1]
     recvs = spec_ref.shape[2]
-
-    def colw_blk(b):
-        return colw_ref.at[:, pl.ds(pl.multiple_of(b * shots, shots), shots), :]
-
-    def roww_blk(j):
-        return roww_ref.at[:, :, pl.ds(pl.multiple_of(j * recvs, recvs), recvs)]
-
-    def row_copy(b, d, peer, own=False):
-        src = spec_ref if own else colw_blk(b)
+    half = spec_ref.shape[0] // 2
+    parts = (0, 1)
+
+    def planes(part):
+        return pl.ds(part * half, half)
+
+    def colw_blk(b, part):
+        return colw_ref.at[planes(part), pl.ds(pl.multiple_of(b * shots, shots), shots), :]
+
+    def roww_blk(j, part):
+        return roww_ref.at[planes(part), :, pl.ds(pl.multiple_of(j * recvs, recvs), recvs)]
+
+    def row_copy(b, part, d, peer, own=False):
+        src = spec_ref.at[planes(part)] if own else colw_blk(b, part)
         return pltpu.make_async_remote_copy(
-            src, colw_blk(b), send_row.at[b, d], recv_row.at[b],
+            src, colw_blk(b, part), send_row.at[b, part, d], recv_row.at[b, part],
             device_id=peer, device_id_type=MESH_ID,
         )
 
-    def col_copy(j, d, peer, own=False):
-        src = spec_ref if own else roww_blk(j)
+    def col_copy(j, part, d, peer, own=False):
+        src = spec_ref.at[planes(part)] if own else roww_blk(j, part)
         return pltpu.make_async_remote_copy(
-            src, roww_blk(j), send_col.at[j, d], recv_col.at[j],
+            src, roww_blk(j, part), send_col.at[j, part, d], recv_col.at[j, part],
             device_id=peer, device_id_type=MESH_ID,
         )
 
@@ -135,77 +139,60 @@
             pl.when(cond)(desc.start)
         started.append((desc, cond))
 
-    def wait_row(b, cond=None):
-        desc = row_copy(b, 0, {"x": x})
+    def when(cond, fn):
         if cond is None:
-            desc.wait_recv()
+            fn()
         else:
-            pl.when(cond)(desc.wait_recv)
-
-    def wait_col(j, cond=None):
-        desc = col_copy(j, 0, {"y": y})
-        if cond is None:
-            desc.wait_recv()
-        else:
-            pl.when(cond)(desc.wait_recv)
-
-    start(col_copy(me_col, 0, {"c": 1 - c}, own=True))
-    start(col_copy(me_col, 1, {"zh": 1 - h}, own=True))
-    start(row_copy(me_row, 0, {"zl": z + 1}, own=True), z < NZ - 1)
-    start(row_copy(me_row, 1, {"zl": z - 1}, own=True), z > 0)
-    start(row_copy(me_row, 2, {"x": xp}, own=True))
-    start(row_copy(me_row, 3, {"x": xm}, own=True))
-    start(col_copy(me_col, 2, {"y": yp}, own=True))
-    start(col_copy(me_col, 3, {"y": ym}, own=True))
+            pl.when(cond)(fn)
+
+    def row_relay(b, sends, cond=None):
+        for part in parts:
+            when(cond, row_copy(b, part, 0, {"x": x}).wait_recv)
+            for d, peer, extra in sends:
+                c2 = cond if extra is None else (extra if cond is None else jnp.logical_and(cond, extra))
+                start(row_copy(b, part, d, peer), c2)
+
+    def col_relay(j, sends, cond=None):
+        for part in parts:
+            when(cond, col_copy(j, part, 0, {"y": y}).wait_recv)
+            for d, peer in sends:
+                start(col_copy(j, part, d, peer), cond)
+
+    for part in parts:
+        start(col_copy(me_col, part, 0, {"c": 1 - c}, own=True))
+        start(col_copy(me_col, part, 1, {"zh": 1 - h}, own=True))
+        start(row_copy(me_row, part, 0, {"zl": z + 1}, own=True), z < NZ - 1)
+        start(row_copy(me_row, part, 1, {"zl": z - 1}, own=True), z > 0)
+        start(row_copy(me_row, part, 2, {"x": xp}, own=True))
+        start(row_copy(me_row, part, 3, {"x": xm}, own=True))
+        start(col_copy(me_col, part, 2, {"y": yp}, own=True))
+        start(col_copy(me_col, part, 3, {"y": ym}, own=True))
     colw_ref[:, pl.ds(pl.multiple_of(me_row * shots, shots), shots), :] = spec_ref[...]
     roww_ref[:, :, pl.ds(pl.multiple_of(me_col * recvs, recvs), recvs)] = spec_ref[...]
 
     j_h = (y * 2 + 1 - h) * 2 + c
     j_c = (y * 2 + h) * 2 + 1 - c
     j_hc = (y * 2 + 1 - h) * 2 + 1 - c
-    wait_col(j_h)
-    start(col_copy(j_h, 0, {"c": 1 - c}))
-    start(col_copy(j_h, 2, {"y": yp}))
-    start(col_copy(j_h, 3, {"y": ym}))
-    wait_col(j_c)
-    start(col_copy(j_c, 2, {"y": yp}))
-    start(col_copy(j_c, 3, {"y": ym}))
+    y_sends = ((2, {"y": yp}), (3, {"y": ym}))
+    col_relay(j_h, ((0, {"c": 1 - c}),) + y_sends)
+    col_relay(j_c, y_sends)
 
     def x_forward(zsrc, cond):
         even = lax.rem(zsrc, 2) == 0
-        b_left = xm * NZ + zsrc
-        b_right = xp * NZ + zsrc
-        wait_row(b_left, jnp.logical_and(cond, even))
-        start(row_copy(b_left, 2, {"x": xp}), jnp.logical_and(cond, even))
+        row_relay(xm * NZ + zsrc, ((2, {"x": xp}, None),), jnp.logical_and(cond, even))
         odd = jnp.logical_not(even)
-        wait_row(b_right, jnp.logical_and(cond, odd))
-        start(row_copy(b_right, 3, {"x": xm}), jnp.logical_and(cond, odd))
-
+        row_relay(xp * NZ + zsrc, ((3, {"x": xm}, None),), jnp.logical_and(cond, odd))
+
+    x_sends = ((2, {"x": xp}, None), (3, {"x": xm}, None))
     for k in range(1, NZ):
-        lo = z >= k
-        b = x * NZ + z - k
-        wait_row(b, lo)
-        start(row_copy(b, 0, {"zl": z + 1}), jnp.logical_and(lo, z < NZ - 1))
-        start(row_copy(b, 2, {"x": xp}), lo)
-        start(row_copy(b, 3, {"x": xm}), lo)
-        hi = z + k < NZ
-        b = x * NZ + z + k
-        wait_row(b, hi)
-        start(row_copy(b, 1, {"zl": z - 1}), jnp.logical_and(hi, z > 0))
-        start(row_copy(b, 2, {"x": xp}), hi)
-        start(row_copy(b, 3, {"x": xm}), hi)
+        row_relay(x * NZ + z - k, ((0, {"zl": z + 1}, z < NZ - 1),) + x_sends, z >= k)
+        row_relay(x * NZ + z + k, ((1, {"zl": z - 1}, z > 0),) + x_sends, z + k < NZ)
         if k == 1:
             x_forward(z, True)
-            wait_col(j_hc)
-            start(col_copy(j_hc, 2, {"y": yp}))
-            start(col_copy(j_hc, 3, {"y": ym}))
+            col_relay(j_hc, y_sends)
             for cc in range(2):
-                jl = (ym * 2 + 0) * 2 + cc
-                wait_col(jl)
-                start(col_copy(jl, 2, {"y": yp}))
-                jr = (yp * 2 + 1) * 2 + cc
-                wait_col(jr)
-                start(col_copy(jr, 3, {"y": ym}))
+                col_relay((ym * 2 + 0) * 2 + cc, ((2, {"y": yp}),))
+                col_relay((yp * 2 + 1) * 2 + cc, ((3, {"y": ym}),))
         else:
             x_forward(z - (k - 1), z >= k - 1)
             x_forward(z + (k - 1), z + (k - 1) < NZ)
@@ -214,22 +201,16 @@
 
     x2 = lax.rem(x + 2, NX)
     for zz in range(NZ):
-        if zz % 2 == 1:
-            wait_row(xm * NZ + zz)
-        else:
-            wait_row(xp * NZ + zz)
-        wait_row(x2 * NZ + zz)
+        row_relay(xm * NZ + zz if zz % 2 == 1 else xp * NZ + zz, ())
+        row_relay(x2 * NZ + zz, ())
     y2 = lax.rem(y + 2, NY)
     for cc in range(2):
-        wait_col((ym * 2 + 1) * 2 + cc)
-        wait_col((yp * 2 + 0) * 2 + cc)
+        col_relay((ym * 2 + 1) * 2 + cc, ())
+        col_relay((yp * 2 + 0) * 2 + cc, ())
         for hh in range(2):
-            wait_col((y2 * 2 + hh) * 2 + cc)
+            col_relay((y2 * 2 + hh) * 2 + cc, ())
     for desc, cond in started:
-        if cond is None:
-            desc.wait_send()
-        else:
-            pl.when(cond)(desc.wait_send)
+        when(cond, desc.wait_send)
 
 
 def gather_spectra(spectra_planes, row_count, col_count):
@@ -243,10 +224,10 @@
         in_specs=[pl.BlockSpec(memory_space=pltpu.VMEM)],
         out_specs=(pl.BlockSpec(memory_space=pltpu.VMEM), pl.BlockSpec(memory_space=pltpu.VMEM)),
         scratch_shapes=[
-            pltpu.SemaphoreType.DMA((row_count,)),
-            pltpu.SemaphoreType.DMA((col_count,)),
-            pltpu.SemaphoreType.DMA((row_count, 4)),
-            pltpu.SemaphoreType.DMA((col_count, 4)),
+            pltpu.SemaphoreType.DMA((row_count, 2)),
+            pltpu.SemaphoreType.DMA((col_count, 2)),
+            pltpu.SemaphoreType.DMA((row_count, 2, 4)),
+            pltpu.SemaphoreType.DMA((col_count, 2, 4)),
         ],
         compiler_params=pltpu.CompilerParams(collective_id=0, has_side_effects=True),
     )(spectra_planes)

time: 115 us -> 115 us (level)
  no operation moved by 1% of the time
where the time goes in v4:
time: 115 us; the launch traced here: 114 us
  Pallas kernels  96.2 us (84%)
  matrix products  9.48 us (8%)
  local copies, waits for them, and re-layouts  4 us (3%)
  other arithmetic  3.67 us (3%)
    pallas_call x1, Pallas kernels, gather_spectra(): pl.pallas_call(gather_kernel, out_shape=(jax.ShapeDtypeStruct((planes, ro...  73.9 us
    pallas_call x1, Pallas kernels, reduce_bands(): pl.pallas_call(reduce_kernel, out_shape=jax.ShapeDtypeStruct((band, width...  22.3 us
    dot_general x1, matrix products, complex_product(): jnp.einsum('qju,quy->qjy', left_section[1], right_section[1], preferred_e...  2.55 us
    dot_general x1, matrix products, complex_product(): jnp.einsum('qju,quy->qjy', left_section[0], right_section[0], preferred_e...  2.31 us

profile of v4, /device:TPU:1, one launch (start us, length us, event | category | flops | bytes accessed | tf_op | source)
XLA Modules:
  0.0 114.1 jit_solution(17556176297952862630)
XLA Ops:
  0.6 0.0 copy-start
  0.7 0.8 dynamic_slice.3
  1.4 1.9 %convert_reduce_fusion = f32[4,128]{1,0:T(4,128)S(1)} fusion(s32[128]{0:T(128)S(1)} %iota_add_fusion.1, s32[4,1024]{1,0:T(4,128)} %param.9), kind=kLoop, calls=%fused_computation.10 | loop fusion | flops 1572352 | bytes 18944 | tf_op jit(solution)/shard_map/reduce_sum | solution.py:31
  3.3 0.1 copy.14
  3.5 0.2 broadcast_in_dim.15
  3.7 0.1 fusion.38
  3.8 0.8 add_divide_fusion
  4.6 0.1 fusion.53
  4.7 1.4 %fusion.25 = bf16[1,8,64,128]{3,1,2,0:T(8,128)(2,1)S(1)} fusion(bf16[4,8,64,128]{3,2,1,0:T(8,128)(2,1)} %bitcast.72, f32[4,32]{1,0:T(4,128)S(1)} %get-tuple-element.19, f32[4,32]{1,0:T(4,128)S(1)} %get-tuple-element.18), kind=kOutput, calls=%fused_computation.22 | convolution fusion | flops 4260608 | bytes 656384 | tf_op jit(solution)/shard_map/dot_general | solution.py:304
  6.2 0.7 copy.36
  6.8 73.9 %shard_map.77 = (bf16[8,2048,128]{2,1,0:T(8,128)(2,1)}, bf16[8,64,2048]{2,1,0:T(8,128)(2,1)}) custom-call(bf16[8,64,128]{2,1,0:T(8,128)(2,1)} %bitcast.75), custom_call_target="tpu_custom_call" | custom-call | tf_op jit(solution)/shard_map/pallas_call | solution.py:218
  80.7 0.0 copy-start.5
  80.7 0.0 copy-start.4
  80.7 2.6 %fusion.2 = f32[4,64,128]{2,1,0:T(8,128)S(1)} fusion(bf16[2,4,2048,128]{3,2,1,0:T(8,128)(2,1)} %bitcast.77, bf16[2,4,64,2048]{3,2,1,0:T(8,128)(2,1)} %bitcast.81), kind=kOutput, calls=%fused_computation.4 | convolution fusion | flops 134217728 | bytes 3276800 | tf_op jit(solution)/shard_map/qju,quy->qjy/dot_general | solution.py:47
  83.3 0.0 copy-done.5
  83.3 2.3 %fusion.16 = f32[1,4,64,128]{3,2,1,0:T(8,128)S(1)} fusion(f32[4,64,128]{2,1,0:T(8,128)S(1)} %fusion.2, bf16[2,4,2048,128]{3,2,1,0:T(8,128)(2,1)} %bitcast.78, bf16[2,4,64,2048]{3,2,1,0:T(8,128)(2,1)S(1)} %bitcast.82), kind=kOutput, calls=%fused_computation.19 | convolution fusion | flops 134250496 | bytes 3407872 | tf_op jit(solution)/shard_map/qju,quy->qjy/dot_general | solution.py:44
  85.6 0.5 fusion
  86.1 0.0 copy-start.1
  86.1 0.5 fusion.22
  86.7 0.5 copy-done.1
  87.2 1.3 %fusion.12 = bf16[32,64,128]{2,0,1:T(8,128)(2,1)S(1)} fusion(bf16[32,64,128]{2,1,0:T(8,128)(2,1)S(1)} %copy-done.1, f32[1,8,64,128]{3,2,1,0:T(8,128)S(1)} %bitcast.74, f32[4,32]{1,0:T(4,128)S(1)} %get-tuple-element.19, f32[4,32]{1,0:T(4,128)S(1)} %get-tuple-element.18), kind=kOutput, calls=%fused_computation.16 | convolution fusion | flops 25952768 | bytes 1311744 | tf_op jit(solution)/shard_map/dot_general | solution.py:333
  88.5 0.0 copy-start.3
  88.5 0.2 copy.17
  88.7 0.0 copy-start.2
  88.7 0.7 multiply_reduce_fusion
  89.4 0.7 reshape.72.part_ref
  90.1 22.3 %shard_map.78 = f32[2,512]{1,0:T(2,128)} custom-call(f32[16,2,512]{2,1,0:T(2,128)} %reshape.72.part_ref), custom_call_target="tpu_custom_call" | custom-call | tf_op jit(solution)/shard_map/pallas_call | solution.py:281
  112.4 0.7 multiply_convert_fusion
  113.1 0.0 copy-done.3
  113.1 0.0 copy-done
  113.1 0.2 convolution_bitcast_fusion
  113.3 0.8 copy.18
  (7 shorter events, 0.1 us)
Async XLA Ops:
  0.6 112.4 %copy-start = (bf16[32,2,128]{2,1,0:T(2,128)(2,1)S(1)}, bf16[32,2,128]{2,1,0:T(2,128)(2,1)}, u32[]{:S(2)}) copy-start(bf16[32,2,128]{2,1,0:T(2,128)(2,1)} %param.11) | copy-start | bytes 49156
  80.7 2.6 %copy-start.5 = (bf16[8,64,2048]{2,1,0:T(8,128)(2,1)S(1)}, bf16[8,64,2048]{2,1,0:T(8,128)(2,1)}, u32[]{:S(2)}) copy-start(bf16[8,64,2048]{2,1,0:T(8,128)(2,1)} %get-tuple-element.8) | copy-start | bytes 6291460
  80.7 4.9 %copy-start.4 = (bf16[8,2048,128]{2,1,0:T(8,128)(2,1)S(1)}, bf16[8,2048,128]{2,1,0:T(8,128)(2,1)}, u32[]{:S(2)}) copy-start(bf16[8,2048,128]{2,1,0:T(8,128)(2,1)} %get-tuple-element.9) | copy-start | bytes 12582916
  86.1 1.0 copy-start.1
  88.5 24.6 %copy-start.3 = (s32[512]{0:T(512)S(1)}, s32[512]{0:T(512)}, u32[]{:S(2)}) copy-start(s32[512]{0:T(512)} %param.10) | copy-start | bytes 6148
  88.7 25.5 %copy-start.2 = (bf16[32,64,128]{2,1,0:T(8,128)(2,1)}, bf16[32,64,128]{2,1,0:T(8,128)(2,1)S(1)}, u32[]{:S(2)}) copy-start(bf16[32,64,128]{2,1,0:T(8,128)(2,1)S(1)} %copy.17) | copy-start | bytes 1572868

commit v5 on v4

--- a/solution.py
+++ b/solution.py
@@ -174,7 +174,6 @@
     j_c = (y * 2 + h) * 2 + 1 - c
     j_hc = (y * 2 + 1 - h) * 2 + 1 - c
     y_sends = ((2, {"y": yp}), (3, {"y": ym}))
-    col_relay(j_h, ((0, {"c": 1 - c}),) + y_sends)
     col_relay(j_c, y_sends)
 
     def x_forward(zsrc, cond):
@@ -183,21 +182,30 @@
         odd = jnp.logical_not(even)
         row_relay(xp * NZ + zsrc, ((3, {"x": xm}, None),), jnp.logical_and(cond, odd))
 
+    def x_forward_at(dist):
+        if dist == 0:
+            x_forward(z, True)
+        else:
+            x_forward(z - dist, z >= dist)
+            x_forward(z + dist, z + dist < NZ)
+
+    lag = 2
     x_sends = ((2, {"x": xp}, None), (3, {"x": xm}, None))
     for k in range(1, NZ):
         row_relay(x * NZ + z - k, ((0, {"zl": z + 1}, z < NZ - 1),) + x_sends, z >= k)
         row_relay(x * NZ + z + k, ((1, {"zl": z - 1}, z > 0),) + x_sends, z + k < NZ)
-        if k == 1:
-            x_forward(z, True)
+        if k - lag >= 0:
+            x_forward_at(k - lag)
+        if k == 2:
+            col_relay(j_h, ((0, {"c": 1 - c}),) + y_sends)
+        if k == 3:
             col_relay(j_hc, y_sends)
+        if k == 4:
             for cc in range(2):
                 col_relay((ym * 2 + 0) * 2 + cc, ((2, {"y": yp}),))
                 col_relay((yp * 2 + 1) * 2 + cc, ((3, {"y": ym}),))
-        else:
-            x_forward(z - (k - 1), z >= k - 1)
-            x_forward(z + (k - 1), z + (k - 1) < NZ)
-    x_forward(z - (NZ - 1), z >= NZ - 1)
-    x_forward(z + (NZ - 1), z + (NZ - 1) < NZ)
+    for dist in range(NZ - lag, NZ):
+        x_forward_at(dist)
 
     x2 = lax.rem(x + 2, NX)
     for zz in range(NZ):

time: 115 us -> 110 us (0.957)
  Pallas kernels: 96.2 us -> 91.4 us
    pallas_call x1, Pallas kernels: 22.3 us -> 19.3 us  [reduce_bands(): pl.pallas_call(reduce_kernel, out_shape=jax.ShapeDtypeStruct((band, width...]
    pallas_call x1, Pallas kernels: 73.9 us -> 72.1 us  [gather_spectra(): pl.pallas_call(gather_kernel, out_shape=(jax.ShapeDtypeStruct((planes, ro...]
where the time goes in v5:
time: 110 us; the launch traced here: 109 us
  Pallas kernels  91.4 us (83%)
  matrix products  9.48 us (9%)
  local copies, waits for them, and re-layouts  4 us (4%)
  other arithmetic  3.67 us (3%)
    pallas_call x1, Pallas kernels, gather_spectra(): pl.pallas_call(gather_kernel, out_shape=(jax.ShapeDtypeStruct((planes, ro...  72.1 us
    pallas_call x1, Pallas kernels, reduce_bands(): pl.pallas_call(reduce_kernel, out_shape=jax.ShapeDtypeStruct((band, width...  19.3 us
    dot_general x1, matrix products, complex_product(): jnp.einsum('qju,quy->qjy', left_section[1], right_section[1], preferred_e...  2.55 us
    dot_general x1, matrix products, complex_product(): jnp.einsum('qju,quy->qjy', left_section[0], right_section[0], preferred_e...  2.32 us
    unnamed x15, local copies, waits for them, and re-layouts  2.26 us

profile of v5, /device:TPU:1, one launch (start us, length us, event | category | flops | bytes accessed | tf_op | source)
XLA Modules:
  0.0 109.4 jit_solution(13864734192014852917)
XLA Ops:
  0.6 0.0 copy-start
  0.7 0.8 dynamic_slice.3
  1.4 1.9 %convert_reduce_fusion = f32[4,128]{1,0:T(4,128)S(1)} fusion(s32[128]{0:T(128)S(1)} %iota_add_fusion.1, s32[4,1024]{1,0:T(4,128)} %param.9), kind=kLoop, calls=%fused_computation.10 | loop fusion | flops 1572352 | bytes 18944 | tf_op jit(solution)/shard_map/reduce_sum | solution.py:31
  3.3 0.1 copy.14
  3.5 0.2 broadcast_in_dim.15
  3.7 0.1 fusion.38
  3.8 0.8 add_divide_fusion
  4.6 0.1 fusion.53
  4.7 1.4 %fusion.25 = bf16[1,8,64,128]{3,1,2,0:T(8,128)(2,1)S(1)} fusion(bf16[4,8,64,128]{3,2,1,0:T(8,128)(2,1)} %bitcast.72, f32[4,32]{1,0:T(4,128)S(1)} %get-tuple-element.19, f32[4,32]{1,0:T(4,128)S(1)} %get-tuple-element.18), kind=kOutput, calls=%fused_computation.22 | convolution fusion | flops 4260608 | bytes 656384 | tf_op jit(solution)/shard_map/dot_general | solution.py:312
  6.2 0.7 copy.36
  6.8 72.1 %shard_map.77 = (bf16[8,2048,128]{2,1,0:T(8,128)(2,1)}, bf16[8,64,2048]{2,1,0:T(8,128)(2,1)}) custom-call(bf16[8,64,128]{2,1,0:T(8,128)(2,1)} %bitcast.75), custom_call_target="tpu_custom_call" | custom-call | tf_op jit(solution)/shard_map/pallas_call | solution.py:226
  78.9 0.0 copy-start.5
  79.0 2.5 %fusion.2 = f32[4,64,128]{2,1,0:T(8,128)S(1)} fusion(bf16[2,4,2048,128]{3,2,1,0:T(8,128)(2,1)} %bitcast.77, bf16[2,4,64,2048]{3,2,1,0:T(8,128)(2,1)} %bitcast.81), kind=kOutput, calls=%fused_computation.4 | convolution fusion | flops 134217728 | bytes 3276800 | tf_op jit(solution)/shard_map/qju,quy->qjy/dot_general | solution.py:47
  81.5 2.3 %fusion.16 = f32[1,4,64,128]{3,2,1,0:T(8,128)S(1)} fusion(f32[4,64,128]{2,1,0:T(8,128)S(1)} %fusion.2, bf16[2,4,2048,128]{3,2,1,0:T(8,128)(2,1)} %bitcast.78, bf16[2,4,64,2048]{3,2,1,0:T(8,128)(2,1)S(1)} %bitcast.82), kind=kOutput, calls=%fused_computation.19 | convolution fusion | flops 134250496 | bytes 3407872 | tf_op jit(solution)/shard_map/qju,quy->qjy/dot_general | solution.py:44
  83.8 0.0 copy-done.4
  83.8 0.5 fusion
  84.3 0.0 copy-start.1
  84.4 0.5 fusion.22
  84.9 0.5 copy-done.1
  85.4 1.3 %fusion.12 = bf16[32,64,128]{2,0,1:T(8,128)(2,1)S(1)} fusion(bf16[32,64,128]{2,1,0:T(8,128)(2,1)S(1)} %copy-done.1, f32[1,8,64,128]{3,2,1,0:T(8,128)S(1)} %bitcast.74, f32[4,32]{1,0:T(4,128)S(1)} %get-tuple-element.19, f32[4,32]{1,0:T(4,128)S(1)} %get-tuple-element.18), kind=kOutput, calls=%fused_computation.16 | convolution fusion | flops 25952768 | bytes 1311744 | tf_op jit(solution)/shard_map/dot_general | solution.py:341
  86.7 0.0 copy-start.3
  86.7 0.2 copy.17
  86.9 0.0 copy-start.2
  86.9 0.7 multiply_reduce_fusion
  87.6 0.7 reshape.72.part_ref
  88.3 19.3 %shard_map.78 = f32[2,512]{1,0:T(2,128)} custom-call(f32[16,2,512]{2,1,0:T(2,128)} %reshape.72.part_ref), custom_call_target="tpu_custom_call" | custom-call | tf_op jit(solution)/shard_map/pallas_call | solution.py:289
  107.6 0.7 multiply_convert_fusion
  108.3 0.0 copy-done.3
  108.3 0.0 copy-done
  108.3 0.2 convolution_bitcast_fusion
  108.5 0.8 copy.18
  109.4 0.0 copy-done.2
  (7 shorter events, 0.1 us)
Async XLA Ops:
  0.6 107.7 %copy-start = (bf16[32,2,128]{2,1,0:T(2,128)(2,1)S(1)}, bf16[32,2,128]{2,1,0:T(2,128)(2,1)}, u32[]{:S(2)}) copy-start(bf16[32,2,128]{2,1,0:T(2,128)(2,1)} %param.11) | copy-start | bytes 49156
  78.9 2.6 %copy-start.5 = (bf16[8,64,2048]{2,1,0:T(8,128)(2,1)S(1)}, bf16[8,64,2048]{2,1,0:T(8,128)(2,1)}, u32[]{:S(2)}) copy-start(bf16[8,64,2048]{2,1,0:T(8,128)(2,1)} %get-tuple-element.8) | copy-start | bytes 6291460
  78.9 4.9 %copy-start.4 = (bf16[8,2048,128]{2,1,0:T(8,128)(2,1)S(1)}, bf16[8,2048,128]{2,1,0:T(8,128)(2,1)}, u32[]{:S(2)}) copy-start(bf16[8,2048,128]{2,1,0:T(8,128)(2,1)} %get-tuple-element.9) | copy-start | bytes 12582916
  84.3 1.0 copy-start.1
  86.7 21.6 %copy-start.3 = (s32[512]{0:T(512)S(1)}, s32[512]{0:T(512)}, u32[]{:S(2)}) copy-start(s32[512]{0:T(512)} %param.10) | copy-start | bytes 6148
  86.9 22.5 %copy-start.2 = (bf16[32,64,128]{2,1,0:T(8,128)(2,1)}, bf16[32,64,128]{2,1,0:T(8,128)(2,1)S(1)}, u32[]{:S(2)}) copy-start(bf16[32,64,128]{2,1,0:T(8,128)(2,1)S(1)} %copy.17) | copy-start | bytes 1572868

commit v6 on v5

--- a/solution.py
+++ b/solution.py
@@ -74,7 +74,10 @@
 NX, NZ, NY = 4, 8, 4
 
 
-def gather_kernel(spec_ref, colw_ref, roww_ref, recv_row, recv_col, send_row, send_col):
+def fused_kernel(spec_ref, traces_ref, aperture_ref, weights_ref, inverse_ref,
+                 prim_ref, stack_ref,
+                 colw_ref, roww_ref, mult_ref, partial_ref, slots_ref,
+                 recv_row, recv_col, send_row, send_col, recv_red, send_red):
     x = lax.axis_index("x")
     z = lax.axis_index("zl")
     y = lax.axis_index("y")
@@ -87,9 +90,21 @@
     me_row = x * NZ + z
     me_col = (y * 2 + h) * 2 + c
 
+    col_peers = []
+    for yy in range(NY):
+        for hh in range(2):
+            for cc in range(2):
+                col_peers.append(((yy * 2 + hh) * 2 + cc, {"y": yy, "zh": hh, "c": cc}))
+
     barrier = pltpu.get_barrier_semaphore()
-    for peer in ({"x": xp}, {"x": xm}, {"y": yp}, {"y": ym}, {"zh": 1 - h}, {"c": 1 - c}):
+    for peer in ({"x": xp}, {"x": xm}):
         pl.semaphore_signal(barrier, 1, device_id=peer, device_id_type=MESH_ID)
+    for j, peer in col_peers:
+        pl.when(j != me_col)(
+            lambda peer=peer: pl.semaphore_signal(
+                barrier, 1, device_id=peer, device_id_type=MESH_ID
+            )
+        )
 
     @pl.when(z > 0)
     def _():
@@ -99,9 +114,10 @@
     def _():
         pl.semaphore_signal(barrier, 1, device_id={"zl": z + 1}, device_id_type=MESH_ID)
 
+    peers_in = 2 + len(col_peers) - 1
     ends = jnp.logical_or(z == 0, z == NZ - 1)
-    pl.when(ends)(lambda: pl.semaphore_wait(barrier, 7))
-    pl.when(jnp.logical_not(ends))(lambda: pl.semaphore_wait(barrier, 8))
+    pl.when(ends)(lambda: pl.semaphore_wait(barrier, peers_in + 1))
+    pl.when(jnp.logical_not(ends))(lambda: pl.semaphore_wait(barrier, peers_in + 2))
 
     started = []
     shots = spec_ref.shape[1]
@@ -217,87 +233,98 @@
         col_relay((yp * 2 + 0) * 2 + cc, ())
         for hh in range(2):
             col_relay((y2 * 2 + hh) * 2 + cc, ())
+    nf = spec_ref.shape[0] // 2
+    surface_root = math.sqrt(roww_ref.shape[2])
+    for f in range(nf):
+        lr = roww_ref[f]
+        li = roww_ref[nf + f]
+        rr = colw_ref[f]
+        ri = colw_ref[nf + f]
+        real_real = jnp.dot(lr, rr, preferred_element_type=jnp.float32)
+        imag_imag = jnp.dot(li, ri, preferred_element_type=jnp.float32)
+        real_imag = jnp.dot(lr, ri, preferred_element_type=jnp.float32)
+        imag_real = jnp.dot(li, rr, preferred_element_type=jnp.float32)
+        mult_ref[f] = -(real_real - imag_imag) / surface_root
+        mult_ref[nf + f] = -(real_imag + imag_real) / surface_root
+
+    def prim_body(t, carry):
+        wave = inverse_ref[t, 0] * mult_ref[0]
+        for p in range(1, 2 * nf):
+            wave = wave + inverse_ref[t, p] * mult_ref[p]
+        prim_ref[t] = (traces_ref[t].astype(jnp.float32) - wave).astype(prim_ref.dtype)
+        return carry
+
+    lax.fori_loop(0, traces_ref.shape[0], prim_body, 0)
+
+    band = partial_ref.shape[1]
+
+    def band_body(j, carry):
+        rows = []
+        for u in range(band):
+            stacked = jnp.dot(
+                prim_ref[j * band + u], aperture_ref[...], preferred_element_type=jnp.float32
+            )
+            rows.append(jnp.sum(stacked * weights_ref[...], axis=0, keepdims=True))
+        partial_ref[j] = jnp.concatenate(rows, axis=0)
+        return carry
+
+    lax.fori_loop(0, partial_ref.shape[0], band_body, 0)
+
+    reduce_sends = []
+    for j, peer in col_peers:
+        desc = pltpu.make_async_remote_copy(
+            partial_ref.at[j], slots_ref.at[me_col], send_red.at[j], recv_red.at[me_col],
+            device_id=peer, device_id_type=MESH_ID,
+        )
+        pl.when(j != me_col)(desc.start)
+        reduce_sends.append((j, desc))
+    slots_ref[me_col] = partial_ref[me_col]
+    for j, peer in col_peers:
+        recv = pltpu.make_async_remote_copy(
+            partial_ref.at[j], slots_ref.at[j], send_red.at[j], recv_red.at[j],
+            device_id=peer, device_id_type=MESH_ID,
+        )
+        pl.when(j != me_col)(recv.wait_recv)
+    total = slots_ref[0]
+    for j in range(1, len(col_peers)):
+        total = total + slots_ref[j]
+    stack_ref[...] = total
+
     for desc, cond in started:
         when(cond, desc.wait_send)
-
-
-def gather_spectra(spectra_planes, row_count, col_count):
-    planes, shots, recvs = spectra_planes.shape
+    for j, desc in reduce_sends:
+        pl.when(j != me_col)(desc.wait_send)
+
+
+def fused_call(spec, traces, aperture, weights, inverse, row_count, col_count):
+    planes, shots, recvs = spec.shape
+    samples = traces.shape[0]
+    band = samples // col_count
+    width = aperture.shape[1]
+    vmem = pl.BlockSpec(memory_space=pltpu.VMEM)
     return pl.pallas_call(
-        gather_kernel,
+        fused_kernel,
         out_shape=(
-            jax.ShapeDtypeStruct((planes, row_count * shots, recvs), spectra_planes.dtype),
-            jax.ShapeDtypeStruct((planes, shots, col_count * recvs), spectra_planes.dtype),
+            jax.ShapeDtypeStruct(traces.shape, jnp.bfloat16),
+            jax.ShapeDtypeStruct((band, width), jnp.float32),
         ),
-        in_specs=[pl.BlockSpec(memory_space=pltpu.VMEM)],
-        out_specs=(pl.BlockSpec(memory_space=pltpu.VMEM), pl.BlockSpec(memory_space=pltpu.VMEM)),
+        in_specs=[vmem, vmem, vmem, vmem, pl.BlockSpec(memory_space=pltpu.SMEM)],
+        out_specs=(vmem, vmem),
         scratch_shapes=[
+            pltpu.VMEM((planes, row_count * shots, recvs), spec.dtype),
+            pltpu.VMEM((planes, shots, col_count * recvs), spec.dtype),
+            pltpu.VMEM((planes, shots, recvs), jnp.float32),
+            pltpu.VMEM((col_count, band, width), jnp.float32),
+            pltpu.VMEM((col_count, band, width), jnp.float32),
             pltpu.SemaphoreType.DMA((row_count, 2)),
             pltpu.SemaphoreType.DMA((col_count, 2)),
             pltpu.SemaphoreType.DMA((row_count, 2, 4)),
             pltpu.SemaphoreType.DMA((col_count, 2, 4)),
-        ],
-        compiler_params=pltpu.CompilerParams(collective_id=0, has_side_effects=True),
-    )(spectra_planes)
-
-
-def reduce_kernel(part_ref, out_ref, slots, recv_sem, send_sem):
-    y = lax.axis_index("y")
-    h = lax.axis_index("zh")
-    c = lax.axis_index("c")
-    me = (y * 2 + h) * 2 + c
-    peers = []
-    for yy in range(NY):
-        for hh in range(2):
-            for cc in range(2):
-                peers.append(((yy * 2 + hh) * 2 + cc, {"y": yy, "zh": hh, "c": cc}))
-    barrier = pltpu.get_barrier_semaphore()
-    for j, peer in peers:
-        pl.when(j != me)(
-            lambda peer=peer: pl.semaphore_signal(
-                barrier, 1, device_id=peer, device_id_type=MESH_ID
-            )
-        )
-    pl.semaphore_wait(barrier, len(peers) - 1)
-    copies = []
-    for j, peer in peers:
-        desc = pltpu.make_async_remote_copy(
-            part_ref.at[j], slots.at[me], send_sem.at[j], recv_sem.at[me],
-            device_id=peer, device_id_type=MESH_ID,
-        )
-        pl.when(j != me)(desc.start)
-        copies.append((j, desc))
-    slots[me] = part_ref[me]
-    for j, desc in copies:
-        recv = pltpu.make_async_remote_copy(
-            part_ref.at[j], slots.at[j], send_sem.at[j], recv_sem.at[j],
-            device_id={"y": y}, device_id_type=MESH_ID,
-        )
-        pl.when(j != me)(recv.wait_recv)
-    total = slots[0]
-    for j in range(1, len(peers)):
-        total = total + slots[j]
-    out_ref[...] = total
-    for j, desc in copies:
-        pl.when(j != me)(desc.wait_send)
-
-
-def reduce_bands(partial, col_count):
-    rows, width = partial.shape
-    band = rows // col_count
-    parts = partial.reshape(col_count, band, width)
-    return pl.pallas_call(
-        reduce_kernel,
-        out_shape=jax.ShapeDtypeStruct((band, width), partial.dtype),
-        in_specs=[pl.BlockSpec(memory_space=pltpu.VMEM)],
-        out_specs=pl.BlockSpec(memory_space=pltpu.VMEM),
-        scratch_shapes=[
-            pltpu.VMEM((col_count, band, width), partial.dtype),
             pltpu.SemaphoreType.DMA((col_count,)),
             pltpu.SemaphoreType.DMA((col_count,)),
         ],
-        compiler_params=pltpu.CompilerParams(collective_id=1, has_side_effects=True),
-    )(parts)
+        compiler_params=pltpu.CompilerParams(collective_id=0, has_side_effects=True),
+    )(spec, traces, aperture, weights, inverse)
 
 
 def per_device(traces, source_pos, receiver_pos, aperture_list, band_index, weight_tiles):
@@ -314,13 +341,7 @@
         traces.reshape(samples, shot_count * recv_count),
         preferred_element_type=jnp.float32,
     )
-    spectra = spectra.astype(jnp.bfloat16).reshape(2, NF, shot_count, recv_count)
-
-    colw, roww = gather_spectra(
-        spectra.reshape(2 * NF, shot_count, recv_count), row_count, col_count
-    )
-    columns_whole = colw.reshape(2, NF, row_count * shot_count, recv_count)
-    rows_whole = roww.reshape(2, NF, shot_count, surface_count)
+    spectra = spectra.astype(jnp.bfloat16)
 
     col_pos = axis_pos(COL)
     row_pos = axis_pos(ROW)
@@ -331,30 +352,16 @@
     aperture = aperture_rows(
         aperture_list, my_receivers, columns, col_pos * recv_count, recv_count, spread_len
     )
-    rows_whole, columns_whole, aperture, stacking_weights = lax.optimization_barrier(
-        (rows_whole, columns_whole, aperture, stacking_weights)
-    )
-
-    summed = complex_product(rows_whole, columns_whole)
-    multiples = -summed / math.sqrt(surface_count)
     inverse = jnp.concatenate([cosine, -sine_table], 0).T / math.sqrt(NF)
-    wave_field = jnp.dot(
+    primaries, stacked = fused_call(
+        spectra.reshape(2 * NF, shot_count, recv_count),
+        traces,
+        aperture,
+        stacking_weights,
         inverse,
-        multiples.reshape(2 * NF, shot_count * recv_count),
-        precision=lax.Precision.HIGHEST,
-        preferred_element_type=jnp.float32,
-    )
-    primaries = (
-        traces.astype(jnp.float32) - wave_field.reshape(samples, shot_count, recv_count)
-    ).astype(jnp.bfloat16)
-
-    partial = jnp.dot(
-        primaries.reshape(samples * shot_count, recv_count),
-        aperture,
-        preferred_element_type=jnp.float32,
-    ).reshape(samples, shot_count, image_panel_width)
-    partial = jnp.sum(partial * stacking_weights[None], axis=1)
-    stacked = reduce_bands(partial, col_count)
+        row_count,
+        col_count,
+    )
     column_stack = (stacked / math.sqrt(shot_count)).astype(jnp.bfloat16)
 
     tile_kinds = weight_tiles.shape[0]

time: 110 us -> 93.1 us (0.85)
  Pallas kernels: 91.4 us -> 83.3 us
  matrix products: 9.48 us -> 1.65 us
    pallas_call x2 -> x1, Pallas kernels: 91.4 us -> 83.3 us  [fused_call(): pl.pallas_call(fused_kernel, out_shape=(jax.ShapeDtypeStruct(traces.shape...]
    dot_general x6 -> x0, matrix products: 7.83 us -> none  [the longest x1 2.55 us: complex_product(): jnp.einsum('qju,quy->qjy', left_section[1], right_section[1], preferred_e...]
    reduce_sum x1, other arithmetic: 1.91 us -> 0.78 us  [aperture_rows(): member = jnp.sum(hits, axis=1)]
    unnamed x15 -> x13, local copies, waits for them, and re-layouts: 2.26 us -> 2.34 us
where the time goes in v6:
time: 93.1 us; the launch traced here: 92.9 us
  Pallas kernels  83.3 us (89%)
  other arithmetic  3.81 us (4%)
  local copies, waits for them, and re-layouts  3.5 us (4%)
  matrix products  1.65 us (2%)
    pallas_call x1, Pallas kernels, fused_call(): pl.pallas_call(fused_kernel, out_shape=(jax.ShapeDtypeStruct(traces.shape...  83.3 us
    unnamed x13, local copies, waits for them, and re-layouts  2.34 us

profile of v6, /device:TPU:1, one launch (start us, length us, event | category | flops | bytes accessed | tf_op | source)
XLA Modules:
  0.0 92.9 jit_solution(3264665347396839833)
XLA Ops:
  0.6 0.0 copy-start
  0.6 0.0 copy-start.2
  0.7 0.1 fusion.14
  0.8 1.4 %fusion = bf16[1,8,64,128]{3,1,2,0:T(8,128)(2,1)S(1)} fusion(bf16[4,8,64,128]{3,2,1,0:T(8,128)(2,1)} %bitcast.23, f32[4,32]{1,0:T(4,128)S(1)} %get-tuple-element.15, f32[4,32]{1,0:T(4,128)S(1)} %get-tuple-element.14), kind=kOutput, calls=%fused_computation.3 | convolution fusion | flops 4260608 | bytes 656384 | tf_op jit(solution)/shard_map/dot_general | solution.py:339
  2.2 0.0 copy-start.4
  2.2 0.7 copy.33
  2.9 0.0 copy-done.2
  2.9 0.8 convert_reduce_fusion
  3.7 0.1 copy.17
  3.8 0.2 broadcast_in_dim.15
  4.0 0.8 dynamic_slice.3
  4.8 0.8 fusion.4.aperture_ref
  5.6 0.0 copy-done.4
  5.6 0.7 add_divide_fusion.weights_ref
  6.4 0.0 copy-start.3
  6.4 0.1 copy.18
  6.4 0.6 multiply_bitcast_fusion.inverse_ref
  7.0 83.3 %shard_map.77 = (bf16[32,64,128]{2,1,0:T(8,128)(2,1)}, f32[2,512]{1,0:T(2,128)}) custom-call(bf16[8,64,128]{2,1,0:T(8,128)(2,1)} %bitcast.25, bf16[32,64,128]{2,1,0:T(8,128)(2,1)} %traces_ref.1, bf16[128,512]{1,0:T(8,128)(2,1)} %fusion.4.aperture_ref, f32[64,512]{1,0:T(8,128)} %add_divide_fusion.weights_ref, f32[32,8]{1,0:T(8,128)} %multiply_bitcast_fusion.inverse_ref), custom_call_target="tpu_custom_call" | custom-call | tf_op jit(solution)/shard_map/pallas_call | solution.py:305
  90.3 0.0 copy-start.1
  90.3 0.0 copy-done.3
  90.4 0.7 multiply_convert_fusion
  91.1 0.0 copy-done
  91.1 0.2 convolution_bitcast_fusion
  91.3 0.8 copy.21
  92.1 0.0 copy-done.1
  92.1 0.8 copy.35
  (5 shorter events, 0.0 us)
Async XLA Ops:
  0.6 90.4 %copy-start = (bf16[32,2,128]{2,1,0:T(2,128)(2,1)S(1)}, bf16[32,2,128]{2,1,0:T(2,128)(2,1)}, u32[]{:S(2)}) copy-start(bf16[32,2,128]{2,1,0:T(2,128)(2,1)} %param.11) | copy-start | bytes 49156
  0.6 2.3 %copy-start.2 = (s32[4,1024]{1,0:T(4,128)S(1)}, s32[4,1024]{1,0:T(4,128)}, u32[]{:S(2)}) copy-start(s32[4,1024]{1,0:T(4,128)} %param.9) | copy-start | bytes 49156
  2.2 3.4 %copy-start.4 = (s32[64]{0:T(128)S(1)}, s32[64]{0:T(128)}, u32[]{:S(2)}) copy-start(s32[64]{0:T(128)} %param.7) | copy-start | bytes 772
  6.4 84.0 %copy-start.3 = (s32[512]{0:T(512)S(1)}, s32[512]{0:T(512)}, u32[]{:S(2)}) copy-start(s32[512]{0:T(512)} %param.10) | copy-start | bytes 6148
  90.3 1.8 %copy-start.1 = (bf16[32,64,128]{2,1,0:T(8,128)(2,1)S(1)}, bf16[32,64,128]{2,1,0:T(8,128)(2,1)}, u32[]{:S(2)}) copy-start(bf16[32,64,128]{2,1,0:T(8,128)(2,1)} %get-tuple-element.18) | copy-start | bytes 1572868

commit v7 on v6

--- a/solution.py
+++ b/solution.py
@@ -176,7 +176,6 @@
 
     for part in parts:
         start(col_copy(me_col, part, 0, {"c": 1 - c}, own=True))
-        start(col_copy(me_col, part, 1, {"zh": 1 - h}, own=True))
         start(row_copy(me_row, part, 0, {"zl": z + 1}, own=True), z < NZ - 1)
         start(row_copy(me_row, part, 1, {"zl": z - 1}, own=True), z > 0)
         start(row_copy(me_row, part, 2, {"x": xp}, own=True))
@@ -213,10 +212,13 @@
         if k - lag >= 0:
             x_forward_at(k - lag)
         if k == 2:
+            for part in parts:
+                start(col_copy(me_col, part, 1, {"zh": 1 - h}, own=True))
+        if k == 4:
             col_relay(j_h, ((0, {"c": 1 - c}),) + y_sends)
-        if k == 3:
+        if k == 5:
             col_relay(j_hc, y_sends)
-        if k == 4:
+        if k == 6:
             for cc in range(2):
                 col_relay((ym * 2 + 0) * 2 + cc, ((2, {"y": yp}),))
                 col_relay((yp * 2 + 1) * 2 + cc, ((3, {"y": ym}),))

time: 93.1 us -> 91.5 us (0.983)
  Pallas kernels: 83.3 us -> 81.7 us
    pallas_call x1, Pallas kernels: 83.3 us -> 81.7 us  [fused_call(): pl.pallas_call(fused_kernel, out_shape=(jax.ShapeDtypeStruct(traces.shape...]
where the time goes in v7:
time: 91.5 us; the launch traced here: 91.3 us
  Pallas kernels  81.7 us (89%)
  other arithmetic  3.81 us (4%)
  local copies, waits for them, and re-layouts  3.5 us (4%)
  matrix products  1.65 us (2%)
    pallas_call x1, Pallas kernels, fused_call(): pl.pallas_call(fused_kernel, out_shape=(jax.ShapeDtypeStruct(traces.shape...  81.7 us
    unnamed x13, local copies, waits for them, and re-layouts  2.34 us

profile of v7, /device:TPU:1, one launch (start us, length us, event | category | flops | bytes accessed | tf_op | source)
XLA Modules:
  0.0 91.3 jit_solution(11965856666901545096)
XLA Ops:
  0.6 0.0 copy-start
  0.6 0.0 copy-start.2
  0.7 0.1 fusion.14
  0.8 1.4 %fusion = bf16[1,8,64,128]{3,1,2,0:T(8,128)(2,1)S(1)} fusion(bf16[4,8,64,128]{3,2,1,0:T(8,128)(2,1)} %bitcast.23, f32[4,32]{1,0:T(4,128)S(1)} %get-tuple-element.15, f32[4,32]{1,0:T(4,128)S(1)} %get-tuple-element.14), kind=kOutput, calls=%fused_computation.3 | convolution fusion | flops 4260608 | bytes 656384 | tf_op jit(solution)/shard_map/dot_general | solution.py:341
  2.2 0.0 copy-start.4
  2.2 0.7 copy.33
  2.9 0.0 copy-done.2
  2.9 0.8 convert_reduce_fusion
  3.7 0.1 copy.17
  3.8 0.2 broadcast_in_dim.15
  4.0 0.8 dynamic_slice.3
  4.8 0.8 fusion.4.aperture_ref
  5.6 0.0 copy-done.4
  5.6 0.7 add_divide_fusion.weights_ref
  6.4 0.0 copy-start.3
  6.4 0.1 copy.18
  6.4 0.6 multiply_bitcast_fusion.inverse_ref
  7.0 81.7 %shard_map.77 = (bf16[32,64,128]{2,1,0:T(8,128)(2,1)}, f32[2,512]{1,0:T(2,128)}) custom-call(bf16[8,64,128]{2,1,0:T(8,128)(2,1)} %bitcast.25, bf16[32,64,128]{2,1,0:T(8,128)(2,1)} %traces_ref.1, bf16[128,512]{1,0:T(8,128)(2,1)} %fusion.4.aperture_ref, f32[64,512]{1,0:T(8,128)} %add_divide_fusion.weights_ref, f32[32,8]{1,0:T(8,128)} %multiply_bitcast_fusion.inverse_ref), custom_call_target="tpu_custom_call" | custom-call | tf_op jit(solution)/shard_map/pallas_call | solution.py:307
  88.7 0.0 copy-start.1
  88.7 0.0 copy-done.3
  88.8 0.7 multiply_convert_fusion
  89.5 0.0 copy-done
  89.5 0.2 convolution_bitcast_fusion
  89.7 0.8 copy.21
  90.5 0.0 copy-done.1
  90.5 0.8 copy.35
  (5 shorter events, 0.0 us)
Async XLA Ops:
  0.6 88.9 %copy-start = (bf16[32,2,128]{2,1,0:T(2,128)(2,1)S(1)}, bf16[32,2,128]{2,1,0:T(2,128)(2,1)}, u32[]{:S(2)}) copy-start(bf16[32,2,128]{2,1,0:T(2,128)(2,1)} %param.11) | copy-start | bytes 49156
  0.6 2.3 %copy-start.2 = (s32[4,1024]{1,0:T(4,128)S(1)}, s32[4,1024]{1,0:T(4,128)}, u32[]{:S(2)}) copy-start(s32[4,1024]{1,0:T(4,128)} %param.9) | copy-start | bytes 49156
  2.2 3.4 %copy-start.4 = (s32[64]{0:T(128)S(1)}, s32[64]{0:T(128)}, u32[]{:S(2)}) copy-start(s32[64]{0:T(128)} %param.7) | copy-start | bytes 772
  6.4 82.4 %copy-start.3 = (s32[512]{0:T(512)S(1)}, s32[512]{0:T(512)}, u32[]{:S(2)}) copy-start(s32[512]{0:T(512)} %param.10) | copy-start | bytes 6148
  88.7 1.8 %copy-start.1 = (bf16[32,64,128]{2,1,0:T(8,128)(2,1)S(1)}, bf16[32,64,128]{2,1,0:T(8,128)(2,1)}, u32[]{:S(2)}) copy-start(bf16[32,64,128]{2,1,0:T(8,128)(2,1)} %get-tuple-element.18) | copy-start | bytes 1572868

commit v8 on v7

--- a/solution.py
+++ b/solution.py
@@ -87,6 +87,7 @@
     xm = lax.rem(x + NX - 1, NX)
     yp = lax.rem(y + 1, NY)
     ym = lax.rem(y + NY - 1, NY)
+    x2 = lax.rem(x + 2, NX)
     me_row = x * NZ + z
     me_col = (y * 2 + h) * 2 + c
 
@@ -97,7 +98,7 @@
                 col_peers.append(((yy * 2 + hh) * 2 + cc, {"y": yy, "zh": hh, "c": cc}))
 
     barrier = pltpu.get_barrier_semaphore()
-    for peer in ({"x": xp}, {"x": xm}):
+    for peer in ({"x": xp}, {"x": xm}, {"x": x2}):
         pl.semaphore_signal(barrier, 1, device_id=peer, device_id_type=MESH_ID)
     for j, peer in col_peers:
         pl.when(j != me_col)(
@@ -114,7 +115,7 @@
     def _():
         pl.semaphore_signal(barrier, 1, device_id={"zl": z + 1}, device_id_type=MESH_ID)
 
-    peers_in = 2 + len(col_peers) - 1
+    peers_in = 3 + len(col_peers) - 1
     ends = jnp.logical_or(z == 0, z == NZ - 1)
     pl.when(ends)(lambda: pl.semaphore_wait(barrier, peers_in + 1))
     pl.when(jnp.logical_not(ends))(lambda: pl.semaphore_wait(barrier, peers_in + 2))
@@ -180,6 +181,7 @@
         start(row_copy(me_row, part, 1, {"zl": z - 1}, own=True), z > 0)
         start(row_copy(me_row, part, 2, {"x": xp}, own=True))
         start(row_copy(me_row, part, 3, {"x": xm}, own=True))
+        start(row_copy(me_row, part, 4, {"x": x2}, own=True))
         start(col_copy(me_col, part, 2, {"y": yp}, own=True))
         start(col_copy(me_col, part, 3, {"y": ym}, own=True))
     colw_ref[:, pl.ds(pl.multiple_of(me_row * shots, shots), shots), :] = spec_ref[...]
@@ -191,26 +193,10 @@
     y_sends = ((2, {"y": yp}), (3, {"y": ym}))
     col_relay(j_c, y_sends)
 
-    def x_forward(zsrc, cond):
-        even = lax.rem(zsrc, 2) == 0
-        row_relay(xm * NZ + zsrc, ((2, {"x": xp}, None),), jnp.logical_and(cond, even))
-        odd = jnp.logical_not(even)
-        row_relay(xp * NZ + zsrc, ((3, {"x": xm}, None),), jnp.logical_and(cond, odd))
-
-    def x_forward_at(dist):
-        if dist == 0:
-            x_forward(z, True)
-        else:
-            x_forward(z - dist, z >= dist)
-            x_forward(z + dist, z + dist < NZ)
-
-    lag = 2
-    x_sends = ((2, {"x": xp}, None), (3, {"x": xm}, None))
+    x_sends = ((2, {"x": xp}, None), (3, {"x": xm}, None), (4, {"x": x2}, None))
     for k in range(1, NZ):
         row_relay(x * NZ + z - k, ((0, {"zl": z + 1}, z < NZ - 1),) + x_sends, z >= k)
         row_relay(x * NZ + z + k, ((1, {"zl": z - 1}, z > 0),) + x_sends, z + k < NZ)
-        if k - lag >= 0:
-            x_forward_at(k - lag)
         if k == 2:
             for part in parts:
                 start(col_copy(me_col, part, 1, {"zh": 1 - h}, own=True))
@@ -222,12 +208,10 @@
             for cc in range(2):
                 col_relay((ym * 2 + 0) * 2 + cc, ((2, {"y": yp}),))
                 col_relay((yp * 2 + 1) * 2 + cc, ((3, {"y": ym}),))
-    for dist in range(NZ - lag, NZ):
-        x_forward_at(dist)
-
-    x2 = lax.rem(x + 2, NX)
+
     for zz in range(NZ):
-        row_relay(xm * NZ + zz if zz % 2 == 1 else xp * NZ + zz, ())
+        row_relay(xm * NZ + zz, ())
+        row_relay(xp * NZ + zz, ())
         row_relay(x2 * NZ + zz, ())
     y2 = lax.rem(y + 2, NY)
     for cc in range(2):
@@ -320,7 +304,7 @@
             pltpu.VMEM((col_count, band, width), jnp.float32),
             pltpu.SemaphoreType.DMA((row_count, 2)),
             pltpu.SemaphoreType.DMA((col_count, 2)),
-            pltpu.SemaphoreType.DMA((row_count, 2, 4)),
+            pltpu.SemaphoreType.DMA((row_count, 2, 5)),
             pltpu.SemaphoreType.DMA((col_count, 2, 4)),
             pltpu.SemaphoreType.DMA((col_count,)),
             pltpu.SemaphoreType.DMA((col_count,)),

time: 91.5 us -> 93.4 us (1.021)
  Pallas kernels: 81.7 us -> 83.5 us
    pallas_call x1, Pallas kernels: 81.7 us -> 83.5 us  [fused_call(): pl.pallas_call(fused_kernel, out_shape=(jax.ShapeDtypeStruct(traces.shape...]
where the time goes in v8:
time: 93.4 us; the launch traced here: 93.2 us
  Pallas kernels  83.5 us (89%)
  other arithmetic  3.81 us (4%)
  local copies, waits for them, and re-layouts  3.5 us (4%)
  matrix products  1.65 us (2%)
    pallas_call x1, Pallas kernels, fused_call(): pl.pallas_call(fused_kernel, out_shape=(jax.ShapeDtypeStruct(traces.shape...  83.5 us
    unnamed x13, local copies, waits for them, and re-layouts  2.34 us

profile of v8, /device:TPU:1, one launch (start us, length us, event | category | flops | bytes accessed | tf_op | source)
XLA Modules:
  0.0 93.2 jit_solution(5864880343124142685)
XLA Ops:
  0.6 0.0 copy-start
  0.6 0.0 copy-start.2
  0.7 0.1 fusion.14
  0.8 1.4 %fusion = bf16[1,8,64,128]{3,1,2,0:T(8,128)(2,1)S(1)} fusion(bf16[4,8,64,128]{3,2,1,0:T(8,128)(2,1)} %bitcast.23, f32[4,32]{1,0:T(4,128)S(1)} %get-tuple-element.15, f32[4,32]{1,0:T(4,128)S(1)} %get-tuple-element.14), kind=kOutput, calls=%fused_computation.3 | convolution fusion | flops 4260608 | bytes 656384 | tf_op jit(solution)/shard_map/dot_general | solution.py:325
  2.2 0.0 copy-start.4
  2.2 0.7 copy.33
  2.9 0.0 copy-done.2
  2.9 0.8 convert_reduce_fusion
  3.7 0.1 copy.17
  3.8 0.2 broadcast_in_dim.15
  4.0 0.8 dynamic_slice.3
  4.8 0.8 fusion.4.aperture_ref
  5.6 0.0 copy-done.4
  5.6 0.7 add_divide_fusion.weights_ref
  6.4 0.0 copy-start.3
  6.4 0.1 copy.18
  6.4 0.6 multiply_bitcast_fusion.inverse_ref
  7.0 83.5 %shard_map.77 = (bf16[32,64,128]{2,1,0:T(8,128)(2,1)}, f32[2,512]{1,0:T(2,128)}) custom-call(bf16[8,64,128]{2,1,0:T(8,128)(2,1)} %bitcast.25, bf16[32,64,128]{2,1,0:T(8,128)(2,1)} %traces_ref.1, bf16[128,512]{1,0:T(8,128)(2,1)} %fusion.4.aperture_ref, f32[64,512]{1,0:T(8,128)} %add_divide_fusion.weights_ref, f32[32,8]{1,0:T(8,128)} %multiply_bitcast_fusion.inverse_ref), custom_call_target="tpu_custom_call" | custom-call | tf_op jit(solution)/shard_map/pallas_call | solution.py:291
  90.5 0.0 copy-start.1
  90.6 0.0 copy-done.3
  90.6 0.7 multiply_convert_fusion
  91.3 0.0 copy-done
  91.3 0.2 convolution_bitcast_fusion
  91.5 0.8 copy.21
  92.4 0.0 copy-done.1
  92.4 0.8 copy.35
  (5 shorter events, 0.0 us)
Async XLA Ops:
  0.6 90.7 %copy-start = (bf16[32,2,128]{2,1,0:T(2,128)(2,1)S(1)}, bf16[32,2,128]{2,1,0:T(2,128)(2,1)}, u32[]{:S(2)}) copy-start(bf16[32,2,128]{2,1,0:T(2,128)(2,1)} %param.11) | copy-start | bytes 49156
  0.6 2.3 %copy-start.2 = (s32[4,1024]{1,0:T(4,128)S(1)}, s32[4,1024]{1,0:T(4,128)}, u32[]{:S(2)}) copy-start(s32[4,1024]{1,0:T(4,128)} %param.9) | copy-start | bytes 49156
  2.2 3.4 %copy-start.4 = (s32[64]{0:T(128)S(1)}, s32[64]{0:T(128)}, u32[]{:S(2)}) copy-start(s32[64]{0:T(128)} %param.7) | copy-start | bytes 772
  6.4 84.2 %copy-start.3 = (s32[512]{0:T(512)S(1)}, s32[512]{0:T(512)}, u32[]{:S(2)}) copy-start(s32[512]{0:T(512)} %param.10) | copy-start | bytes 6148
  90.5 1.8 %copy-start.1 = (bf16[32,64,128]{2,1,0:T(8,128)(2,1)S(1)}, bf16[32,64,128]{2,1,0:T(8,128)(2,1)}, u32[]{:S(2)}) copy-start(bf16[32,64,128]{2,1,0:T(8,128)(2,1)} %get-tuple-element.18) | copy-start | bytes 1572868

commit v9 on v7

--- a/solution.py
+++ b/solution.py
@@ -1,6 +1,8 @@
 import math
 
 import jax
+import ml_dtypes
+import numpy as np
 import jax.numpy as jnp
 from jax import lax
 from jax.experimental import pallas as pl
@@ -13,6 +15,15 @@
 
 ROW = ("x", "zl")
 COL = ("y", "zh", "c")
+
+
+def phase_tables_np(samples):
+    freq_bins = (2 * np.arange(NF, dtype=np.int32) + 1) * (NFFT // (4 * NF))
+    sample_ticks = np.arange(samples, dtype=np.int32)
+    phase_turns = freq_bins[:, None] * sample_ticks[None, :] % NFFT
+    phase_angle = phase_turns.astype(np.float32) * np.float32(2.0 * math.pi / NFFT)
+    angle = phase_angle.astype(np.float64)
+    return (np.cos(angle).astype(np.float32), np.sin(angle).astype(np.float32))
 
 
 def phase_tables(samples):
@@ -260,7 +271,20 @@
 
     band = partial_ref.shape[1]
 
-    def band_body(j, carry):
+    def band_peer(i):
+        hh = lax.rem(1 - h + i // 8, 2)
+        yy = lax.rem(i, 8) // 2
+        cc = lax.rem(i, 2)
+        return (yy * 2 + hh) * 2 + cc, {"y": yy, "zh": hh, "c": cc}
+
+    def reduce_copy(j, peer):
+        return pltpu.make_async_remote_copy(
+            partial_ref.at[j], slots_ref.at[me_col], send_red.at[j], recv_red.at[me_col],
+            device_id=peer, device_id_type=MESH_ID,
+        )
+
+    def band_body(i, carry):
+        j, peer = band_peer(i)
         rows = []
         for u in range(band):
             stacked = jnp.dot(
@@ -268,18 +292,11 @@
             )
             rows.append(jnp.sum(stacked * weights_ref[...], axis=0, keepdims=True))
         partial_ref[j] = jnp.concatenate(rows, axis=0)
+        pl.when(j != me_col)(reduce_copy(j, peer).start)
         return carry
 
     lax.fori_loop(0, partial_ref.shape[0], band_body, 0)
 
-    reduce_sends = []
-    for j, peer in col_peers:
-        desc = pltpu.make_async_remote_copy(
-            partial_ref.at[j], slots_ref.at[me_col], send_red.at[j], recv_red.at[me_col],
-            device_id=peer, device_id_type=MESH_ID,
-        )
-        pl.when(j != me_col)(desc.start)
-        reduce_sends.append((j, desc))
     slots_ref[me_col] = partial_ref[me_col]
     for j, peer in col_peers:
         recv = pltpu.make_async_remote_copy(
@@ -294,8 +311,8 @@
 
     for desc, cond in started:
         when(cond, desc.wait_send)
-    for j, desc in reduce_sends:
-        pl.when(j != me_col)(desc.wait_send)
+    for j, peer in col_peers:
+        pl.when(j != me_col)(reduce_copy(j, peer).wait_send)
 
 
 def fused_call(spec, traces, aperture, weights, inverse, row_count, col_count):
@@ -336,8 +353,12 @@
     surface_count = recv_count * col_count
     image_panel_width = band_index.shape[0]
     depth_slab_samples = samples // col_count
-    cosine, sine_table = phase_tables(samples)
-    forward = (jnp.concatenate([cosine, -sine_table], 0) / math.sqrt(samples)).astype(jnp.bfloat16)
+    cosine, sine_table = phase_tables_np(samples)
+    forward = jnp.asarray(
+        (np.concatenate([cosine, -sine_table], 0) / np.float32(math.sqrt(samples))).astype(
+            ml_dtypes.bfloat16
+        )
+    )
     spectra = jnp.dot(
         forward,
         traces.reshape(samples, shot_count * recv_count),
@@ -354,7 +375,7 @@
     aperture = aperture_rows(
         aperture_list, my_receivers, columns, col_pos * recv_count, recv_count, spread_len
     )
-    inverse = jnp.concatenate([cosine, -sine_table], 0).T / math.sqrt(NF)
+    inverse = jnp.asarray(np.concatenate([cosine, -sine_table], 0).T / np.float32(math.sqrt(NF)))
     primaries, stacked = fused_call(
         spectra.reshape(2 * NF, shot_count, recv_count),
         traces,

time: 91.5 us -> 89.1 us (0.974)
  Pallas kernels: 81.7 us -> 80 us
    pallas_call x1, Pallas kernels: 81.7 us -> 80 us  [fused_call(): pl.pallas_call(fused_kernel, out_shape=(jax.ShapeDtypeStruct(traces.shape...]
where the time goes in v9:
time: 89.1 us; the launch traced here: 88.8 us
  Pallas kernels  80 us (90%)
  local copies, waits for them, and re-layouts  3.42 us (4%)
  other arithmetic  3.09 us (3%)
  matrix products  1.67 us (2%)
    pallas_call x1, Pallas kernels, fused_call(): pl.pallas_call(fused_kernel, out_shape=(jax.ShapeDtypeStruct(traces.shape...  80 us
    unnamed x13, local copies, waits for them, and re-layouts  2.34 us

profile of v9, /device:TPU:1, one launch (start us, length us, event | category | flops | bytes accessed | tf_op | source)
XLA Modules:
  0.0 88.8 jit_solution(5264494501552973658)
XLA Ops:
  0.6 0.0 copy-start
  0.6 0.0 copy-start.2
  0.7 1.5 %fusion = bf16[1,8,64,128]{3,1,2,0:T(8,128)(2,1)S(1)} fusion(bf16[8,32]{1,0:T(8,128)(2,1)} %constant.53.clone, bf16[4,8,64,128]{3,2,1,0:T(8,128)(2,1)} %bitcast.22), kind=kOutput, calls=%fused_computation.3 | convolution fusion | flops 4259840 | bytes 655872 | tf_op jit(solution)/shard_map/dot_general | solution.py:362
  2.1 0.0 copy-start.4
  2.1 0.7 copy.26
  2.8 0.0 copy-done.2
  2.8 0.8 convert_reduce_fusion
  3.6 0.1 copy.12
  3.7 0.2 broadcast_in_dim.15
  3.9 0.8 dynamic_slice.3
  4.7 0.8 fusion.4.aperture_ref
  5.5 0.0 copy-done.4
  5.5 0.0 copy-start.3
  5.5 0.7 add_divide_fusion.weights_ref
  6.2 80.0 %shard_map.95 = (bf16[32,64,128]{2,1,0:T(8,128)(2,1)}, f32[2,512]{1,0:T(2,128)}) custom-call(bf16[8,64,128]{2,1,0:T(8,128)(2,1)} %bitcast.24, bf16[32,64,128]{2,1,0:T(8,128)(2,1)} %traces_ref.1, bf16[128,512]{1,0:T(8,128)(2,1)} %fusion.4.aperture_ref, f32[64,512]{1,0:T(8,128)} %add_divide_fusion.weights_ref, f32[32,8]{1,0:T(8,128)} %constant.54.clone.inverse_ref), custom_call_target="tpu_custom_call" | custom-call | tf_op jit(solution)/shard_map/pallas_call | solution.py:324
  86.2 0.0 copy-start.1
  86.2 0.0 copy-done.3
  86.2 0.7 multiply_convert_fusion
  87.0 0.0 copy-done
  87.0 0.2 convolution_bitcast_fusion
  87.2 0.8 copy.14
  88.0 0.0 copy-done.1
  88.0 0.8 copy.28
  (3 shorter events, 0.0 us)
Async XLA Ops:
  0.6 86.4 %copy-start = (bf16[32,2,128]{2,1,0:T(2,128)(2,1)S(1)}, bf16[32,2,128]{2,1,0:T(2,128)(2,1)}, u32[]{:S(2)}) copy-start(bf16[32,2,128]{2,1,0:T(2,128)(2,1)} %param.13) | copy-start | bytes 49156
  0.6 2.2 %copy-start.2 = (s32[4,1024]{1,0:T(4,128)S(1)}, s32[4,1024]{1,0:T(4,128)}, u32[]{:S(2)}) copy-start(s32[4,1024]{1,0:T(4,128)} %param.11) | copy-start | bytes 49156
  2.1 3.4 %copy-start.4 = (s32[64]{0:T(128)S(1)}, s32[64]{0:T(128)}, u32[]{:S(2)}) copy-start(s32[64]{0:T(128)} %param.9) | copy-start | bytes 772
  5.5 80.7 %copy-start.3 = (s32[512]{0:T(512)S(1)}, s32[512]{0:T(512)}, u32[]{:S(2)}) copy-start(s32[512]{0:T(512)} %param.12) | copy-start | bytes 6148
  86.2 1.8 %copy-start.1 = (bf16[32,64,128]{2,1,0:T(8,128)(2,1)S(1)}, bf16[32,64,128]{2,1,0:T(8,128)(2,1)}, u32[]{:S(2)}) copy-start(bf16[32,64,128]{2,1,0:T(8,128)(2,1)} %get-tuple-element.12) | copy-start | bytes 1572868

commit v10 on v9

--- a/solution.py
+++ b/solution.py
@@ -85,9 +85,9 @@
 NX, NZ, NY = 4, 8, 4
 
 
-def fused_kernel(spec_ref, traces_ref, aperture_ref, weights_ref, inverse_ref,
+def fused_kernel(spec_ref, traces_ref, lists_ref, rpos_ref, spos_ref, inverse_ref,
                  prim_ref, stack_ref,
-                 colw_ref, roww_ref, mult_ref, partial_ref, slots_ref,
+                 colw_ref, roww_ref, mult_ref, partial_ref, slots_ref, aperture_ref, weights_ref,
                  recv_row, recv_col, send_row, send_col, recv_red, send_red):
     x = lax.axis_index("x")
     z = lax.axis_index("zl")
@@ -235,6 +235,34 @@
                 col_relay((yp * 2 + 1) * 2 + cc, ((3, {"y": ym}),))
     for dist in range(NZ - lag, NZ):
         x_forward_at(dist)
+
+    recvs_n = aperture_ref.shape[0]
+    width = aperture_ref.shape[1]
+    tiles, listed = lists_ref.shape
+    tile_width = width // tiles
+    spread_len = width * NX * NZ // 4
+    first = me_col * recvs_n
+
+    def as_column(row):
+        n = row.shape[1]
+        eye = lax.broadcasted_iota(jnp.int32, (n, n), 0) == lax.broadcasted_iota(jnp.int32, (n, n), 1)
+        return jnp.sum(jnp.where(eye, row.astype(jnp.float32), 0.0), axis=1, keepdims=True)
+
+    cols = (me_row * width + lax.broadcasted_iota(jnp.int32, (1, width), 1)).astype(jnp.float32)
+    rpos = as_column(rpos_ref[:, pl.ds(pl.multiple_of(first, recvs_n), recvs_n)])
+    offset = (rpos - cols) / spread_len
+    taper = 1.0 / (1.0 + offset * offset)
+    rows_here = first + lax.broadcasted_iota(jnp.int32, (recvs_n, listed), 0)
+    for t in range(tiles):
+        hits = (lists_ref[pl.ds(t, 1), :] == rows_here).astype(jnp.float32)
+        member = jnp.sum(hits, axis=1, keepdims=True)
+        part = taper[:, t * tile_width:(t + 1) * tile_width]
+        aperture_ref[:, t * tile_width:(t + 1) * tile_width] = (
+            member * part * (2.0 / math.sqrt(listed))
+        ).astype(aperture_ref.dtype)
+    spos = as_column(spos_ref[...])
+    soffset = (spos - cols) / spread_len
+    weights_ref[...] = 1.0 / (1.0 + soffset * soffset)
 
     x2 = lax.rem(x + 2, NX)
     for zz in range(NZ):
@@ -315,11 +343,10 @@
         pl.when(j != me_col)(reduce_copy(j, peer).wait_send)
 
 
-def fused_call(spec, traces, aperture, weights, inverse, row_count, col_count):
+def fused_call(spec, traces, lists, rpos, spos, inverse, width, row_count, col_count):
     planes, shots, recvs = spec.shape
     samples = traces.shape[0]
     band = samples // col_count
-    width = aperture.shape[1]
     vmem = pl.BlockSpec(memory_space=pltpu.VMEM)
     return pl.pallas_call(
         fused_kernel,
@@ -327,7 +354,7 @@
             jax.ShapeDtypeStruct(traces.shape, jnp.bfloat16),
             jax.ShapeDtypeStruct((band, width), jnp.float32),
         ),
-        in_specs=[vmem, vmem, vmem, vmem, pl.BlockSpec(memory_space=pltpu.SMEM)],
+        in_specs=[vmem, vmem, vmem, vmem, vmem, pl.BlockSpec(memory_space=pltpu.SMEM)],
         out_specs=(vmem, vmem),
         scratch_shapes=[
             pltpu.VMEM((planes, row_count * shots, recvs), spec.dtype),
@@ -335,6 +362,8 @@
             pltpu.VMEM((planes, shots, recvs), jnp.float32),
             pltpu.VMEM((col_count, band, width), jnp.float32),
             pltpu.VMEM((col_count, band, width), jnp.float32),
+            pltpu.VMEM((recvs, width), jnp.bfloat16),
+            pltpu.VMEM((shots, width), jnp.float32),
             pltpu.SemaphoreType.DMA((row_count, 2)),
             pltpu.SemaphoreType.DMA((col_count, 2)),
             pltpu.SemaphoreType.DMA((row_count, 2, 4)),
@@ -343,7 +372,7 @@
             pltpu.SemaphoreType.DMA((col_count,)),
         ],
         compiler_params=pltpu.CompilerParams(collective_id=0, has_side_effects=True),
-    )(spec, traces, aperture, weights, inverse)
+    )(spec, traces, lists, rpos, spos, inverse)
 
 
 def per_device(traces, source_pos, receiver_pos, aperture_list, band_index, weight_tiles):
@@ -359,29 +388,19 @@
             ml_dtypes.bfloat16
         )
     )
-    spectra = jnp.dot(
-        forward,
-        traces.reshape(samples, shot_count * recv_count),
-        preferred_element_type=jnp.float32,
-    )
-    spectra = spectra.astype(jnp.bfloat16)
-
-    col_pos = axis_pos(COL)
-    row_pos = axis_pos(ROW)
-    columns = row_pos * image_panel_width + jnp.arange(image_panel_width, dtype=jnp.int32)
-    spread_len = image_panel_width * row_count // 4
-    stacking_weights = shot_weights(source_pos, columns, spread_len)
-    my_receivers = lax.dynamic_slice_in_dim(receiver_pos, col_pos * recv_count, recv_count, 0)
-    aperture = aperture_rows(
-        aperture_list, my_receivers, columns, col_pos * recv_count, recv_count, spread_len
-    )
+    spectra = jnp.einsum(
+        "pt,tsr->psr", forward, traces, preferred_element_type=jnp.float32
+    ).astype(jnp.bfloat16)
+
     inverse = jnp.asarray(np.concatenate([cosine, -sine_table], 0).T / np.float32(math.sqrt(NF)))
     primaries, stacked = fused_call(
-        spectra.reshape(2 * NF, shot_count, recv_count),
+        spectra,
         traces,
-        aperture,
-        stacking_weights,
+        aperture_list,
+        receiver_pos.reshape(1, -1),
+        source_pos.reshape(1, -1),
         inverse,
+        image_panel_width,
         row_count,
         col_count,
     )

time: 89.1 us -> 85.6 us (0.961)
  other arithmetic: 3.09 us -> 0.76 us
  local copies, waits for them, and re-layouts: 3.42 us -> 2.33 us
    unnamed x13 -> x8, local copies, waits for them, and re-layouts: 2.34 us -> 1.65 us
where the time goes in v10:
time: 85.6 us; the launch traced here: 85.5 us
  Pallas kernels  80 us (93%)
  local copies, waits for them, and re-layouts  2.33 us (3%)
  matrix products  1.66 us (2%)
    pallas_call x1, Pallas kernels, fused_call(): pl.pallas_call(fused_kernel, out_shape=(jax.ShapeDtypeStruct(traces.shape...  80 us

profile of v10, /device:TPU:1, one launch (start us, length us, event | category | flops | bytes accessed | tf_op | source)
XLA Modules:
  0.0 85.5 jit_solution(8439910804046708747)
XLA Ops:
  0.6 0.0 copy-start
  0.6 1.4 %fusion = bf16[8,64,128]{2,0,1:T(8,128)(2,1)S(1)} fusion(bf16[8,32,1]{1,0,2:T(8,128)(2,1)} %constant.12, bf16[32,64,128]{2,1,0:T(8,128)(2,1)} %traces_ref.1), kind=kOutput, calls=%fused_computation.1 | convolution fusion | flops 4194304 | bytes 655872 | tf_op jit(solution)/shard_map/pt,tsr->psr/dot_general | solution.py:391
  2.1 0.7 copy.19.spec_ref
  2.8 0.0 copy-start.2
  2.8 80.0 %shard_map.95 = (bf16[32,64,128]{2,1,0:T(8,128)(2,1)}, f32[2,512]{1,0:T(2,128)}) custom-call(bf16[8,64,128]{2,1,0:T(8,128)(2,1)} %copy.19.spec_ref, bf16[32,64,128]{2,1,0:T(8,128)(2,1)} %traces_ref.1, s32[4,1024]{1,0:T(4,128)} %lists_ref.1, s32[1,2048]{1,0:T(1,128)} %bitcast.8, s32[1,64]{1,0:T(1,128)} %bitcast.9, f32[32,8]{1,0:T(8,128)} %constant.10.clone.inverse_ref), custom_call_target="tpu_custom_call" | custom-call | tf_op jit(solution)/shard_map/pallas_call | solution.py:351
  82.8 0.0 copy-start.1
  82.8 0.0 copy-done.2
  82.9 0.7 multiply_convert_fusion
  83.6 0.0 copy-done
  83.6 0.2 convolution_bitcast_fusion
  83.8 0.8 copy.13
  84.7 0.0 copy-done.1
  84.7 0.8 copy.21
  (1 shorter events, 0.0 us)
Async XLA Ops:
  0.6 83.0 %copy-start = (bf16[32,2,128]{2,1,0:T(2,128)(2,1)S(1)}, bf16[32,2,128]{2,1,0:T(2,128)(2,1)}, u32[]{:S(2)}) copy-start(bf16[32,2,128]{2,1,0:T(2,128)(2,1)} %param.13) | copy-start | bytes 49156
  2.8 80.1 %copy-start.2 = (s32[512]{0:T(512)S(1)}, s32[512]{0:T(512)}, u32[]{:S(2)}) copy-start(s32[512]{0:T(512)} %param.12) | copy-start | bytes 6148
  82.8 1.8 %copy-start.1 = (bf16[32,64,128]{2,1,0:T(8,128)(2,1)S(1)}, bf16[32,64,128]{2,1,0:T(8,128)(2,1)}, u32[]{:S(2)}) copy-start(bf16[32,64,128]{2,1,0:T(8,128)(2,1)} %get-tuple-element.10) | copy-start | bytes 1572868

commit v11 on v10

--- a/solution.py
+++ b/solution.py
@@ -222,17 +222,16 @@
         row_relay(x * NZ + z + k, ((1, {"zl": z - 1}, z > 0),) + x_sends, z + k < NZ)
         if k - lag >= 0:
             x_forward_at(k - lag)
-        if k == 2:
+        if k == 4:
             for part in parts:
                 start(col_copy(me_col, part, 1, {"zh": 1 - h}, own=True))
-        if k == 4:
+        if k == 6:
             col_relay(j_h, ((0, {"c": 1 - c}),) + y_sends)
-        if k == 5:
+        if k == 7:
             col_relay(j_hc, y_sends)
-        if k == 6:
-            for cc in range(2):
-                col_relay((ym * 2 + 0) * 2 + cc, ((2, {"y": yp}),))
-                col_relay((yp * 2 + 1) * 2 + cc, ((3, {"y": ym}),))
+    for cc in range(2):
+        col_relay((ym * 2 + 0) * 2 + cc, ((2, {"y": yp}),))
+        col_relay((yp * 2 + 1) * 2 + cc, ((3, {"y": ym}),))
     for dist in range(NZ - lag, NZ):
         x_forward_at(dist)
 

time: 85.6 us -> 88.4 us (1.033)
  Pallas kernels: 80 us -> 82.8 us
    pallas_call x1, Pallas kernels: 80 us -> 82.8 us  [fused_call(): pl.pallas_call(fused_kernel, out_shape=(jax.ShapeDtypeStruct(traces.shape...]
where the time goes in v11:
time: 88.4 us; the launch traced here: 88.2 us
  Pallas kernels  82.8 us (94%)
  local copies, waits for them, and re-layouts  2.33 us (3%)
  matrix products  1.66 us (2%)
    pallas_call x1, Pallas kernels, fused_call(): pl.pallas_call(fused_kernel, out_shape=(jax.ShapeDtypeStruct(traces.shape...  82.8 us

profile of v11, /device:TPU:1, one launch (start us, length us, event | category | flops | bytes accessed | tf_op | source)
XLA Modules:
  0.0 88.2 jit_solution(11398115077693086792)
XLA Ops:
  0.6 0.0 copy-start
  0.6 1.4 %fusion = bf16[8,64,128]{2,0,1:T(8,128)(2,1)S(1)} fusion(bf16[8,32,1]{1,0,2:T(8,128)(2,1)} %constant.12, bf16[32,64,128]{2,1,0:T(8,128)(2,1)} %traces_ref.1), kind=kOutput, calls=%fused_computation.1 | convolution fusion | flops 4194304 | bytes 655872 | tf_op jit(solution)/shard_map/pt,tsr->psr/dot_general | solution.py:390
  2.1 0.7 copy.19.spec_ref
  2.8 0.0 copy-start.2
  2.8 82.8 %shard_map.95 = (bf16[32,64,128]{2,1,0:T(8,128)(2,1)}, f32[2,512]{1,0:T(2,128)}) custom-call(bf16[8,64,128]{2,1,0:T(8,128)(2,1)} %copy.19.spec_ref, bf16[32,64,128]{2,1,0:T(8,128)(2,1)} %traces_ref.1, s32[4,1024]{1,0:T(4,128)} %lists_ref.1, s32[1,2048]{1,0:T(1,128)} %bitcast.8, s32[1,64]{1,0:T(1,128)} %bitcast.9, f32[32,8]{1,0:T(8,128)} %constant.10.clone.inverse_ref), custom_call_target="tpu_custom_call" | custom-call | tf_op jit(solution)/shard_map/pallas_call | solution.py:350
  85.5 0.0 copy-start.1
  85.6 0.0 copy-done.2
  85.6 0.7 multiply_convert_fusion
  86.3 0.0 copy-done
  86.3 0.2 convolution_bitcast_fusion
  86.6 0.8 copy.13
  87.4 0.0 copy-done.1
  87.4 0.8 copy.21
  (1 shorter events, 0.0 us)
Async XLA Ops:
  0.6 85.7 %copy-start = (bf16[32,2,128]{2,1,0:T(2,128)(2,1)S(1)}, bf16[32,2,128]{2,1,0:T(2,128)(2,1)}, u32[]{:S(2)}) copy-start(bf16[32,2,128]{2,1,0:T(2,128)(2,1)} %param.13) | copy-start | bytes 49156
  2.8 82.8 %copy-start.2 = (s32[512]{0:T(512)S(1)}, s32[512]{0:T(512)}, u32[]{:S(2)}) copy-start(s32[512]{0:T(512)} %param.12) | copy-start | bytes 6148
  85.5 1.8 %copy-start.1 = (bf16[32,64,128]{2,1,0:T(8,128)(2,1)S(1)}, bf16[32,64,128]{2,1,0:T(8,128)(2,1)}, u32[]{:S(2)}) copy-start(bf16[32,64,128]{2,1,0:T(8,128)(2,1)} %get-tuple-element.10) | copy-start | bytes 1572868

commit v12 on v10

--- a/solution.py
+++ b/solution.py
@@ -172,8 +172,8 @@
         else:
             pl.when(cond)(fn)
 
-    def row_relay(b, sends, cond=None):
-        for part in parts:
+    def row_relay(b, sends, cond=None, only=parts):
+        for part in only:
             when(cond, row_copy(b, part, 0, {"x": x}).wait_recv)
             for d, peer, extra in sends:
                 c2 = cond if extra is None else (extra if cond is None else jnp.logical_and(cond, extra))
@@ -218,8 +218,9 @@
     lag = 2
     x_sends = ((2, {"x": xp}, None), (3, {"x": xm}, None))
     for k in range(1, NZ):
-        row_relay(x * NZ + z - k, ((0, {"zl": z + 1}, z < NZ - 1),) + x_sends, z >= k)
-        row_relay(x * NZ + z + k, ((1, {"zl": z - 1}, z > 0),) + x_sends, z + k < NZ)
+        for part in parts:
+            row_relay(x * NZ + z - k, ((0, {"zl": z + 1}, z < NZ - 1),) + x_sends, z >= k, (part,))
+            row_relay(x * NZ + z + k, ((1, {"zl": z - 1}, z > 0),) + x_sends, z + k < NZ, (part,))
         if k - lag >= 0:
             x_forward_at(k - lag)
         if k == 2:

time: 85.6 us -> 84.7 us (0.989)
  Pallas kernels: 80 us -> 79.1 us
    pallas_call x1, Pallas kernels: 80 us -> 79.1 us  [fused_call(): pl.pallas_call(fused_kernel, out_shape=(jax.ShapeDtypeStruct(traces.shape...]
where the time goes in v12:
time: 84.7 us; the launch traced here: 84.5 us
  Pallas kernels  79.1 us (93%)
  local copies, waits for them, and re-layouts  2.33 us (3%)
  matrix products  1.66 us (2%)
    pallas_call x1, Pallas kernels, fused_call(): pl.pallas_call(fused_kernel, out_shape=(jax.ShapeDtypeStruct(traces.shape...  79.1 us

profile of v12, /device:TPU:1, one launch (start us, length us, event | category | flops | bytes accessed | tf_op | source)
XLA Modules:
  0.0 84.5 jit_solution(17582106181743136461)
XLA Ops:
  0.6 0.0 copy-start
  0.6 1.4 %fusion = bf16[8,64,128]{2,0,1:T(8,128)(2,1)S(1)} fusion(bf16[8,32,1]{1,0,2:T(8,128)(2,1)} %constant.12, bf16[32,64,128]{2,1,0:T(8,128)(2,1)} %traces_ref.1), kind=kOutput, calls=%fused_computation.1 | convolution fusion | flops 4194304 | bytes 655872 | tf_op jit(solution)/shard_map/pt,tsr->psr/dot_general | solution.py:392
  2.1 0.7 copy.19.spec_ref
  2.8 0.0 copy-start.2
  2.8 79.1 %shard_map.95 = (bf16[32,64,128]{2,1,0:T(8,128)(2,1)}, f32[2,512]{1,0:T(2,128)}) custom-call(bf16[8,64,128]{2,1,0:T(8,128)(2,1)} %copy.19.spec_ref, bf16[32,64,128]{2,1,0:T(8,128)(2,1)} %traces_ref.1, s32[4,1024]{1,0:T(4,128)} %lists_ref.1, s32[1,2048]{1,0:T(1,128)} %bitcast.8, s32[1,64]{1,0:T(1,128)} %bitcast.9, f32[32,8]{1,0:T(8,128)} %constant.10.clone.inverse_ref), custom_call_target="tpu_custom_call" | custom-call | tf_op jit(solution)/shard_map/pallas_call | solution.py:352
  81.9 0.0 copy-start.1
  81.9 0.0 copy-done.2
  81.9 0.7 multiply_convert_fusion
  82.7 0.0 copy-done
  82.7 0.2 convolution_bitcast_fusion
  82.9 0.8 copy.13
  83.7 0.0 copy-done.1
  83.7 0.8 copy.21
  (1 shorter events, 0.0 us)
Async XLA Ops:
  0.6 82.0 %copy-start = (bf16[32,2,128]{2,1,0:T(2,128)(2,1)S(1)}, bf16[32,2,128]{2,1,0:T(2,128)(2,1)}, u32[]{:S(2)}) copy-start(bf16[32,2,128]{2,1,0:T(2,128)(2,1)} %param.13) | copy-start | bytes 49156
  2.8 79.1 %copy-start.2 = (s32[512]{0:T(512)S(1)}, s32[512]{0:T(512)}, u32[]{:S(2)}) copy-start(s32[512]{0:T(512)} %param.12) | copy-start | bytes 6148
  81.9 1.8 %copy-start.1 = (bf16[32,64,128]{2,1,0:T(8,128)(2,1)S(1)}, bf16[32,64,128]{2,1,0:T(8,128)(2,1)}, u32[]{:S(2)}) copy-start(bf16[32,64,128]{2,1,0:T(8,128)(2,1)} %get-tuple-element.10) | copy-start | bytes 1572868

commit v13 on v12

--- a/solution.py
+++ b/solution.py
@@ -215,12 +215,26 @@
             x_forward(z - dist, z >= dist)
             x_forward(z + dist, z + dist < NZ)
 
-    lag = 2
+    lag = 3
     x_sends = ((2, {"x": xp}, None), (3, {"x": xm}, None))
+
+    def send_across(items):
+        for b, part, cond in items:
+            for d, peer, _ in x_sends:
+                start(row_copy(b, part, d, peer), cond)
+
+    pending = []
     for k in range(1, NZ):
+        arrived = []
         for part in parts:
-            row_relay(x * NZ + z - k, ((0, {"zl": z + 1}, z < NZ - 1),) + x_sends, z >= k, (part,))
-            row_relay(x * NZ + z + k, ((1, {"zl": z - 1}, z > 0),) + x_sends, z + k < NZ, (part,))
+            b_lo = x * NZ + z - k
+            row_relay(b_lo, ((0, {"zl": z + 1}, z < NZ - 1),), z >= k, (part,))
+            arrived.append((b_lo, part, z >= k))
+            b_hi = x * NZ + z + k
+            row_relay(b_hi, ((1, {"zl": z - 1}, z > 0),), z + k < NZ, (part,))
+            arrived.append((b_hi, part, z + k < NZ))
+        send_across(pending)
+        pending = arrived
         if k - lag >= 0:
             x_forward_at(k - lag)
         if k == 2:
@@ -234,6 +248,7 @@
             for cc in range(2):
                 col_relay((ym * 2 + 0) * 2 + cc, ((2, {"y": yp}),))
                 col_relay((yp * 2 + 1) * 2 + cc, ((3, {"y": ym}),))
+    send_across(pending)
     for dist in range(NZ - lag, NZ):
         x_forward_at(dist)
 

time: 84.7 us -> 90.7 us (1.071)
  Pallas kernels: 79.1 us -> 85 us
    pallas_call x1, Pallas kernels: 79.1 us -> 85 us  [fused_call(): pl.pallas_call(fused_kernel, out_shape=(jax.ShapeDtypeStruct(traces.shape...]
where the time goes in v13:
time: 90.7 us; the launch traced here: 90.5 us
  Pallas kernels  85 us (94%)
  local copies, waits for them, and re-layouts  2.33 us (3%)
  matrix products  1.66 us (2%)
    pallas_call x1, Pallas kernels, fused_call(): pl.pallas_call(fused_kernel, out_shape=(jax.ShapeDtypeStruct(traces.shape...  85 us

profile of v13, /device:TPU:1, one launch (start us, length us, event | category | flops | bytes accessed | tf_op | source)
XLA Modules:
  0.0 90.5 jit_solution(18046949789833480999)
XLA Ops:
  0.6 0.0 copy-start
  0.6 1.4 %fusion = bf16[8,64,128]{2,0,1:T(8,128)(2,1)S(1)} fusion(bf16[8,32,1]{1,0,2:T(8,128)(2,1)} %constant.12, bf16[32,64,128]{2,1,0:T(8,128)(2,1)} %traces_ref.1), kind=kOutput, calls=%fused_computation.1 | convolution fusion | flops 4194304 | bytes 655872 | tf_op jit(solution)/shard_map/pt,tsr->psr/dot_general | solution.py:407
  2.1 0.7 copy.19.spec_ref
  2.8 0.0 copy-start.2
  2.8 85.0 %shard_map.95 = (bf16[32,64,128]{2,1,0:T(8,128)(2,1)}, f32[2,512]{1,0:T(2,128)}) custom-call(bf16[8,64,128]{2,1,0:T(8,128)(2,1)} %copy.19.spec_ref, bf16[32,64,128]{2,1,0:T(8,128)(2,1)} %traces_ref.1, s32[4,1024]{1,0:T(4,128)} %lists_ref.1, s32[1,2048]{1,0:T(1,128)} %bitcast.8, s32[1,64]{1,0:T(1,128)} %bitcast.9, f32[32,8]{1,0:T(8,128)} %constant.10.clone.inverse_ref), custom_call_target="tpu_custom_call" | custom-call | tf_op jit(solution)/shard_map/pallas_call | solution.py:367
  87.8 0.0 copy-start.1
  87.8 0.0 copy-done.2
  87.9 0.7 multiply_convert_fusion
  88.6 0.0 copy-done
  88.6 0.2 convolution_bitcast_fusion
  88.8 0.8 copy.13
  89.7 0.0 copy-done.1
  89.7 0.8 copy.21
  (1 shorter events, 0.0 us)
Async XLA Ops:
  0.6 88.0 %copy-start = (bf16[32,2,128]{2,1,0:T(2,128)(2,1)S(1)}, bf16[32,2,128]{2,1,0:T(2,128)(2,1)}, u32[]{:S(2)}) copy-start(bf16[32,2,128]{2,1,0:T(2,128)(2,1)} %param.13) | copy-start | bytes 49156
  2.8 85.1 %copy-start.2 = (s32[512]{0:T(512)S(1)}, s32[512]{0:T(512)}, u32[]{:S(2)}) copy-start(s32[512]{0:T(512)} %param.12) | copy-start | bytes 6148
  87.8 1.8 %copy-start.1 = (bf16[32,64,128]{2,1,0:T(8,128)(2,1)S(1)}, bf16[32,64,128]{2,1,0:T(8,128)(2,1)}, u32[]{:S(2)}) copy-start(bf16[32,64,128]{2,1,0:T(8,128)(2,1)} %get-tuple-element.10) | copy-start | bytes 1572868

commit v14 on v12

--- a/solution.py
+++ b/solution.py
@@ -219,8 +219,8 @@
     x_sends = ((2, {"x": xp}, None), (3, {"x": xm}, None))
     for k in range(1, NZ):
         for part in parts:
-            row_relay(x * NZ + z - k, ((0, {"zl": z + 1}, z < NZ - 1),) + x_sends, z >= k, (part,))
-            row_relay(x * NZ + z + k, ((1, {"zl": z - 1}, z > 0),) + x_sends, z + k < NZ, (part,))
+            row_relay(x * NZ + z - k, x_sends + ((0, {"zl": z + 1}, z < NZ - 1),), z >= k, (part,))
+            row_relay(x * NZ + z + k, x_sends + ((1, {"zl": z - 1}, z > 0),), z + k < NZ, (part,))
         if k - lag >= 0:
             x_forward_at(k - lag)
         if k == 2:

time: 84.7 us -> 84.7 us (level)
  no operation moved by 1% of the time
where the time goes in v14:
time: 84.7 us; the launch traced here: 84.5 us
  Pallas kernels  79.1 us (93%)
  local copies, waits for them, and re-layouts  2.33 us (3%)
  matrix products  1.66 us (2%)
    pallas_call x1, Pallas kernels, fused_call(): pl.pallas_call(fused_kernel, out_shape=(jax.ShapeDtypeStruct(traces.shape...  79.1 us

profile of v14, /device:TPU:1, one launch (start us, length us, event | category | flops | bytes accessed | tf_op | source)
XLA Modules:
  0.0 84.5 jit_solution(16509449098424004784)
XLA Ops:
  0.6 0.0 copy-start
  0.6 1.4 %fusion = bf16[8,64,128]{2,0,1:T(8,128)(2,1)S(1)} fusion(bf16[8,32,1]{1,0,2:T(8,128)(2,1)} %constant.12, bf16[32,64,128]{2,1,0:T(8,128)(2,1)} %traces_ref.1), kind=kOutput, calls=%fused_computation.1 | convolution fusion | flops 4194304 | bytes 655872 | tf_op jit(solution)/shard_map/pt,tsr->psr/dot_general | solution.py:392
  2.1 0.7 copy.19.spec_ref
  2.8 0.0 copy-start.2
  2.8 79.1 %shard_map.95 = (bf16[32,64,128]{2,1,0:T(8,128)(2,1)}, f32[2,512]{1,0:T(2,128)}) custom-call(bf16[8,64,128]{2,1,0:T(8,128)(2,1)} %copy.19.spec_ref, bf16[32,64,128]{2,1,0:T(8,128)(2,1)} %traces_ref.1, s32[4,1024]{1,0:T(4,128)} %lists_ref.1, s32[1,2048]{1,0:T(1,128)} %bitcast.8, s32[1,64]{1,0:T(1,128)} %bitcast.9, f32[32,8]{1,0:T(8,128)} %constant.10.clone.inverse_ref), custom_call_target="tpu_custom_call" | custom-call | tf_op jit(solution)/shard_map/pallas_call | solution.py:352
  81.9 0.0 copy-start.1
  81.9 0.0 copy-done.2
  81.9 0.7 multiply_convert_fusion
  82.7 0.0 copy-done
  82.7 0.2 convolution_bitcast_fusion
  82.9 0.8 copy.13
  83.7 0.0 copy-done.1
  83.7 0.8 copy.21
  (1 shorter events, 0.0 us)
Async XLA Ops:
  0.6 82.0 %copy-start = (bf16[32,2,128]{2,1,0:T(2,128)(2,1)S(1)}, bf16[32,2,128]{2,1,0:T(2,128)(2,1)}, u32[]{:S(2)}) copy-start(bf16[32,2,128]{2,1,0:T(2,128)(2,1)} %param.13) | copy-start | bytes 49156
  2.8 79.1 %copy-start.2 = (s32[512]{0:T(512)S(1)}, s32[512]{0:T(512)}, u32[]{:S(2)}) copy-start(s32[512]{0:T(512)} %param.12) | copy-start | bytes 6148
  81.9 1.8 %copy-start.1 = (bf16[32,64,128]{2,1,0:T(8,128)(2,1)S(1)}, bf16[32,64,128]{2,1,0:T(8,128)(2,1)}, u32[]{:S(2)}) copy-start(bf16[32,64,128]{2,1,0:T(8,128)(2,1)} %get-tuple-element.10) | copy-start | bytes 1572868

commit v15 on v14

--- a/solution.py
+++ b/solution.py
@@ -215,7 +215,7 @@
             x_forward(z - dist, z >= dist)
             x_forward(z + dist, z + dist < NZ)
 
-    lag = 2
+    lag = 1
     x_sends = ((2, {"x": xp}, None), (3, {"x": xm}, None))
     for k in range(1, NZ):
         for part in parts:

time: 84.7 us -> 86.9 us (1.026)
  the two profiles are of different devices: /device:TPU:1 before, /device:TPU:29 now
where the time goes in v15:
time: 86.9 us; the launch traced here: 86.7 us
  Pallas kernels  81.3 us (94%)
  local copies, waits for them, and re-layouts  2.33 us (3%)
  matrix products  1.66 us (2%)
    pallas_call x1, Pallas kernels, fused_call(): pl.pallas_call(fused_kernel, out_shape=(jax.ShapeDtypeStruct(traces.shape...  81.3 us

profile of v15, /device:TPU:29, one launch (start us, length us, event | category | flops | bytes accessed | tf_op | source)
XLA Modules:
  0.0 86.7 jit_solution(5276813510984140669)
XLA Ops:
  0.6 0.0 copy-start
  0.6 1.4 %fusion = bf16[8,64,128]{2,0,1:T(8,128)(2,1)S(1)} fusion(bf16[8,32,1]{1,0,2:T(8,128)(2,1)} %constant.12, bf16[32,64,128]{2,1,0:T(8,128)(2,1)} %traces_ref.1), kind=kOutput, calls=%fused_computation.1 | convolution fusion | flops 4194304 | bytes 655872 | tf_op jit(solution)/shard_map/pt,tsr->psr/dot_general | solution.py:392
  2.1 0.7 copy.19.spec_ref
  2.8 0.0 copy-start.2
  2.8 81.3 %shard_map.95 = (bf16[32,64,128]{2,1,0:T(8,128)(2,1)}, f32[2,512]{1,0:T(2,128)}) custom-call(bf16[8,64,128]{2,1,0:T(8,128)(2,1)} %copy.19.spec_ref, bf16[32,64,128]{2,1,0:T(8,128)(2,1)} %traces_ref.1, s32[4,1024]{1,0:T(4,128)} %lists_ref.1, s32[1,2048]{1,0:T(1,128)} %bitcast.8, s32[1,64]{1,0:T(1,128)} %bitcast.9, f32[32,8]{1,0:T(8,128)} %constant.10.clone.inverse_ref), custom_call_target="tpu_custom_call" | custom-call | tf_op jit(solution)/shard_map/pallas_call | solution.py:352
  84.1 0.0 copy-start.1
  84.1 0.0 copy-done.2
  84.1 0.7 multiply_convert_fusion
  84.9 0.0 copy-done
  84.9 0.2 convolution_bitcast_fusion
  85.1 0.8 copy.13
  85.9 0.0 copy-done.1
  85.9 0.8 copy.21
  (1 shorter events, 0.0 us)
Async XLA Ops:
  0.6 84.2 %copy-start = (bf16[32,2,128]{2,1,0:T(2,128)(2,1)S(1)}, bf16[32,2,128]{2,1,0:T(2,128)(2,1)}, u32[]{:S(2)}) copy-start(bf16[32,2,128]{2,1,0:T(2,128)(2,1)} %param.13) | copy-start | bytes 49156
  2.8 81.3 %copy-start.2 = (s32[512]{0:T(512)S(1)}, s32[512]{0:T(512)}, u32[]{:S(2)}) copy-start(s32[512]{0:T(512)} %param.12) | copy-start | bytes 6148
  84.1 1.8 %copy-start.1 = (bf16[32,64,128]{2,1,0:T(8,128)(2,1)S(1)}, bf16[32,64,128]{2,1,0:T(8,128)(2,1)}, u32[]{:S(2)}) copy-start(bf16[32,64,128]{2,1,0:T(8,128)(2,1)} %get-tuple-element.10) | copy-start | bytes 1572868

commit v16 on v15

--- a/solution.py
+++ b/solution.py
@@ -215,7 +215,7 @@
             x_forward(z - dist, z >= dist)
             x_forward(z + dist, z + dist < NZ)
 
-    lag = 1
+    lag = 3
     x_sends = ((2, {"x": xp}, None), (3, {"x": xm}, None))
     for k in range(1, NZ):
         for part in parts:

time: 86.9 us -> 86.5 us (level)
  the two profiles are of different devices: /device:TPU:29 before, /device:TPU:1 now
where the time goes in v16:
time: 86.5 us; the launch traced here: 86.4 us
  Pallas kernels  80.9 us (94%)
  local copies, waits for them, and re-layouts  2.33 us (3%)
  matrix products  1.66 us (2%)
    pallas_call x1, Pallas kernels, fused_call(): pl.pallas_call(fused_kernel, out_shape=(jax.ShapeDtypeStruct(traces.shape...  80.9 us

profile of v16, /device:TPU:1, one launch (start us, length us, event | category | flops | bytes accessed | tf_op | source)
XLA Modules:
  0.0 86.4 jit_solution(12599821440151009777)
XLA Ops:
  0.6 0.0 copy-start
  0.6 1.4 %fusion = bf16[8,64,128]{2,0,1:T(8,128)(2,1)S(1)} fusion(bf16[8,32,1]{1,0,2:T(8,128)(2,1)} %constant.12, bf16[32,64,128]{2,1,0:T(8,128)(2,1)} %traces_ref.1), kind=kOutput, calls=%fused_computation.1 | convolution fusion | flops 4194304 | bytes 655872 | tf_op jit(solution)/shard_map/pt,tsr->psr/dot_general | solution.py:392
  2.1 0.7 copy.19.spec_ref
  2.8 0.0 copy-start.2
  2.8 80.9 %shard_map.95 = (bf16[32,64,128]{2,1,0:T(8,128)(2,1)}, f32[2,512]{1,0:T(2,128)}) custom-call(bf16[8,64,128]{2,1,0:T(8,128)(2,1)} %copy.19.spec_ref, bf16[32,64,128]{2,1,0:T(8,128)(2,1)} %traces_ref.1, s32[4,1024]{1,0:T(4,128)} %lists_ref.1, s32[1,2048]{1,0:T(1,128)} %bitcast.8, s32[1,64]{1,0:T(1,128)} %bitcast.9, f32[32,8]{1,0:T(8,128)} %constant.10.clone.inverse_ref), custom_call_target="tpu_custom_call" | custom-call | tf_op jit(solution)/shard_map/pallas_call | solution.py:352
  83.7 0.0 copy-start.1
  83.7 0.0 copy-done.2
  83.8 0.7 multiply_convert_fusion
  84.5 0.0 copy-done
  84.5 0.2 convolution_bitcast_fusion
  84.7 0.8 copy.13
  85.6 0.0 copy-done.1
  85.6 0.8 copy.21
  (1 shorter events, 0.0 us)
Async XLA Ops:
  0.6 83.9 %copy-start = (bf16[32,2,128]{2,1,0:T(2,128)(2,1)S(1)}, bf16[32,2,128]{2,1,0:T(2,128)(2,1)}, u32[]{:S(2)}) copy-start(bf16[32,2,128]{2,1,0:T(2,128)(2,1)} %param.13) | copy-start | bytes 49156
  2.8 80.9 %copy-start.2 = (s32[512]{0:T(512)S(1)}, s32[512]{0:T(512)}, u32[]{:S(2)}) copy-start(s32[512]{0:T(512)} %param.12) | copy-start | bytes 6148
  83.7 1.8 %copy-start.1 = (bf16[32,64,128]{2,1,0:T(8,128)(2,1)S(1)}, bf16[32,64,128]{2,1,0:T(8,128)(2,1)}, u32[]{:S(2)}) copy-start(bf16[32,64,128]{2,1,0:T(8,128)(2,1)} %get-tuple-element.10) | copy-start | bytes 1572868

commit v17 on v14

--- a/solution.py
+++ b/solution.py
@@ -265,29 +265,43 @@
     soffset = (spos - cols) / spread_len
     weights_ref[...] = 1.0 / (1.0 + soffset * soffset)
 
-    x2 = lax.rem(x + 2, NX)
-    for zz in range(NZ):
-        row_relay(xm * NZ + zz if zz % 2 == 1 else xp * NZ + zz, ())
-        row_relay(x2 * NZ + zz, ())
     y2 = lax.rem(y + 2, NY)
     for cc in range(2):
         col_relay((ym * 2 + 1) * 2 + cc, ())
         col_relay((yp * 2 + 0) * 2 + cc, ())
         for hh in range(2):
             col_relay((y2 * 2 + hh) * 2 + cc, ())
+    for zz in range(NZ):
+        row_relay(xm * NZ + zz if zz % 2 == 1 else xp * NZ + zz, ())
+
     nf = spec_ref.shape[0] // 2
     surface_root = math.sqrt(roww_ref.shape[2])
-    for f in range(nf):
-        lr = roww_ref[f]
-        li = roww_ref[nf + f]
-        rr = colw_ref[f]
-        ri = colw_ref[nf + f]
-        real_real = jnp.dot(lr, rr, preferred_element_type=jnp.float32)
-        imag_imag = jnp.dot(li, ri, preferred_element_type=jnp.float32)
-        real_imag = jnp.dot(lr, ri, preferred_element_type=jnp.float32)
-        imag_real = jnp.dot(li, rr, preferred_element_type=jnp.float32)
-        mult_ref[f] = -(real_real - imag_imag) / surface_root
-        mult_ref[nf + f] = -(real_imag + imag_real) / surface_root
+    span = NZ * shots
+    mult_ref[...] = jnp.zeros(mult_ref.shape, mult_ref.dtype)
+
+    def product_part(xc):
+        u = pl.ds(pl.multiple_of(xc * span, span), span)
+        for f in range(nf):
+            lr = roww_ref[f, :, u]
+            li = roww_ref[nf + f, :, u]
+            rr = colw_ref[f, u, :]
+            ri = colw_ref[nf + f, u, :]
+            real_real = jnp.dot(lr, rr, preferred_element_type=jnp.float32)
+            imag_imag = jnp.dot(li, ri, preferred_element_type=jnp.float32)
+            real_imag = jnp.dot(lr, ri, preferred_element_type=jnp.float32)
+            imag_real = jnp.dot(li, rr, preferred_element_type=jnp.float32)
+            mult_ref[f] += real_real - imag_imag
+            mult_ref[nf + f] += real_imag + imag_real
+
+    product_part(x)
+    product_part(xm)
+    product_part(xp)
+    x2 = lax.rem(x + 2, NX)
+    for zz in range(NZ):
+        row_relay(x2 * NZ + zz, ())
+    product_part(x2)
+    for p in range(2 * nf):
+        mult_ref[p] = -mult_ref[p] / surface_root
 
     def prim_body(t, carry):
         wave = inverse_ref[t, 0] * mult_ref[0]

time: 84.7 us -> 83.8 us (0.989)
  Pallas kernels: 79.1 us -> 78.2 us
    pallas_call x1, Pallas kernels: 79.1 us -> 78.2 us  [fused_call(): pl.pallas_call(fused_kernel, out_shape=(jax.ShapeDtypeStruct(traces.shape...]
where the time goes in v17:
time: 83.8 us; the launch traced here: 83.7 us
  Pallas kernels  78.2 us (93%)
  local copies, waits for them, and re-layouts  2.33 us (3%)
  matrix products  1.66 us (2%)
    pallas_call x1, Pallas kernels, fused_call(): pl.pallas_call(fused_kernel, out_shape=(jax.ShapeDtypeStruct(traces.shape...  78.2 us

profile of v17, /device:TPU:1, one launch (start us, length us, event | category | flops | bytes accessed | tf_op | source)
XLA Modules:
  0.0 83.7 jit_solution(4123441001038687409)
XLA Ops:
  0.6 0.0 copy-start
  0.6 1.4 %fusion = bf16[8,64,128]{2,0,1:T(8,128)(2,1)S(1)} fusion(bf16[8,32,1]{1,0,2:T(8,128)(2,1)} %constant.12, bf16[32,64,128]{2,1,0:T(8,128)(2,1)} %traces_ref.1), kind=kOutput, calls=%fused_computation.1 | convolution fusion | flops 4194304 | bytes 655872 | tf_op jit(solution)/shard_map/pt,tsr->psr/dot_general | solution.py:406
  2.1 0.7 copy.19.spec_ref
  2.8 0.0 copy-start.2
  2.8 78.2 %shard_map.95 = (bf16[32,64,128]{2,1,0:T(8,128)(2,1)}, f32[2,512]{1,0:T(2,128)}) custom-call(bf16[8,64,128]{2,1,0:T(8,128)(2,1)} %copy.19.spec_ref, bf16[32,64,128]{2,1,0:T(8,128)(2,1)} %traces_ref.1, s32[4,1024]{1,0:T(4,128)} %lists_ref.1, s32[1,2048]{1,0:T(1,128)} %bitcast.8, s32[1,64]{1,0:T(1,128)} %bitcast.9, f32[32,8]{1,0:T(8,128)} %constant.10.clone.inverse_ref), custom_call_target="tpu_custom_call" | custom-call | tf_op jit(solution)/shard_map/pallas_call | solution.py:366
  81.0 0.0 copy-start.1
  81.0 0.0 copy-done.2
  81.1 0.7 multiply_convert_fusion
  81.8 0.0 copy-done
  81.8 0.2 convolution_bitcast_fusion
  82.0 0.8 %copy.13 = f32[128,512]{1,0:T(8,128)} copy(f32[128,512]{0,1:T(8,128)S(1)} %convolution_bitcast_fusion) | data formatting | bytes 524288
  82.9 0.0 copy-done.1
  82.9 0.8 copy.21
  (1 shorter events, 0.0 us)
Async XLA Ops:
  0.6 81.2 %copy-start = (bf16[32,2,128]{2,1,0:T(2,128)(2,1)S(1)}, bf16[32,2,128]{2,1,0:T(2,128)(2,1)}, u32[]{:S(2)}) copy-start(bf16[32,2,128]{2,1,0:T(2,128)(2,1)} %param.13) | copy-start | bytes 49156
  2.8 78.2 %copy-start.2 = (s32[512]{0:T(512)S(1)}, s32[512]{0:T(512)}, u32[]{:S(2)}) copy-start(s32[512]{0:T(512)} %param.12) | copy-start | bytes 6148
  81.0 1.8 %copy-start.1 = (bf16[32,64,128]{2,1,0:T(8,128)(2,1)S(1)}, bf16[32,64,128]{2,1,0:T(8,128)(2,1)}, u32[]{:S(2)}) copy-start(bf16[32,64,128]{2,1,0:T(8,128)(2,1)} %get-tuple-element.10) | copy-start | bytes 1572868

commit v18 on v17

--- a/solution.py
+++ b/solution.py
@@ -200,7 +200,8 @@
     j_c = (y * 2 + h) * 2 + 1 - c
     j_hc = (y * 2 + 1 - h) * 2 + 1 - c
     y_sends = ((2, {"y": yp}), (3, {"y": ym}))
-    col_relay(j_c, y_sends)
+    to_partner = (0, {"c": 1 - c})
+    col_relay(j_c, ())
 
     def x_forward(zsrc, cond):
         even = lax.rem(zsrc, 2) == 0
@@ -229,11 +230,10 @@
         if k == 4:
             col_relay(j_h, ((0, {"c": 1 - c}),) + y_sends)
         if k == 5:
-            col_relay(j_hc, y_sends)
+            col_relay(j_hc, ())
         if k == 6:
-            for cc in range(2):
-                col_relay((ym * 2 + 0) * 2 + cc, ((2, {"y": yp}),))
-                col_relay((yp * 2 + 1) * 2 + cc, ((3, {"y": ym}),))
+            col_relay((ym * 2 + 0) * 2 + c, ((2, {"y": yp}), to_partner))
+            col_relay((yp * 2 + 1) * 2 + c, ((3, {"y": ym}), to_partner))
     for dist in range(NZ - lag, NZ):
         x_forward_at(dist)
 
@@ -266,11 +266,13 @@
     weights_ref[...] = 1.0 / (1.0 + soffset * soffset)
 
     y2 = lax.rem(y + 2, NY)
-    for cc in range(2):
-        col_relay((ym * 2 + 1) * 2 + cc, ())
-        col_relay((yp * 2 + 0) * 2 + cc, ())
+    col_relay((ym * 2 + 1) * 2 + c, (to_partner,))
+    col_relay((yp * 2 + 0) * 2 + c, (to_partner,))
+    for hh in range(2):
+        col_relay((y2 * 2 + hh) * 2 + c, (to_partner,))
+    for plane in (ym, yp, y2):
         for hh in range(2):
-            col_relay((y2 * 2 + hh) * 2 + cc, ())
+            col_relay((plane * 2 + hh) * 2 + 1 - c, ())
     for zz in range(NZ):
         row_relay(xm * NZ + zz if zz % 2 == 1 else xp * NZ + zz, ())
 

time: 83.8 us -> 83.5 us (level)
  no operation moved by 1% of the time
where the time goes in v18:
time: 83.5 us; the launch traced here: 83.4 us
  Pallas kernels  77.9 us (93%)
  local copies, waits for them, and re-layouts  2.33 us (3%)
  matrix products  1.66 us (2%)
    pallas_call x1, Pallas kernels, fused_call(): pl.pallas_call(fused_kernel, out_shape=(jax.ShapeDtypeStruct(traces.shape...  77.9 us

profile of v18, /device:TPU:1, one launch (start us, length us, event | category | flops | bytes accessed | tf_op | source)
XLA Modules:
  0.0 83.4 jit_solution(4447605589754143926)
XLA Ops:
  0.6 0.0 copy-start
  0.6 1.4 %fusion = bf16[8,64,128]{2,0,1:T(8,128)(2,1)S(1)} fusion(bf16[8,32,1]{1,0,2:T(8,128)(2,1)} %constant.12, bf16[32,64,128]{2,1,0:T(8,128)(2,1)} %traces_ref.1), kind=kOutput, calls=%fused_computation.1 | convolution fusion | flops 4194304 | bytes 655872 | tf_op jit(solution)/shard_map/pt,tsr->psr/dot_general | solution.py:408
  2.1 0.7 copy.19.spec_ref
  2.8 0.0 copy-start.2
  2.8 77.9 %shard_map.95 = (bf16[32,64,128]{2,1,0:T(8,128)(2,1)}, f32[2,512]{1,0:T(2,128)}) custom-call(bf16[8,64,128]{2,1,0:T(8,128)(2,1)} %copy.19.spec_ref, bf16[32,64,128]{2,1,0:T(8,128)(2,1)} %traces_ref.1, s32[4,1024]{1,0:T(4,128)} %lists_ref.1, s32[1,2048]{1,0:T(1,128)} %bitcast.8, s32[1,64]{1,0:T(1,128)} %bitcast.9, f32[32,8]{1,0:T(8,128)} %constant.10.clone.inverse_ref), custom_call_target="tpu_custom_call" | custom-call | tf_op jit(solution)/shard_map/pallas_call | solution.py:368
  80.7 0.0 copy-start.1
  80.7 0.0 copy-done.2
  80.8 0.7 multiply_convert_fusion
  81.5 0.0 copy-done
  81.5 0.2 convolution_bitcast_fusion
  81.7 0.8 %copy.13 = f32[128,512]{1,0:T(8,128)} copy(f32[128,512]{0,1:T(8,128)S(1)} %convolution_bitcast_fusion) | data formatting | bytes 524288
  82.6 0.0 copy-done.1
  82.6 0.8 copy.21
  (1 shorter events, 0.0 us)
Async XLA Ops:
  0.6 80.9 %copy-start = (bf16[32,2,128]{2,1,0:T(2,128)(2,1)S(1)}, bf16[32,2,128]{2,1,0:T(2,128)(2,1)}, u32[]{:S(2)}) copy-start(bf16[32,2,128]{2,1,0:T(2,128)(2,1)} %param.13) | copy-start | bytes 49156
  2.8 78.0 %copy-start.2 = (s32[512]{0:T(512)S(1)}, s32[512]{0:T(512)}, u32[]{:S(2)}) copy-start(s32[512]{0:T(512)} %param.12) | copy-start | bytes 6148
  80.7 1.8 %copy-start.1 = (bf16[32,64,128]{2,1,0:T(8,128)(2,1)S(1)}, bf16[32,64,128]{2,1,0:T(8,128)(2,1)}, u32[]{:S(2)}) copy-start(bf16[32,64,128]{2,1,0:T(8,128)(2,1)} %get-tuple-element.10) | copy-start | bytes 1572868

commit v19 on v18

--- a/solution.py
+++ b/solution.py
@@ -85,9 +85,9 @@
 NX, NZ, NY = 4, 8, 4
 
 
-def fused_kernel(spec_ref, traces_ref, lists_ref, rpos_ref, spos_ref, inverse_ref,
+def fused_kernel(traces_ref, forward_ref, lists_ref, rpos_ref, spos_ref, inverse_ref,
                  prim_ref, stack_ref,
-                 colw_ref, roww_ref, mult_ref, partial_ref, slots_ref, aperture_ref, weights_ref,
+                 spec_ref, colw_ref, roww_ref, mult_ref, partial_ref, slots_ref, aperture_ref, weights_ref,
                  recv_row, recv_col, send_row, send_col, recv_red, send_red):
     x = lax.axis_index("x")
     z = lax.axis_index("zl")
@@ -124,6 +124,18 @@
     @pl.when(z < NZ - 1)
     def _():
         pl.semaphore_signal(barrier, 1, device_id={"zl": z + 1}, device_id_type=MESH_ID)
+
+    samples = traces_ref.shape[0]
+    group = 4
+    for p0 in range(0, spec_ref.shape[0], group):
+        def spectra_body(t, accs, p0=p0):
+            sample = traces_ref[t].astype(jnp.float32)
+            return tuple(acc + forward_ref[p0 + g, t] * sample for g, acc in enumerate(accs))
+
+        zero = jnp.zeros(spec_ref.shape[1:], jnp.float32)
+        accs = lax.fori_loop(0, samples, spectra_body, (zero,) * group)
+        for g in range(group):
+            spec_ref[p0 + g] = accs[g].astype(spec_ref.dtype)
 
     peers_in = 2 + len(col_peers) - 1
     ends = jnp.logical_or(z == 0, z == NZ - 1)
@@ -360,9 +372,9 @@
         pl.when(j != me_col)(reduce_copy(j, peer).wait_send)
 
 
-def fused_call(spec, traces, lists, rpos, spos, inverse, width, row_count, col_count):
-    planes, shots, recvs = spec.shape
-    samples = traces.shape[0]
+def fused_call(traces, forward, lists, rpos, spos, inverse, width, row_count, col_count):
+    samples, shots, recvs = traces.shape
+    planes = forward.shape[0]
     band = samples // col_count
     vmem = pl.BlockSpec(memory_space=pltpu.VMEM)
     return pl.pallas_call(
@@ -371,11 +383,19 @@
             jax.ShapeDtypeStruct(traces.shape, jnp.bfloat16),
             jax.ShapeDtypeStruct((band, width), jnp.float32),
         ),
-        in_specs=[vmem, vmem, vmem, vmem, vmem, pl.BlockSpec(memory_space=pltpu.SMEM)],
+        in_specs=[
+            vmem,
+            pl.BlockSpec(memory_space=pltpu.SMEM),
+            vmem,
+            vmem,
+            vmem,
+            pl.BlockSpec(memory_space=pltpu.SMEM),
+        ],
         out_specs=(vmem, vmem),
         scratch_shapes=[
-            pltpu.VMEM((planes, row_count * shots, recvs), spec.dtype),
-            pltpu.VMEM((planes, shots, col_count * recvs), spec.dtype),
+            pltpu.VMEM((planes, shots, recvs), jnp.bfloat16),
+            pltpu.VMEM((planes, row_count * shots, recvs), jnp.bfloat16),
+            pltpu.VMEM((planes, shots, col_count * recvs), jnp.bfloat16),
             pltpu.VMEM((planes, shots, recvs), jnp.float32),
             pltpu.VMEM((col_count, band, width), jnp.float32),
             pltpu.VMEM((col_count, band, width), jnp.float32),
@@ -389,7 +409,7 @@
             pltpu.SemaphoreType.DMA((col_count,)),
         ],
         compiler_params=pltpu.CompilerParams(collective_id=0, has_side_effects=True),
-    )(spec, traces, lists, rpos, spos, inverse)
+    )(traces, forward, lists, rpos, spos, inverse)
 
 
 def per_device(traces, source_pos, receiver_pos, aperture_list, band_index, weight_tiles):
@@ -401,18 +421,15 @@
     depth_slab_samples = samples // col_count
     cosine, sine_table = phase_tables_np(samples)
     forward = jnp.asarray(
-        (np.concatenate([cosine, -sine_table], 0) / np.float32(math.sqrt(samples))).astype(
-            ml_dtypes.bfloat16
-        )
-    )
-    spectra = jnp.einsum(
-        "pt,tsr->psr", forward, traces, preferred_element_type=jnp.float32
-    ).astype(jnp.bfloat16)
+        (np.concatenate([cosine, -sine_table], 0) / np.float32(math.sqrt(samples)))
+        .astype(ml_dtypes.bfloat16)
+        .astype(np.float32)
+    )
 
     inverse = jnp.asarray(np.concatenate([cosine, -sine_table], 0).T / np.float32(math.sqrt(NF)))
     primaries, stacked = fused_call(
-        spectra,
         traces,
+        forward,
         aperture_list,
         receiver_pos.reshape(1, -1),
         source_pos.reshape(1, -1),

time: 83.5 us -> 82.2 us (0.984)
  matrix products: 1.66 us -> 0.21 us
    dot_general x1 -> x0, matrix products: 1.45 us -> none  [per_device(): jnp.einsum('pt,tsr->psr', forward, traces, preferred_element_type=jnp.flo...]
where the time goes in v19:
time: 82.2 us; the launch traced here: 82 us
  Pallas kernels  78.7 us (96%)
  local copies, waits for them, and re-layouts  1.65 us (2%)
    pallas_call x1, Pallas kernels, fused_call(): pl.pallas_call(fused_kernel, out_shape=(jax.ShapeDtypeStruct(traces.shape...  78.7 us
    unnamed x8, local copies, waits for them, and re-layouts  1.65 us

profile of v19, /device:TPU:1, one launch (start us, length us, event | category | flops | bytes accessed | tf_op | source)
XLA Modules:
  0.0 82.0 jit_solution(16257971909668681374)
XLA Ops:
  0.6 0.0 copy-start
  0.6 0.0 copy-start.2
  0.7 78.7 %shard_map.95 = (bf16[32,64,128]{2,1,0:T(8,128)(2,1)}, f32[2,512]{1,0:T(2,128)}) custom-call(bf16[32,64,128]{2,1,0:T(8,128)(2,1)} %traces_ref.1, f32[8,32]{1,0:T(8,128)} %constant.9.clone.forward_ref, s32[4,1024]{1,0:T(4,128)} %lists_ref.1, s32[1,2048]{1,0:T(1,128)} %bitcast.6, s32[1,64]{1,0:T(1,128)} %bitcast.7, f32[32,8]{1,0:T(8,128)} %constant.10.clone.inverse_ref), custom_call_target="tpu_custom_call" | custom-call | tf_op jit(solution)/shard_map/pallas_call | solution.py:380
  79.3 0.0 copy-start.1
  79.3 0.0 copy-done.2
  79.4 0.7 multiply_convert_fusion
  80.1 0.0 copy-done
  80.1 0.2 convolution_bitcast_fusion
  80.3 0.8 %copy.11 = f32[128,512]{1,0:T(8,128)} copy(f32[128,512]{0,1:T(8,128)S(1)} %convolution_bitcast_fusion) | data formatting | bytes 524288
  81.2 0.0 copy-done.1
  81.2 0.8 copy.15
  (1 shorter events, 0.0 us)
Async XLA Ops:
  0.6 79.5 %copy-start = (bf16[32,2,128]{2,1,0:T(2,128)(2,1)S(1)}, bf16[32,2,128]{2,1,0:T(2,128)(2,1)}, u32[]{:S(2)}) copy-start(bf16[32,2,128]{2,1,0:T(2,128)(2,1)} %param.13) | copy-start | bytes 49156
  0.6 78.7 %copy-start.2 = (s32[512]{0:T(512)S(1)}, s32[512]{0:T(512)}, u32[]{:S(2)}) copy-start(s32[512]{0:T(512)} %param.12) | copy-start | bytes 6148
  79.3 1.8 %copy-start.1 = (bf16[32,64,128]{2,1,0:T(8,128)(2,1)S(1)}, bf16[32,64,128]{2,1,0:T(8,128)(2,1)}, u32[]{:S(2)}) copy-start(bf16[32,64,128]{2,1,0:T(8,128)(2,1)} %get-tuple-element.10) | copy-start | bytes 1572868

commit v20 on v19

--- a/solution.py
+++ b/solution.py
@@ -165,9 +165,10 @@
         )
 
     def col_copy(j, part, d, peer, own=False):
-        src = spec_ref.at[planes(part)] if own else roww_blk(j, part)
+        whole = roww_ref.at[:, :, pl.ds(pl.multiple_of(j * recvs, recvs), recvs)]
+        src = spec_ref if own else whole
         return pltpu.make_async_remote_copy(
-            src, roww_blk(j, part), send_col.at[j, part, d], recv_col.at[j, part],
+            src, whole, send_col.at[j, part, d], recv_col.at[j, part],
             device_id=peer, device_id_type=MESH_ID,
         )
 
@@ -192,19 +193,19 @@
                 start(row_copy(b, part, d, peer), c2)
 
     def col_relay(j, sends, cond=None):
-        for part in parts:
+        for part in (0,):
             when(cond, col_copy(j, part, 0, {"y": y}).wait_recv)
             for d, peer in sends:
                 start(col_copy(j, part, d, peer), cond)
 
+    start(col_copy(me_col, 0, 0, {"c": 1 - c}, own=True))
     for part in parts:
-        start(col_copy(me_col, part, 0, {"c": 1 - c}, own=True))
         start(row_copy(me_row, part, 0, {"zl": z + 1}, own=True), z < NZ - 1)
         start(row_copy(me_row, part, 1, {"zl": z - 1}, own=True), z > 0)
         start(row_copy(me_row, part, 2, {"x": xp}, own=True))
         start(row_copy(me_row, part, 3, {"x": xm}, own=True))
-        start(col_copy(me_col, part, 2, {"y": yp}, own=True))
-        start(col_copy(me_col, part, 3, {"y": ym}, own=True))
+    start(col_copy(me_col, 0, 2, {"y": yp}, own=True))
+    start(col_copy(me_col, 0, 3, {"y": ym}, own=True))
     colw_ref[:, pl.ds(pl.multiple_of(me_row * shots, shots), shots), :] = spec_ref[...]
     roww_ref[:, :, pl.ds(pl.multiple_of(me_col * recvs, recvs), recvs)] = spec_ref[...]
 
@@ -237,8 +238,7 @@
         if k - lag >= 0:
             x_forward_at(k - lag)
         if k == 2:
-            for part in parts:
-                start(col_copy(me_col, part, 1, {"zh": 1 - h}, own=True))
+            start(col_copy(me_col, 0, 1, {"zh": 1 - h}, own=True))
         if k == 4:
             col_relay(j_h, ((0, {"c": 1 - c}),) + y_sends)
         if k == 5:

time: 82.2 us -> 82.1 us (level)
  no operation moved by 1% of the time
where the time goes in v20:
time: 82.1 us; the launch traced here: 81.9 us
  Pallas kernels  78.6 us (96%)
  local copies, waits for them, and re-layouts  1.65 us (2%)
    pallas_call x1, Pallas kernels, fused_call(): pl.pallas_call(fused_kernel, out_shape=(jax.ShapeDtypeStruct(traces.shape...  78.6 us
    unnamed x8, local copies, waits for them, and re-layouts  1.65 us

profile of v20, /device:TPU:1, one launch (start us, length us, event | category | flops | bytes accessed | tf_op | source)
XLA Modules:
  0.0 81.9 jit_solution(9613035037442093793)
XLA Ops:
  0.6 0.0 copy-start
  0.6 0.0 copy-start.2
  0.7 78.6 %shard_map.95 = (bf16[32,64,128]{2,1,0:T(8,128)(2,1)}, f32[2,512]{1,0:T(2,128)}) custom-call(bf16[32,64,128]{2,1,0:T(8,128)(2,1)} %traces_ref.1, f32[8,32]{1,0:T(8,128)} %constant.9.clone.forward_ref, s32[4,1024]{1,0:T(4,128)} %lists_ref.1, s32[1,2048]{1,0:T(1,128)} %bitcast.6, s32[1,64]{1,0:T(1,128)} %bitcast.7, f32[32,8]{1,0:T(8,128)} %constant.10.clone.inverse_ref), custom_call_target="tpu_custom_call" | custom-call | tf_op jit(solution)/shard_map/pallas_call | solution.py:380
  79.3 0.0 copy-start.1
  79.3 0.0 copy-done.2
  79.3 0.7 multiply_convert_fusion
  80.1 0.0 copy-done
  80.1 0.2 convolution_bitcast_fusion
  80.3 0.8 %copy.11 = f32[128,512]{1,0:T(8,128)} copy(f32[128,512]{0,1:T(8,128)S(1)} %convolution_bitcast_fusion) | data formatting | bytes 524288
  81.1 0.0 copy-done.1
  81.1 0.8 copy.15
  (1 shorter events, 0.0 us)
Async XLA Ops:
  0.6 79.4 %copy-start = (bf16[32,2,128]{2,1,0:T(2,128)(2,1)S(1)}, bf16[32,2,128]{2,1,0:T(2,128)(2,1)}, u32[]{:S(2)}) copy-start(bf16[32,2,128]{2,1,0:T(2,128)(2,1)} %param.13) | copy-start | bytes 49156
  0.6 78.7 %copy-start.2 = (s32[512]{0:T(512)S(1)}, s32[512]{0:T(512)}, u32[]{:S(2)}) copy-start(s32[512]{0:T(512)} %param.12) | copy-start | bytes 6148
  79.3 1.8 %copy-start.1 = (bf16[32,64,128]{2,1,0:T(8,128)(2,1)S(1)}, bf16[32,64,128]{2,1,0:T(8,128)(2,1)}, u32[]{:S(2)}) copy-start(bf16[32,64,128]{2,1,0:T(8,128)(2,1)} %get-tuple-element.10) | copy-start | bytes 1572868

commit v21 on v20

--- a/solution.py
+++ b/solution.py
@@ -324,7 +324,7 @@
         prim_ref[t] = (traces_ref[t].astype(jnp.float32) - wave).astype(prim_ref.dtype)
         return carry
 
-    lax.fori_loop(0, traces_ref.shape[0], prim_body, 0)
+    lax.fori_loop(0, traces_ref.shape[0], prim_body, 0, unroll=True)
 
     band = partial_ref.shape[1]
 
@@ -352,7 +352,7 @@
         pl.when(j != me_col)(reduce_copy(j, peer).start)
         return carry
 
-    lax.fori_loop(0, partial_ref.shape[0], band_body, 0)
+    lax.fori_loop(0, partial_ref.shape[0], band_body, 0, unroll=True)
 
     slots_ref[me_col] = partial_ref[me_col]
     for j, peer in col_peers:

time: 82.1 us -> 82 us (level)
  no operation moved by 1% of the time
where the time goes in v21:
time: 82 us; the launch traced here: 81.8 us
  Pallas kernels  78.5 us (96%)
  local copies, waits for them, and re-layouts  1.65 us (2%)
    pallas_call x1, Pallas kernels, fused_call(): pl.pallas_call(fused_kernel, out_shape=(jax.ShapeDtypeStruct(traces.shape...  78.5 us
    unnamed x8, local copies, waits for them, and re-layouts  1.65 us

profile of v21, /device:TPU:1, one launch (start us, length us, event | category | flops | bytes accessed | tf_op | source)
XLA Modules:
  0.0 81.8 jit_solution(6000028097513386548)
XLA Ops:
  0.6 0.0 copy-start
  0.6 0.0 copy-start.2
  0.7 78.5 %shard_map.95 = (bf16[32,64,128]{2,1,0:T(8,128)(2,1)}, f32[2,512]{1,0:T(2,128)}) custom-call(bf16[32,64,128]{2,1,0:T(8,128)(2,1)} %traces_ref.1, f32[8,32]{1,0:T(8,128)} %constant.9.clone.forward_ref, s32[4,1024]{1,0:T(4,128)} %lists_ref.1, s32[1,2048]{1,0:T(1,128)} %bitcast.6, s32[1,64]{1,0:T(1,128)} %bitcast.7, f32[32,8]{1,0:T(8,128)} %constant.10.clone.inverse_ref), custom_call_target="tpu_custom_call" | custom-call | tf_op jit(solution)/shard_map/pallas_call | solution.py:380
  79.1 0.0 copy-start.1
  79.2 0.0 copy-done.2
  79.2 0.7 multiply_convert_fusion
  79.9 0.0 copy-done
  79.9 0.2 convolution_bitcast_fusion
  80.2 0.8 %copy.11 = f32[128,512]{1,0:T(8,128)} copy(f32[128,512]{0,1:T(8,128)S(1)} %convolution_bitcast_fusion) | data formatting | bytes 524288
  81.0 0.0 copy-done.1
  81.0 0.8 copy.15
  (1 shorter events, 0.0 us)
Async XLA Ops:
  0.6 79.3 %copy-start = (bf16[32,2,128]{2,1,0:T(2,128)(2,1)S(1)}, bf16[32,2,128]{2,1,0:T(2,128)(2,1)}, u32[]{:S(2)}) copy-start(bf16[32,2,128]{2,1,0:T(2,128)(2,1)} %param.13) | copy-start | bytes 49156
  0.6 78.5 %copy-start.2 = (s32[512]{0:T(512)S(1)}, s32[512]{0:T(512)}, u32[]{:S(2)}) copy-start(s32[512]{0:T(512)} %param.12) | copy-start | bytes 6148
  79.1 1.8 %copy-start.1 = (bf16[32,64,128]{2,1,0:T(8,128)(2,1)S(1)}, bf16[32,64,128]{2,1,0:T(8,128)(2,1)}, u32[]{:S(2)}) copy-start(bf16[32,64,128]{2,1,0:T(8,128)(2,1)} %get-tuple-element.10) | copy-start | bytes 1572868

commit v22 on v21

--- a/solution.py
+++ b/solution.py
@@ -237,7 +237,7 @@
             row_relay(x * NZ + z + k, x_sends + ((1, {"zl": z - 1}, z > 0),), z + k < NZ, (part,))
         if k - lag >= 0:
             x_forward_at(k - lag)
-        if k == 2:
+        if k == 1:
             start(col_copy(me_col, 0, 1, {"zh": 1 - h}, own=True))
         if k == 4:
             col_relay(j_h, ((0, {"c": 1 - c}),) + y_sends)

time: 82 us -> 83.3 us (1.016)
  Pallas kernels: 78.5 us -> 79.8 us
    pallas_call x1, Pallas kernels: 78.5 us -> 79.8 us  [fused_call(): pl.pallas_call(fused_kernel, out_shape=(jax.ShapeDtypeStruct(traces.shape...]
where the time goes in v22:
time: 83.3 us; the launch traced here: 83.1 us
  Pallas kernels  79.8 us (96%)
  local copies, waits for them, and re-layouts  1.65 us (2%)
    pallas_call x1, Pallas kernels, fused_call(): pl.pallas_call(fused_kernel, out_shape=(jax.ShapeDtypeStruct(traces.shape...  79.8 us

profile of v22, /device:TPU:1, one launch (start us, length us, event | category | flops | bytes accessed | tf_op | source)
XLA Modules:
  0.0 83.1 jit_solution(3528338818415129304)
XLA Ops:
  0.6 0.0 copy-start
  0.6 0.0 copy-start.2
  0.7 79.8 %shard_map.95 = (bf16[32,64,128]{2,1,0:T(8,128)(2,1)}, f32[2,512]{1,0:T(2,128)}) custom-call(bf16[32,64,128]{2,1,0:T(8,128)(2,1)} %traces_ref.1, f32[8,32]{1,0:T(8,128)} %constant.9.clone.forward_ref, s32[4,1024]{1,0:T(4,128)} %lists_ref.1, s32[1,2048]{1,0:T(1,128)} %bitcast.6, s32[1,64]{1,0:T(1,128)} %bitcast.7, f32[32,8]{1,0:T(8,128)} %constant.10.clone.inverse_ref), custom_call_target="tpu_custom_call" | custom-call | tf_op jit(solution)/shard_map/pallas_call | solution.py:380
  80.5 0.0 copy-start.1
  80.5 0.0 copy-done.2
  80.5 0.7 multiply_convert_fusion
  81.3 0.0 copy-done
  81.3 0.2 convolution_bitcast_fusion
  81.5 0.8 %copy.11 = f32[128,512]{1,0:T(8,128)} copy(f32[128,512]{0,1:T(8,128)S(1)} %convolution_bitcast_fusion) | data formatting | bytes 524288
  82.3 0.0 copy-done.1
  82.3 0.8 copy.15
  (1 shorter events, 0.0 us)
Async XLA Ops:
  0.6 80.6 %copy-start = (bf16[32,2,128]{2,1,0:T(2,128)(2,1)S(1)}, bf16[32,2,128]{2,1,0:T(2,128)(2,1)}, u32[]{:S(2)}) copy-start(bf16[32,2,128]{2,1,0:T(2,128)(2,1)} %param.13) | copy-start | bytes 49156
  0.6 79.9 %copy-start.2 = (s32[512]{0:T(512)S(1)}, s32[512]{0:T(512)}, u32[]{:S(2)}) copy-start(s32[512]{0:T(512)} %param.12) | copy-start | bytes 6148
  80.5 1.8 %copy-start.1 = (bf16[32,64,128]{2,1,0:T(8,128)(2,1)S(1)}, bf16[32,64,128]{2,1,0:T(8,128)(2,1)}, u32[]{:S(2)}) copy-start(bf16[32,64,128]{2,1,0:T(8,128)(2,1)} %get-tuple-element.10) | copy-start | bytes 1572868

commit v23 on v21

--- a/solution.py
+++ b/solution.py
@@ -145,8 +145,8 @@
     started = []
     shots = spec_ref.shape[1]
     recvs = spec_ref.shape[2]
-    half = spec_ref.shape[0] // 2
-    parts = (0, 1)
+    half = spec_ref.shape[0]
+    parts = (0,)
 
     def planes(part):
         return pl.ds(part * half, half)

time: 82 us -> 85.8 us (1.046)
  Pallas kernels: 78.5 us -> 82.3 us
    pallas_call x1, Pallas kernels: 78.5 us -> 82.3 us  [fused_call(): pl.pallas_call(fused_kernel, out_shape=(jax.ShapeDtypeStruct(traces.shape...]
where the time goes in v23:
time: 85.8 us; the launch traced here: 85.6 us
  Pallas kernels  82.3 us (96%)
  local copies, waits for them, and re-layouts  1.65 us (2%)
    pallas_call x1, Pallas kernels, fused_call(): pl.pallas_call(fused_kernel, out_shape=(jax.ShapeDtypeStruct(traces.shape...  82.3 us

profile of v23, /device:TPU:1, one launch (start us, length us, event | category | flops | bytes accessed | tf_op | source)
XLA Modules:
  0.0 85.6 jit_solution(11843363386109610120)
XLA Ops:
  0.6 0.0 copy-start
  0.6 0.0 copy-start.2
  0.7 82.3 %shard_map.95 = (bf16[32,64,128]{2,1,0:T(8,128)(2,1)}, f32[2,512]{1,0:T(2,128)}) custom-call(bf16[32,64,128]{2,1,0:T(8,128)(2,1)} %traces_ref.1, f32[8,32]{1,0:T(8,128)} %constant.9.clone.forward_ref, s32[4,1024]{1,0:T(4,128)} %lists_ref.1, s32[1,2048]{1,0:T(1,128)} %bitcast.6, s32[1,64]{1,0:T(1,128)} %bitcast.7, f32[32,8]{1,0:T(8,128)} %constant.10.clone.inverse_ref), custom_call_target="tpu_custom_call" | custom-call | tf_op jit(solution)/shard_map/pallas_call | solution.py:380
  82.9 0.0 copy-start.1
  82.9 0.0 copy-done.2
  83.0 0.7 multiply_convert_fusion
  83.7 0.0 copy-done
  83.7 0.2 convolution_bitcast_fusion
  83.9 0.8 copy.11
  84.8 0.0 copy-done.1
  84.8 0.8 copy.15
  (1 shorter events, 0.0 us)
Async XLA Ops:
  0.6 83.1 %copy-start = (bf16[32,2,128]{2,1,0:T(2,128)(2,1)S(1)}, bf16[32,2,128]{2,1,0:T(2,128)(2,1)}, u32[]{:S(2)}) copy-start(bf16[32,2,128]{2,1,0:T(2,128)(2,1)} %param.13) | copy-start | bytes 49156
  0.6 82.3 %copy-start.2 = (s32[512]{0:T(512)S(1)}, s32[512]{0:T(512)}, u32[]{:S(2)}) copy-start(s32[512]{0:T(512)} %param.12) | copy-start | bytes 6148
  82.9 1.8 %copy-start.1 = (bf16[32,64,128]{2,1,0:T(8,128)(2,1)S(1)}, bf16[32,64,128]{2,1,0:T(8,128)(2,1)}, u32[]{:S(2)}) copy-start(bf16[32,64,128]{2,1,0:T(8,128)(2,1)} %get-tuple-element.10) | copy-start | bytes 1572868
